TPU v7x, 256 devices: a whole 4x4x8 slice. The times are simulated.
256 devices in a mesh: spec: 16 (over y, x), grid: 16 (over z, core).
Axes of the slice: x: 4, y: 4, z: 8, core: 2. Of those that a mesh axis runs over, the one named last changes fastest.
Arguments:
- spectrum: float32 [1296, 64, 4096], P('spec', None, 'grid'), may hold values from 0.05 to 1
- group_speed: float32 [36], replicated, may hold values from 0.3 to 0.9
- depth_factor: float32 [64, 4096], P(None, 'grid'), may hold values from 0.4 to 1
- sea_mask: int32 [64, 4096], P(None, 'grid'), may hold values 0 or 1
- interaction: bfloat16 [1296, 1296], replicated, may hold values from -0.15625 to 0.15625
- wind_speed: float32 [64, 4096], P('spec', 'grid'), may hold values from 0.5 to 1.5
- wind_dir: float32 [64, 4096], P('spec', 'grid'), may hold values from -3.140625 to 3.140625
- nest_owner: int32 [32768, 1], P(('spec', 'grid')), may hold values from 0 to 15; in each aligned block of 128 rows (0 to 127, 128 to 255, ...) at most 16 rows name the same one
- nest_point: int32 [32768], P(('spec', 'grid')), may hold values from 0 to 127
- nest_cell: int32 [32768], P(('spec', 'grid')), may hold values from 0 to 1023
- weight_index: int32 [32768], P(('spec', 'grid')), may hold values from 0 to 63
- weight_table: float32 [64], replicated, may hold values from 0.2 to 1
Outputs:
- spectrum_out: float32 [1296, 64, 4096], P(None, 'spec', 'grid')
- nest_spectra: float32 [1296, 32768], P(None, ('spec', 'grid'))
Inputs may be any that keep to these rules, and one draw needn't show every extreme that they name: `nest_owner`: among the 128 entries of one device no owner is named by more than 16 entries, a bound that some block reaches.
All inputs are finite; a program needn't handle non-finite values. No bound on the sum of `sea_mask` on one device may be relied on, other than what follows from the above.
Results may differ from a plain program's by a relative error of at most 0.0035.
Values may be sent and summed in bfloat16 or wider, within the bound.
A program may use at most 128 MiB of HBM per device.

v0:
```python
import functools
import math

import jax
import jax.numpy as jnp
from jax import lax
from jax.experimental import pallas as pl
from jax.experimental.pallas import tpu as pltpu
from jax.sharding import PartitionSpec as P

SOURCE_STEPS = 4
NB_OWN = 128
CAP = 16


TWO_PI = 2.0 * math.pi
RATE = 0.2
WIND_GAIN = 0.8
WHITECAP = 1.0
EPSILON = 1e-06
HIGHEST = lax.Precision.HIGHEST


def headings(offset, number, freq_count, dir_count):
    component = offset + jnp.arange(number, dtype=jnp.int32)
    heading = TWO_PI * ((component // freq_count).astype(jnp.float32) + 0.5) / dir_count
    return (heading, component % freq_count)


def wind_term(heading, freq_index, freq_count, speed_flat, direction_flat):
    alignment = (
        jnp.cos(heading)[:, None] * jnp.cos(direction_flat)[None]
        + jnp.sin(heading)[:, None] * jnp.sin(direction_flat)[None]
    )
    scale_freq = (freq_index + 1).astype(jnp.float32) / freq_count
    return WIND_GAIN * scale_freq[:, None] * speed_flat[None] * jnp.maximum(alignment, 0.0)


def propagate_kernel(
    rx_ref, ry_ref, spec_ref, factor_ref, sea_ref, out_ref,
    send_first, send_last, recv_west, recv_east, send_sem, recv_sem,
):
    comps, rows, lons = spec_ref.shape
    grid_count = lax.axis_size("grid")
    me = lax.axis_index("grid")
    spec = lax.axis_index("spec")
    right = lax.rem(me + 1, grid_count)
    left = lax.rem(me + grid_count - 1, grid_count)
    barrier = pltpu.get_barrier_semaphore()
    for neighbour in (left, right):
        pl.semaphore_signal(barrier, inc=1, device_id=(spec, neighbour), device_id_type=pl.DeviceIdType.MESH)
    pl.semaphore_wait(barrier, 2)

    factor = factor_ref[...]
    sea = sea_ref[...]
    edge_lane = lax.broadcasted_iota(jnp.int32, (rows, 128), 1)
    factor_first = factor[:, 0:1]
    factor_last = factor[:, lons - 1 : lons]

    def edges(kk, carry):
        first, last = carry
        rx = rx_ref[kk]
        s_first = spec_ref[kk, :, 0:128][:, 0:1]
        s_last = spec_ref[kk, :, lons - 128 : lons][:, 127:128]
        first = jnp.where(edge_lane == kk, rx * factor_first * s_first, first)
        last = jnp.where(edge_lane == kk, rx * factor_last * s_last, last)
        return first, last

    zero = jnp.zeros((rows, 128), jnp.float32)
    first, last = lax.fori_loop(0, comps, edges, (zero, zero))
    send_first[...] = first
    send_last[...] = last
    to_right = pltpu.make_async_remote_copy(
        src_ref=send_last, dst_ref=recv_west, send_sem=send_sem.at[0], recv_sem=recv_sem.at[0],
        device_id=(spec, right), device_id_type=pl.DeviceIdType.MESH,
    )
    to_left = pltpu.make_async_remote_copy(
        src_ref=send_first, dst_ref=recv_east, send_sem=send_sem.at[1], recv_sem=recv_sem.at[1],
        device_id=(spec, left), device_id_type=pl.DeviceIdType.MESH,
    )
    to_right.start()
    to_left.start()
    to_right.wait()
    to_left.wait()

    lane = lax.broadcasted_iota(jnp.int32, (rows, lons), 1)
    row = lax.broadcasted_iota(jnp.int32, (rows, lons), 0)

    def one(kk, carry):
        rx = rx_ref[kk]
        ry = ry_ref[kk]
        s = spec_ref[kk]
        west_col = jnp.sum(jnp.where(edge_lane == kk, recv_west[...], 0.0), axis=1, keepdims=True)
        east_col = jnp.sum(jnp.where(edge_lane == kk, recv_east[...], 0.0), axis=1, keepdims=True)
        fx = rx * factor * s
        west = jnp.where(lane == 0, west_col, pltpu.roll(fx, 1, 1))
        east = jnp.where(lane == lons - 1, east_col, pltpu.roll(fx, lons - 1, 1))
        change = jnp.where(rx > 0, fx - west, east - fx)
        ax = sea * (s - change)
        fy = ry * factor * ax
        south = jnp.where(row == 0, 0.0, pltpu.roll(fy, 1, 0))
        north = jnp.where(row == rows - 1, 0.0, pltpu.roll(fy, rows - 1, 0))
        change_y = jnp.where(ry > 0, fy - south, north - fy)
        out_ref[kk] = (sea * (ax - change_y)).astype(out_ref.dtype)
        return carry

    lax.fori_loop(0, comps, one, 0)


def propagate(spectrum, rate_x, rate_y, factor, sea_float):
    comps, rows, lons = spectrum.shape
    smem = pl.BlockSpec(memory_space=pltpu.SMEM)
    vmem = pl.BlockSpec(memory_space=pltpu.VMEM)
    return pl.pallas_call(
        propagate_kernel,
        in_specs=[smem, smem, vmem, vmem, vmem],
        out_specs=vmem,
        out_shape=jax.ShapeDtypeStruct((comps, rows, lons), jnp.bfloat16),
        scratch_shapes=[
            pltpu.VMEM((rows, 128), jnp.float32),
            pltpu.VMEM((rows, 128), jnp.float32),
            pltpu.VMEM((rows, 128), jnp.float32),
            pltpu.VMEM((rows, 128), jnp.float32),
            pltpu.SemaphoreType.DMA((2,)),
            pltpu.SemaphoreType.DMA((2,)),
        ],
        compiler_params=pltpu.CompilerParams(
            collective_id=0, has_side_effects=True, vmem_limit_bytes=48 * 1024 * 1024
        ),
        cost_estimate=pl.CostEstimate(
            flops=30 * comps * rows * lons, bytes_accessed=6 * comps * rows * lons, transcendentals=0
        ),
    )(rate_x, rate_y, spectrum, factor, sea_float)


def local(
    spectrum,
    group_speed,
    depth_factor,
    sea_mask,
    interaction,
    wind_speed,
    wind_dir,
    nest_owner,
    nest_point,
    nest_cell,
    weight_index,
    weight_table,
):
    comp_dev = spectrum.shape[0]
    freq_count = group_speed.shape[0]
    comp_total = interaction.shape[0]
    dir_count = comp_total // freq_count
    spec_count = lax.axis_size("spec")
    grid_count = lax.axis_size("grid")
    heading, freq_index = headings(
        lax.axis_index("spec") * comp_dev, comp_dev, freq_count, dir_count
    )
    group_rate = jnp.take(group_speed, freq_index)
    rate_x = group_rate * jnp.cos(heading)
    rate_y = group_rate * jnp.sin(heading)
    sea_float = sea_mask.astype(jnp.float32)
    factor = depth_factor * sea_float
    lon_count = spectrum.shape[2]
    propagated = propagate(spectrum, rate_x, rate_y, factor, sea_float)

    row_count = spectrum.shape[1] // spec_count
    received = lax.all_to_all(propagated, "spec", split_axis=1, concat_axis=0, tiled=True)
    cell_count = row_count * lon_count
    spectra_now = received.astype(jnp.float32).reshape(comp_total, cell_count)
    sea_rows = lax.dynamic_slice_in_dim(sea_float, lax.axis_index("spec") * row_count, row_count, 0)
    sea_cells = sea_rows.reshape(-1)
    all_heading, all_freq = headings(0, comp_total, freq_count, dir_count)
    wind_gain = wind_term(
        all_heading, all_freq, freq_count, wind_speed.reshape(-1), wind_dir.reshape(-1)
    )
    for step_number in range(SOURCE_STEPS):
        spread = jnp.sqrt(jnp.mean(spectra_now * spectra_now, axis=0) + EPSILON)
        rounded = spectra_now.astype(jnp.bfloat16)
        transfer = jnp.dot(interaction, rounded, preferred_element_type=jnp.float32)
        spectra_now = (
            sea_cells[None]
            * (
                spectra_now
                + RATE * (wind_gain * spectra_now + spectra_now * transfer / spread[None])
            )
            / (1.0 + RATE * WHITECAP * spread[None])
        )

    slots = grid_count * CAP
    owners = nest_owner[:, 0]
    member = (owners[:, None] == jnp.arange(grid_count, dtype=jnp.int32)[None]).astype(jnp.int32)
    slot_rank = jnp.sum((jnp.cumsum(member, axis=0) - member) * member, axis=1)
    column = owners * CAP + slot_rank
    weights = jnp.take(weight_table, weight_index)
    pick_slot = (column[:, None] == jnp.arange(slots, dtype=jnp.int32)[None]).astype(jnp.float32)
    pick_cell = (nest_cell[:, None] == jnp.arange(cell_count, dtype=jnp.int32)[None]).astype(jnp.float32)
    slot_cell = jnp.dot(pick_slot.T, pick_cell, precision=HIGHEST, preferred_element_type=jnp.float32)
    slot_weight = jnp.dot(pick_slot.T, weights, precision=HIGHEST, preferred_element_type=jnp.float32)
    slot_label = jnp.dot(
        pick_slot.T, nest_point.astype(jnp.float32) + 1.0, precision=HIGHEST,
        preferred_element_type=jnp.float32,
    ) - 1.0
    gathered = lax.dot_general(
        slot_cell, spectra_now, (((1,), (1,)), ((), ())), precision=HIGHEST,
        preferred_element_type=jnp.float32,
    )
    send = jnp.concatenate([gathered * slot_weight[:, None], slot_label[:, None]], axis=1)
    send = send.astype(jnp.bfloat16).reshape(grid_count, CAP, comp_total + 1)
    arrived = lax.all_to_all(send, "grid", split_axis=0, concat_axis=0, tiled=True)
    arrived = arrived.reshape(slots, comp_total + 1)
    select = (arrived[:, comp_total][:, None] == jnp.arange(NB_OWN, dtype=jnp.bfloat16)[None]).astype(
        jnp.bfloat16
    )
    nest_spectra = lax.dot_general(
        arrived[:, :comp_total], select, (((0,), (0,)), ((), ())),
        preferred_element_type=jnp.float32,
    )
    return (spectra_now.reshape(comp_total, row_count, lon_count), nest_spectra)


def solution(mesh):
    in_specs = (
        P("spec", None, "grid"),
        P(),
        P(None, "grid"),
        P(None, "grid"),
        P(),
        P("spec", "grid"),
        P("spec", "grid"),
        P(("spec", "grid"), None),
        P(("spec", "grid")),
        P(("spec", "grid")),
        P(("spec", "grid")),
        P(),
    )
    out_specs = (P(None, "spec", "grid"), P(None, ("spec", "grid")))
    return jax.shard_map(local, mesh=mesh, in_specs=in_specs, out_specs=out_specs, check_vma=False)
```

profile of v0, /device:TPU:1, one launch (start us, length us, event | category | flops | bytes accessed | tf_op | source)
XLA Modules:
  0.0 155.9 jit_solution(11265999355072855400)
XLA Ops:
  0.7 1.6 %gather_fusion = f32[81]{0:T(128)S(1)} fusion(f32[36]{0:T(128)} %param.13, s32[1024]{0:T(1024)S(1)} %pad_clamp_fusion.1), kind=kCustom, calls=%fused_computation | custom fusion | bytes 972 | tf_op jit(solution)/shard_map/jit(_take)/gather | solution.py:159
  2.4 0.8 convert_element_type.53.sea_ref
  3.2 0.9 convert_multiply_fusion.2.factor_ref
  4.1 30.3 %shard_map.131 = bf16[81,64,256]{2,1,0:T(8,128)(2,1)S(1)} custom-call(f32[81]{0:T(128)S(1)} %cosine_multiply_fusion.rx_ref, f32[81]{0:T(128)S(1)} %get-tuple-element.4.ry_ref, f32[81,64,256]{2,1,0:T(8,128)} %spec_ref.1, f32[64,256]{1,0:T(8,128)S(1)} %convert_multiply_fusion.2.factor_ref, f32[64,256]{1,0:T(8,128)S(1)} %convert_element_type.53.sea_ref), custom_call_target="tpu_custom_call" | custom-call | flops 39813120 | bytes 7962624 | tf_op jit(solution)/shard_map/pallas_call | solution.py:114
  34.6 3.1 %copy.20 = bf16[81,64,256]{2,0,1:T(8,128)(2,1)} copy(bf16[81,64,256]{2,1,0:T(8,128)(2,1)S(1)} %shard_map.131) | data formatting | bytes 5308416 | tf_op jit(solution)/shard_map/pallas_call | solution.py:114
  37.7 6.8 %all-to-all-start = ((bf16[81,64,256]{2,0,1:T(8,128)(2,1)}), bf16[81,64,256]{2,0,1:T(8,128)(2,1)S(1)}, u32[]{:S(2)}, u32[]{:S(2)}) async-start(bf16[81,64,256]{2,0,1:T(8,128)(2,1)} %copy.20), calls=%async_computation | async-start | bytes 5767168 | tf_op jit(solution)/shard_map/all_to_all | solution.py:168
  45.2 0.3 concatenate.12
  45.5 1.4 gather_fusion.1
  47.2 1.5 fusion.29
  48.7 35.4 %all-to-all-done = bf16[81,64,256]{2,0,1:T(8,128)(2,1)S(1)} async-done(((bf16[81,64,256]{2,0,1:T(8,128)(2,1)}), bf16[81,64,256]{2,0,1:T(8,128)(2,1)S(1)}, u32[]{:S(2)}, u32[]{:S(2)}) %all-to-all-start) | async-done | bytes 2654240 | tf_op jit(solution)/shard_map/all_to_all | solution.py:168
  84.1 2.1 %multiply_reduce_fusion.3 = (f32[4,256]{1,0:T(4,128)S(1)}, bf16[81,16,4,256]{3,2,0,1:T(4,128)(2,1)S(1)}) fusion(bf16[81,16,4,256]{3,0,2,1:T(8,128)(2,1)S(1)} %bitcast.90), kind=kLoop, calls=%fused_computation.34 | loop fusion | flops 3980288 | bytes 5312512 | tf_op jit(solution)/shard_map/reduce_sum | solution.py:178
  86.2 0.6 copy.25
  86.9 6.6 %multiply_reduce_fusion.2 = (f32[1024]{0:T(1024)S(1)}, f32[1296,1024]{1,0:T(8,128)S(1)}) fusion(f32[1024]{0:T(1024)S(1)} %multiply_add_fusion.3, f32[1024]{0:T(1024)S(1)} %bitcast.97, bf16[1296,1296]{1,0:T(8,128)(2,1)S(1)} %copy-done.7, bf16[1296,1024]{1,0:T(8,128)(2,1)S(1)} %bitcast.95, f32[1024]{0:T(1024)S(1)} %bitcast.107, ...), kind=kOutput, calls=%fused_computation.33 | convolution fusion | flops 3462413312 | bytes 11366080 | tf_op jit(solution)/shard_map/dot_general | solution.py:180
  93.5 6.8 %multiply_reduce_fusion.1 = (f32[1024]{0:T(1024)S(1)}, f32[1296,1024]{1,0:T(8,128)S(1)}) fusion(f32[1024]{0:T(1024)S(1)} %get-tuple-element.11, f32[1296,1024]{1,0:T(8,128)S(1)} %get-tuple-element.15, f32[1024]{0:T(1024)S(1)} %get-tuple-element.10, bf16[1296,1296]{1,0:T(8,128)(2,1)S(1)} %copy-done.7, f32[1024]{0:T(1024)S(1)} %bitcast.108, ...), kind=kOutput, calls=%fused_computation.32 | convolution fusion | flops 3462413312 | bytes 14020288 | tf_op jit(solution)/shard_map/dot_general | solution.py:180
  100.4 6.5 %multiply_reduce_fusion = (f32[1024]{0:T(1024)S(1)}, f32[1296,1024]{1,0:T(8,128)S(1)}) fusion(f32[1024]{0:T(1024)S(1)} %get-tuple-element.9, f32[1296,1024]{1,0:T(8,128)S(1)} %get-tuple-element.17, f32[1024]{0:T(1024)S(1)} %get-tuple-element.8, bf16[1296,1296]{1,0:T(8,128)(2,1)S(1)} %copy-done.7, f32[1024]{0:T(1024)S(1)} %bitcast.109, ...), kind=kOutput, calls=%fused_computation.31 | convolution fusion | flops 3462413312 | bytes 14020288 | tf_op jit(solution)/shard_map/dot_general | solution.py:180
  106.9 6.2 %fusion.10 = f32[1296,1024]{1,0:T(8,128)S(1)} fusion(f32[1296,1024]{1,0:T(8,128)S(1)} %get-tuple-element.19, bf16[1296,1296]{1,0:T(8,128)(2,1)S(1)} %copy-done.7, f32[1024]{0:T(1024)S(1)} %get-tuple-element.7, f32[1024]{0:T(1024)S(1)} %get-tuple-element.6, f32[1024]{0:T(1024)S(1)} %bitcast.110, f32[1296]{0:T(1024)S(1)} %get-tuple-element.21, ...), kind=kOutput, calls=%fused_computation.16 | convolution fusion | flops 3459760128 | bytes 14016192 | tf_op jit(solution)/shard_map/dot_general | solution.py:180
  113.1 2.3 %copy-done.1 = f32[1296,1024]{1,0:T(8,128)} copy-done((f32[1296,1024]{1,0:T(8,128)}, f32[1296,1024]{1,0:T(8,128)S(1)}, u32[]{:S(2)}) %copy-start.1) | copy-done | bytes 5308440
  115.4 4.6 %fusion.26 = bf16[256,1296]{0,1:T(8,128)(2,1)S(1)} fusion(f32[256,1024]{1,0:T(8,128)S(1)} %copy-done.2, f32[1296,1024]{1,0:T(8,128)S(1)} %fusion.10, f32[256]{0:T(256)S(1)} %bitcast.117), kind=kOutput, calls=%fused_computation.40 | convolution fusion | flops 4077527040 | bytes 7021568 | tf_op jit(solution)/shard_map/dot_general | solution.py:204
  120.0 0.3 copy.22
  120.4 1.0 pad_maximum_fusion
  121.4 11.7 %all-to-all-start.1 = ((bf16[16,16,1297]{2,1,0:T(8,128)(2,1)}), bf16[16,16,1297]{2,1,0:T(8,128)(2,1)S(1)}, u32[]{:S(2)}, u32[]{:S(2)}) async-start(bf16[16,16,1297]{2,1,0:T(8,128)(2,1)} %pad_maximum_fusion), calls=%async_computation.1 | async-start | bytes 1441792 | tf_op jit(solution)/shard_map/all_to_all | solution.py:210
  133.1 7.6 %reshape.167 = f32[1296,4,256]{2,1,0:T(4,128)} reshape(f32[1296,1024]{1,0:T(8,128)} %copy-done.1) | data formatting | bytes 10616832 | tf_op jit(solution)/shard_map/reshape | solution.py:219
  140.8 13.7 %all-to-all-done.1 = bf16[16,16,1297]{2,1,0:T(8,128)(2,1)S(1)} async-done(((bf16[16,16,1297]{2,1,0:T(8,128)(2,1)}), bf16[16,16,1297]{2,1,0:T(8,128)(2,1)S(1)}, u32[]{:S(2)}, u32[]{:S(2)}) %all-to-all-start.1) | async-done | bytes 664096 | tf_op jit(solution)/shard_map/all_to_all | solution.py:210
  154.6 1.3 fusion.27
  (47 shorter events, 1.3 us)
Async XLA Ops:
  0.6 44.9 %copy-start = (f32[64]{0:T(128)S(1)}, f32[64]{0:T(128)}, u32[]{:S(2)}) copy-start(f32[64]{0:T(128)} %param.23) | copy-start | bytes 772
  34.5 10.0 %copy-start.3 = (f32[4,256]{1,0:T(4,128)S(1)}, f32[4,256]{1,0:T(4,128)}, u32[]{:S(2)}) copy-start(f32[4,256]{1,0:T(4,128)} %param.18) | copy-start | bytes 12292
  34.5 10.1 %copy-start.4 = (f32[4,256]{1,0:T(4,128)S(1)}, f32[4,256]{1,0:T(4,128)}, u32[]{:S(2)}) copy-start(f32[4,256]{1,0:T(4,128)} %param.17) | copy-start | bytes 12292
  34.5 10.1 %copy-start.5 = (s32[128,1]{0,1:T(1,128)S(1)}, s32[128,1]{0,1:T(1,128)}, u32[]{:S(2)}) copy-start(s32[128,1]{0,1:T(1,128)} %param.19) | copy-start | bytes 1540
  34.5 10.5 %copy-start.8 = (s32[128]{0:T(128)S(1)}, s32[128]{0:T(128)}, u32[]{:S(2)}) copy-start(s32[128]{0:T(128)} %param.20) | copy-start | bytes 1540
  34.5 11.0 %copy-start.9 = (s32[128]{0:T(128)S(1)}, s32[128]{0:T(128)}, u32[]{:S(2)}) copy-start(s32[128]{0:T(128)} %param.22) | copy-start | bytes 1540
  34.5 12.6 %copy-start.6 = (s32[128]{0:T(128)S(1)}, s32[128]{0:T(128)}, u32[]{:S(2)}) copy-start(s32[128]{0:T(128)} %param.21) | copy-start | bytes 1540
  37.7 46.4 %all-to-all-start = ((bf16[81,64,256]{2,0,1:T(8,128)(2,1)}), bf16[81,64,256]{2,0,1:T(8,128)(2,1)S(1)}, u32[]{:S(2)}, u32[]{:S(2)}) async-start(bf16[81,64,256]{2,0,1:T(8,128)(2,1)} %copy.20), calls=%async_computation | async-start | bytes 5767168 | tf_op jit(solution)/shard_map/all_to_all | solution.py:168
  84.1 2.8 %copy-start.7 = (bf16[1296,1296]{1,0:T(8,128)(2,1)S(1)}, bf16[1296,1296]{1,0:T(8,128)(2,1)}, u32[]{:S(2)}) copy-start(bf16[1296,1296]{1,0:T(8,128)(2,1)} %param.16) | copy-start | bytes 10077700
  106.9 8.5 %copy-start.2 = (f32[256,1024]{1,0:T(8,128)S(1)}, f32[256,1024]{1,0:T(8,128)}, u32[]{:S(2)}) copy-start(f32[256,1024]{1,0:T(8,128)} %fusion.29) | copy-start | bytes 3145732
  113.1 2.3 %copy-start.1 = (f32[1296,1024]{1,0:T(8,128)}, f32[1296,1024]{1,0:T(8,128)S(1)}, u32[]{:S(2)}) copy-start(f32[1296,1024]{1,0:T(8,128)S(1)} %fusion.10) | copy-start | bytes 15925252
  121.4 33.1 %all-to-all-start.1 = ((bf16[16,16,1297]{2,1,0:T(8,128)(2,1)}), bf16[16,16,1297]{2,1,0:T(8,128)(2,1)S(1)}, u32[]{:S(2)}, u32[]{:S(2)}) async-start(bf16[16,16,1297]{2,1,0:T(8,128)(2,1)} %pad_maximum_fusion), calls=%async_computation.1 | async-start | bytes 1441792 | tf_op jit(solution)/shard_map/all_to_all | solution.py:210
where the time goes:
time: 156 us
  waiting for transfers between devices  49.1 us (31%)
  matrix products  33.8 us (22%)
  Pallas kernels  30.3 us (19%)
  starting transfers between devices  18.5 us (12%)
  local copies, waits for them, and re-layouts  17.6 us (11%)
  other arithmetic  5.6 us (4%)
    all_to_all x1, waiting for transfers between devices, local(): lax.all_to_all(propagated, 'spec', split_axis=1, concat_axis=0, tiled=True)  35.4 us
    pallas_call x1, Pallas kernels, propagate(): pl.pallas_call(propagate_kernel, in_specs=[smem, smem, vmem, vmem, vmem],...  30.3 us
    dot_general x4, matrix products, local(): transfer = jnp.dot(interaction, rounded, preferred_element_type=jnp.float32)  26.1 us
    all_to_all x1, waiting for transfers between devices, local(): lax.all_to_all(send, 'grid', split_axis=0, concat_axis=0, tiled=True)  13.7 us
    all_to_all x1, starting transfers between devices, local(): lax.all_to_all(send, 'grid', split_axis=0, concat_axis=0, tiled=True)  11.7 us
    reshape x1, local copies, waits for them, and re-layouts, local(): return (spectra_now.reshape(comp_total, row_count, lon_count), nest_spectra)  7.64 us
    all_to_all x1, starting transfers between devices, local(): lax.all_to_all(propagated, 'spec', split_axis=1, concat_axis=0, tiled=True)  6.75 us
    dot_general x1, matrix products, local(): lax.dot_general(slot_cell, spectra_now, (((1,), (1,)), ((), ())), precisi...  4.65 us
  transfers between devices with their start and end apart: 2, of which 2 were waited for; matrix products, arithmetic and copies ran while one was open for 8% of the time, Pallas kernels for 0%

commit v1 on v0

--- a/solution.py
+++ b/solution.py
@@ -39,9 +39,12 @@
 def propagate_kernel(
     rx_ref, ry_ref, spec_ref, factor_ref, sea_ref, out_ref,
     send_first, send_last, recv_west, recv_east, send_sem, recv_sem,
+    result_lo, result_hi, send_buf, a2a_send, a2a_recv,
 ):
     comps, rows, lons = spec_ref.shape
+    spec_count = lax.axis_size("spec")
     grid_count = lax.axis_size("grid")
+    chunk = rows // spec_count
     me = lax.axis_index("grid")
     spec = lax.axis_index("spec")
     right = lax.rem(me + 1, grid_count)
@@ -49,7 +52,15 @@
     barrier = pltpu.get_barrier_semaphore()
     for neighbour in (left, right):
         pl.semaphore_signal(barrier, inc=1, device_id=(spec, neighbour), device_id_type=pl.DeviceIdType.MESH)
-    pl.semaphore_wait(barrier, 2)
+
+    def greet(d, carry):
+        @pl.when(d != spec)
+        def _():
+            pl.semaphore_signal(barrier, inc=1, device_id=(d, me), device_id_type=pl.DeviceIdType.MESH)
+        return carry
+
+    lax.fori_loop(0, spec_count, greet, 0)
+    pl.semaphore_wait(barrier, 2 + spec_count - 1)
 
     factor = factor_ref[...]
     sea = sea_ref[...]
@@ -67,7 +78,7 @@
         return first, last
 
     zero = jnp.zeros((rows, 128), jnp.float32)
-    first, last = lax.fori_loop(0, comps, edges, (zero, zero))
+    first, last = lax.fori_loop(0, comps, edges, (zero, zero), unroll=3)
     send_first[...] = first
     send_last[...] = last
     to_right = pltpu.make_async_remote_copy(
@@ -101,21 +112,60 @@
         south = jnp.where(row == 0, 0.0, pltpu.roll(fy, 1, 0))
         north = jnp.where(row == rows - 1, 0.0, pltpu.roll(fy, rows - 1, 0))
         change_y = jnp.where(ry > 0, fy - south, north - fy)
-        out_ref[kk] = (sea * (ax - change_y)).astype(out_ref.dtype)
-        return carry
-
-    lax.fori_loop(0, comps, one, 0)
-
-
-def propagate(spectrum, rate_x, rate_y, factor, sea_float):
+        res = sea * (ax - change_y)
+        place = pl.ds(pl.multiple_of(kk * rows, rows), rows)
+        result_lo[place, :] = res[:, :128]
+        result_hi[place, :] = res[:, 128:]
+        return carry
+
+    lax.fori_loop(0, comps, one, 0, unroll=3)
+
+    def copy_to(d, slot):
+        return pltpu.make_async_remote_copy(
+            src_ref=send_buf.at[d], dst_ref=out_ref.at[slot], send_sem=a2a_send.at[d],
+            recv_sem=a2a_recv.at[slot], device_id=(d, me), device_id_type=pl.DeviceIdType.MESH,
+        )
+
+    def regroup(d, carry):
+        for r in range(chunk):
+            i = d * chunk + r
+            for half, part in ((0, result_lo), (1, result_hi)):
+                at = r * lons + half * 128
+                send_buf[d, :, at : at + 128] = part[pl.ds(i, comps, stride=rows), :].astype(send_buf.dtype)
+
+        @pl.when(d != spec)
+        def _():
+            copy_to(d, spec).start()
+
+        @pl.when(d == spec)
+        def _():
+            out_ref[d] = send_buf[d]
+
+        return carry
+
+    lax.fori_loop(0, spec_count, regroup, 0)
+
+    def finish(d, carry):
+        @pl.when(d != spec)
+        def _():
+            copy_to(d, d).wait_send()
+            copy_to(d, d).wait_recv()
+
+        return carry
+
+    lax.fori_loop(0, spec_count, finish, 0)
+
+
+def propagate(spectrum, rate_x, rate_y, factor, sea_float, spec_count):
     comps, rows, lons = spectrum.shape
+    chunk = rows // spec_count
     smem = pl.BlockSpec(memory_space=pltpu.SMEM)
     vmem = pl.BlockSpec(memory_space=pltpu.VMEM)
     return pl.pallas_call(
         propagate_kernel,
         in_specs=[smem, smem, vmem, vmem, vmem],
         out_specs=vmem,
-        out_shape=jax.ShapeDtypeStruct((comps, rows, lons), jnp.bfloat16),
+        out_shape=jax.ShapeDtypeStruct((spec_count, comps, chunk * lons), jnp.bfloat16),
         scratch_shapes=[
             pltpu.VMEM((rows, 128), jnp.float32),
             pltpu.VMEM((rows, 128), jnp.float32),
@@ -123,9 +173,14 @@
             pltpu.VMEM((rows, 128), jnp.float32),
             pltpu.SemaphoreType.DMA((2,)),
             pltpu.SemaphoreType.DMA((2,)),
+            pltpu.VMEM((comps * rows, 128), jnp.float32),
+            pltpu.VMEM((comps * rows, 128), jnp.float32),
+            pltpu.VMEM((spec_count, comps, chunk * lons), jnp.bfloat16),
+            pltpu.SemaphoreType.DMA((spec_count,)),
+            pltpu.SemaphoreType.DMA((spec_count,)),
         ],
         compiler_params=pltpu.CompilerParams(
-            collective_id=0, has_side_effects=True, vmem_limit_bytes=48 * 1024 * 1024
+            collective_id=0, has_side_effects=True, vmem_limit_bytes=56 * 1024 * 1024
         ),
         cost_estimate=pl.CostEstimate(
             flops=30 * comps * rows * lons, bytes_accessed=6 * comps * rows * lons, transcendentals=0
@@ -162,10 +217,8 @@
     sea_float = sea_mask.astype(jnp.float32)
     factor = depth_factor * sea_float
     lon_count = spectrum.shape[2]
-    propagated = propagate(spectrum, rate_x, rate_y, factor, sea_float)
-
+    received = propagate(spectrum, rate_x, rate_y, factor, sea_float, spec_count)
     row_count = spectrum.shape[1] // spec_count
-    received = lax.all_to_all(propagated, "spec", split_axis=1, concat_axis=0, tiled=True)
     cell_count = row_count * lon_count
     spectra_now = received.astype(jnp.float32).reshape(comp_total, cell_count)
     sea_rows = lax.dynamic_slice_in_dim(sea_float, lax.axis_index("spec") * row_count, row_count, 0)

time: 156 us -> 177 us (1.13); the launches traced: 156 us -> 174 us
  Pallas kernels: 30.3 us -> 67.1 us
  waiting for transfers between devices: 49.1 us -> 13.7 us
  matrix products: 33.8 us -> 43.5 us
  starting transfers between devices: 18.5 us -> 22 us
  other arithmetic: 5.6 us -> 8.24 us
    pallas_call x1, Pallas kernels: 30.3 us -> 67.1 us  [propagate(): pl.pallas_call(propagate_kernel, in_specs=[smem, smem, vmem, vmem, vmem],...]
    all_to_all x1 -> x0, waiting for transfers between devices: 35.4 us -> none  [local(): lax.all_to_all(propagated, 'spec', split_axis=1, concat_axis=0, tiled=True)]
    dot_general x4, matrix products: 26.1 us -> 37.2 us  [local(): transfer = jnp.dot(interaction, rounded, preferred_element_type=jnp.float32)]
    all_to_all x1, starting transfers between devices: 11.7 us -> 22 us  [local(): lax.all_to_all(send, 'grid', split_axis=0, concat_axis=0, tiled=True)]
    all_to_all x1 -> x0, starting transfers between devices: 6.75 us -> none  [local(): lax.all_to_all(propagated, 'spec', split_axis=1, concat_axis=0, tiled=True)]
    reshape x0 -> x1, local copies, waits for them, and re-layouts: none -> 4.08 us  [local(): spectra_now = received.astype(jnp.float32).reshape(comp_total, cell_count)]
    pallas_call x1 -> x0, local copies, waits for them, and re-layouts: 3.12 us -> none  [propagate(): pl.pallas_call(propagate_kernel, in_specs=[smem, smem, vmem, vmem, vmem],...]
  transfers between devices with their start and end apart: 2 -> 1, of which waited for: 2 -> 1; matrix products, arithmetic and copies ran while one was open for 8% -> 4% of each run, Pallas kernels for 0% -> 0%
where the time goes in v1:
time: 177 us; the launch traced here: 174 us
  Pallas kernels  67.1 us (38%)
  matrix products  43.5 us (25%)
  starting transfers between devices  22 us (12%)
  local copies, waits for them, and re-layouts  18.5 us (10%)
  waiting for transfers between devices  13.7 us (8%)
  other arithmetic  8.24 us (5%)
    pallas_call x1, Pallas kernels, propagate(): pl.pallas_call(propagate_kernel, in_specs=[smem, smem, vmem, vmem, vmem],...  67.1 us
    dot_general x4, matrix products, local(): transfer = jnp.dot(interaction, rounded, preferred_element_type=jnp.float32)  37.2 us
    all_to_all x1, starting transfers between devices, local(): lax.all_to_all(send, 'grid', split_axis=0, concat_axis=0, tiled=True)  22 us
    all_to_all x1, waiting for transfers between devices, local(): lax.all_to_all(send, 'grid', split_axis=0, concat_axis=0, tiled=True)  13.7 us
    reshape x1, local copies, waits for them, and re-layouts, local(): return (spectra_now.reshape(comp_total, row_count, lon_count), nest_spectra)  7.64 us
    dot_general x1, matrix products, local(): lax.dot_general(slot_cell, spectra_now, (((1,), (1,)), ((), ())), precisi...  4.38 us
    reshape x1, local copies, waits for them, and re-layouts, local(): spectra_now = received.astype(jnp.float32).reshape(comp_total, cell_count)  4.08 us
  transfers between devices with their start and end apart: 1, of which 1 were waited for; matrix products, arithmetic and copies ran while one was open for 4% of the time, Pallas kernels for 0%

profile of v1, /device:TPU:1, one launch (start us, length us, event | category | flops | bytes accessed | tf_op | source)
XLA Modules:
  0.0 173.9 jit_solution(14853566493616442799)
XLA Ops:
  0.7 1.6 gather_fusion
  2.3 0.6 sine_multiply_fusion
  2.9 0.6 cosine_multiply_fusion.rx_ref
  3.4 1.5 convert_element_type.51.sea_ref
  4.9 1.5 convert_multiply_fusion.factor_ref
  6.4 67.1 %shard_map.131 = bf16[16,81,1024]{2,1,0:T(8,128)(2,1)} custom-call(f32[81]{0:T(128)} %cosine_multiply_fusion.rx_ref, f32[81]{0:T(128)} %get-tuple-element.2.ry_ref, f32[81,64,256]{2,1,0:T(8,128)} %spec_ref.1, f32[64,256]{1,0:T(8,128)} %convert_multiply_fusion.factor_ref, f32[64,256]{1,0:T(8,128)} %convert_element_type.51.sea_ref), custom_call_target="tpu_custom_call" | custom-call | flops 39813120 | bytes 7962624 | tf_op jit(solution)/shard_map/pallas_call | solution.py:164
  73.5 2.5 %multiply_reduce_fusion = f32[1024]{0:T(1024)S(1)} fusion(bf16[16,81,1024]{2,1,0:T(8,128)(2,1)} %shard_map.131), kind=kLoop, calls=%fused_computation.2 | loop fusion | flops 3980288 | bytes 2658304 | tf_op jit(solution)/shard_map/reduce_sum | solution.py:231
  76.0 4.1 %reshape.157 = f32[1296,1024]{1,0:T(8,128)} reshape(bf16[16,81,1024]{2,1,0:T(8,128)(2,1)} %shard_map.131) | data formatting | bytes 7962624 | tf_op jit(solution)/shard_map/reshape | solution.py:223
  80.2 0.7 dynamic-slice_bitcast_fusion
  81.1 11.4 %multiply_reduce_fusion.3 = (f32[1024]{0:T(1024)S(1)}, f32[1296,1024]{1,0:T(8,128)S(1)}) fusion(f32[1024]{0:T(1024)S(1)} %get-tuple-element.13, f32[1296,1024]{1,0:T(8,128)} %reshape.157, f32[1024]{0:T(1024)S(1)} %get-tuple-element.12, bf16[1296,1296]{1,0:T(8,128)(2,1)} %param.16, f32[1024]{0:T(1024)S(1)} %bitcast.104, f32[1296]{0:T(1024)S(1)} %get-tuple-element.21, ...), kind=kOutput, calls=%fused_computation.33 | convolution fusion | flops 3462413312 | bytes 14020288 | tf_op jit(solution)/shard_map/dot_general | solution.py:233
  92.5 6.6 %multiply_reduce_fusion.2 = (f32[1024]{0:T(1024)S(1)}, f32[1296,1024]{1,0:T(8,128)S(1)}) fusion(f32[1024]{0:T(1024)S(1)} %get-tuple-element.9, f32[1296,1024]{1,0:T(8,128)S(1)} %get-tuple-element.15, f32[1024]{0:T(1024)S(1)} %get-tuple-element.8, bf16[1296,1296]{1,0:T(8,128)(2,1)S(1)} %copy-done.6, f32[1024]{0:T(1024)S(1)} %bitcast.105, ...), kind=kOutput, calls=%fused_computation.32 | convolution fusion | flops 3462413312 | bytes 14020288 | tf_op jit(solution)/shard_map/dot_general | solution.py:233
  99.2 8.1 %multiply_reduce_fusion.1 = (f32[1024]{0:T(1024)S(1)}, f32[1296,1024]{1,0:T(8,128)}) fusion(f32[1024]{0:T(1024)S(1)} %get-tuple-element.7, f32[1296,1024]{1,0:T(8,128)S(1)} %get-tuple-element.17, f32[1024]{0:T(1024)S(1)} %get-tuple-element.6, bf16[1296,1296]{1,0:T(8,128)(2,1)S(1)} %copy-done.6, f32[1024]{0:T(1024)S(1)} %bitcast.106, ...), kind=kOutput, calls=%fused_computation.31 | convolution fusion | flops 3462413312 | bytes 14020288 | tf_op jit(solution)/shard_map/dot_general | solution.py:233
  107.8 0.4 fusion.31
  108.2 1.2 gather_fusion.1
  109.6 11.1 %fusion.5 = f32[1296,1024]{1,0:T(8,128)S(1)} fusion(f32[1296,1024]{1,0:T(8,128)} %get-tuple-element.19, bf16[1296,1296]{1,0:T(8,128)(2,1)} %param.16, f32[1024]{0:T(1024)S(1)} %get-tuple-element.5, f32[1024]{0:T(1024)S(1)} %get-tuple-element.4, f32[1024]{0:T(1024)S(1)} %bitcast.107, f32[1296]{0:T(1024)S(1)} %get-tuple-element.21, f32[1024]{0:T(1024)S(1)} %bitcast.103, ...), kind=kOutput, calls=%fused_computation.9 | convolution fusion | flops 3459760128 | bytes 14016192 | tf_op jit(solution)/shard_map/dot_general | solution.py:233
  120.7 2.3 %copy-done.1 = f32[1296,1024]{1,0:T(8,128)} copy-done((f32[1296,1024]{1,0:T(8,128)}, f32[1296,1024]{1,0:T(8,128)S(1)}, u32[]{:S(2)}) %copy-start.1) | copy-done | bytes 5308440
  123.0 4.4 %fusion.28 = bf16[256,1296]{0,1:T(8,128)(2,1)S(1)} fusion(f32[256,1024]{1,0:T(8,128)S(1)} %fusion.31, f32[1296,1024]{1,0:T(8,128)S(1)} %fusion.5, f32[256]{0:T(256)S(1)} %bitcast.114), kind=kOutput, calls=%fused_computation.40 | convolution fusion | flops 4077527040 | bytes 7021568 | tf_op jit(solution)/shard_map/dot_general | solution.py:257
  127.4 0.3 copy.15
  127.9 0.3 concatenate.12
  128.2 1.0 pad_maximum_fusion
  129.2 22.0 %all-to-all-start = ((bf16[16,16,1297]{2,1,0:T(8,128)(2,1)}), bf16[16,16,1297]{2,1,0:T(8,128)(2,1)S(1)}, u32[]{:S(2)}, u32[]{:S(2)}) async-start(bf16[16,16,1297]{2,1,0:T(8,128)(2,1)} %pad_maximum_fusion), calls=%async_computation | async-start | bytes 1441792 | tf_op jit(solution)/shard_map/all_to_all | solution.py:263
  151.2 7.6 %reshape.158 = f32[1296,4,256]{2,1,0:T(4,128)} reshape(f32[1296,1024]{1,0:T(8,128)} %copy-done.1) | data formatting | bytes 10616832 | tf_op jit(solution)/shard_map/reshape | solution.py:272
  158.8 13.7 %all-to-all-done = bf16[16,16,1297]{2,1,0:T(8,128)(2,1)S(1)} async-done(((bf16[16,16,1297]{2,1,0:T(8,128)(2,1)}), bf16[16,16,1297]{2,1,0:T(8,128)(2,1)S(1)}, u32[]{:S(2)}, u32[]{:S(2)}) %all-to-all-start) | async-done | bytes 664096 | tf_op jit(solution)/shard_map/all_to_all | solution.py:263
  172.7 1.3 fusion.29
  (40 shorter events, 1.2 us)
Async XLA Ops:
  0.6 107.6 %copy-start = (f32[64]{0:T(128)S(1)}, f32[64]{0:T(128)}, u32[]{:S(2)}) copy-start(f32[64]{0:T(128)} %param.23) | copy-start | bytes 772
  73.5 7.4 %copy-start.2 = (f32[4,256]{1,0:T(4,128)S(1)}, f32[4,256]{1,0:T(4,128)}, u32[]{:S(2)}) copy-start(f32[4,256]{1,0:T(4,128)} %param.18) | copy-start | bytes 12292
  73.5 7.5 %copy-start.3 = (f32[4,256]{1,0:T(4,128)S(1)}, f32[4,256]{1,0:T(4,128)}, u32[]{:S(2)}) copy-start(f32[4,256]{1,0:T(4,128)} %param.17) | copy-start | bytes 12292
  81.1 11.4 %copy-start.6 = (bf16[1296,1296]{1,0:T(8,128)(2,1)S(1)}, bf16[1296,1296]{1,0:T(8,128)(2,1)}, u32[]{:S(2)}) copy-start(bf16[1296,1296]{1,0:T(8,128)(2,1)} %param.16) | copy-start | bytes 10077700
  99.1 8.2 %copy-start.4 = (s32[128,1]{0,1:T(1,128)S(1)}, s32[128,1]{0,1:T(1,128)}, u32[]{:S(2)}) copy-start(s32[128,1]{0,1:T(1,128)} %param.19) | copy-start | bytes 1540
  99.1 8.6 %copy-start.7 = (s32[128]{0:T(128)S(1)}, s32[128]{0:T(128)}, u32[]{:S(2)}) copy-start(s32[128]{0:T(128)} %param.22) | copy-start | bytes 1540
  99.1 8.7 %copy-start.5 = (s32[128]{0:T(128)S(1)}, s32[128]{0:T(128)}, u32[]{:S(2)}) copy-start(s32[128]{0:T(128)} %param.21) | copy-start | bytes 1540
  120.7 2.3 %copy-start.1 = (f32[1296,1024]{1,0:T(8,128)}, f32[1296,1024]{1,0:T(8,128)S(1)}, u32[]{:S(2)}) copy-start(f32[1296,1024]{1,0:T(8,128)S(1)} %fusion.5) | copy-start | bytes 15925252
  120.7 7.0 %copy-start.8 = (s32[128]{0:T(128)S(1)}, s32[128]{0:T(128)}, u32[]{:S(2)}) copy-start(s32[128]{0:T(128)} %param.20) | copy-start | bytes 1540
  129.2 43.3 %all-to-all-start = ((bf16[16,16,1297]{2,1,0:T(8,128)(2,1)}), bf16[16,16,1297]{2,1,0:T(8,128)(2,1)S(1)}, u32[]{:S(2)}, u32[]{:S(2)}) async-start(bf16[16,16,1297]{2,1,0:T(8,128)(2,1)} %pad_maximum_fusion), calls=%async_computation | async-start | bytes 1441792 | tf_op jit(solution)/shard_map/all_to_all | solution.py:263

commit v2 on v1

--- a/solution.py
+++ b/solution.py
@@ -118,38 +118,46 @@
         result_hi[place, :] = res[:, 128:]
         return carry
 
-    lax.fori_loop(0, comps, one, 0, unroll=3)
-
-    def copy_to(d, slot):
+    def copy_to(d, slot, start, size):
         return pltpu.make_async_remote_copy(
-            src_ref=send_buf.at[d], dst_ref=out_ref.at[slot], send_sem=a2a_send.at[d],
-            recv_sem=a2a_recv.at[slot], device_id=(d, me), device_id_type=pl.DeviceIdType.MESH,
+            src_ref=send_buf.at[d, pl.ds(start, size)], dst_ref=out_ref.at[slot, pl.ds(start, size)],
+            send_sem=a2a_send.at[d], recv_sem=a2a_recv.at[slot], device_id=(d, me),
+            device_id_type=pl.DeviceIdType.MESH,
         )
 
-    def regroup(d, carry):
-        for r in range(chunk):
-            i = d * chunk + r
-            for half, part in ((0, result_lo), (1, result_hi)):
-                at = r * lons + half * 128
-                send_buf[d, :, at : at + 128] = part[pl.ds(i, comps, stride=rows), :].astype(send_buf.dtype)
-
-        @pl.when(d != spec)
-        def _():
-            copy_to(d, spec).start()
-
-        @pl.when(d == spec)
-        def _():
-            out_ref[d] = send_buf[d]
-
-        return carry
-
-    lax.fori_loop(0, spec_count, regroup, 0)
+    tile = 16
+    count = comps // tile
+    blocks = [(tile * b, tile) for b in range(count - 1)]
+    blocks.append((tile * (count - 1), comps - tile * (count - 1)))
+    for start, size in blocks:
+        lax.fori_loop(start, start + size, one, 0)
+
+        def regroup(d, carry, start=start, size=size):
+            for r in range(chunk):
+                i = start * rows + d * chunk + r
+                for half, part in ((0, result_lo), (1, result_hi)):
+                    at = r * lons + half * 128
+                    send_buf[d, pl.ds(start, size), at : at + 128] = part[
+                        pl.ds(i, size, stride=rows), :
+                    ].astype(send_buf.dtype)
+
+            @pl.when(d != spec)
+            def _():
+                copy_to(d, spec, start, size).start()
+
+            @pl.when(d == spec)
+            def _():
+                out_ref[d, pl.ds(start, size), :] = send_buf[d, pl.ds(start, size), :]
+
+            return carry
+
+        lax.fori_loop(0, spec_count, regroup, 0)
 
     def finish(d, carry):
         @pl.when(d != spec)
         def _():
-            copy_to(d, d).wait_send()
-            copy_to(d, d).wait_recv()
+            copy_to(d, d, 0, comps).wait_send()
+            copy_to(d, d, 0, comps).wait_recv()
 
         return carry
 

time: 177 us -> 150 us (0.85); the launches traced: 174 us -> 150 us
  starting transfers between devices: 22 us -> 9.03 us
  Pallas kernels: 67.1 us -> 55.7 us
    all_to_all x1, starting transfers between devices: 22 us -> 9.03 us  [local(): lax.all_to_all(send, 'grid', split_axis=0, concat_axis=0, tiled=True)]
    pallas_call x1, Pallas kernels: 67.1 us -> 55.7 us  [propagate(): pl.pallas_call(propagate_kernel, in_specs=[smem, smem, vmem, vmem, vmem],...]
  transfers between devices with their start and end apart: 1 -> 1, of which waited for: 1 -> 1; matrix products, arithmetic and copies ran while one was open for 4% -> 5% of each run, Pallas kernels for 0% -> 0%
where the time goes in v2:
time: 150 us
  Pallas kernels  55.7 us (37%)
  matrix products  43.5 us (29%)
  local copies, waits for them, and re-layouts  18.5 us (12%)
  waiting for transfers between devices  13.7 us (9%)
  starting transfers between devices  9.03 us (6%)
  other arithmetic  8.24 us (5%)
    pallas_call x1, Pallas kernels, propagate(): pl.pallas_call(propagate_kernel, in_specs=[smem, smem, vmem, vmem, vmem],...  55.7 us
    dot_general x4, matrix products, local(): transfer = jnp.dot(interaction, rounded, preferred_element_type=jnp.float32)  37.2 us
    all_to_all x1, waiting for transfers between devices, local(): lax.all_to_all(send, 'grid', split_axis=0, concat_axis=0, tiled=True)  13.7 us
    all_to_all x1, starting transfers between devices, local(): lax.all_to_all(send, 'grid', split_axis=0, concat_axis=0, tiled=True)  9.03 us
    reshape x1, local copies, waits for them, and re-layouts, local(): return (spectra_now.reshape(comp_total, row_count, lon_count), nest_spectra)  7.64 us
    dot_general x1, matrix products, local(): lax.dot_general(slot_cell, spectra_now, (((1,), (1,)), ((), ())), precisi...  4.38 us
    reshape x1, local copies, waits for them, and re-layouts, local(): spectra_now = received.astype(jnp.float32).reshape(comp_total, cell_count)  4.08 us
    unnamed x24, local copies, waits for them, and re-layouts  3.12 us
  transfers between devices with their start and end apart: 1, of which 1 were waited for; matrix products, arithmetic and copies ran while one was open for 5% of the time, Pallas kernels for 0%

profile of v2, /device:TPU:1, one launch (start us, length us, event | category | flops | bytes accessed | tf_op | source)
XLA Modules:
  0.0 149.6 jit_solution(3636543002661232619)
XLA Ops:
  0.7 1.6 %gather_fusion = f32[81]{0:T(128)S(1)} fusion(f32[36]{0:T(128)} %param.13, s32[1024]{0:T(1024)S(1)} %pad_clamp_fusion.1), kind=kCustom, calls=%fused_computation | custom fusion | bytes 972 | tf_op jit(solution)/shard_map/jit(_take)/gather | solution.py:222
  2.3 0.6 sine_multiply_fusion
  2.9 0.6 cosine_multiply_fusion.rx_ref
  3.4 1.5 convert_element_type.51.sea_ref
  4.9 1.5 %convert_multiply_fusion.factor_ref = f32[64,256]{1,0:T(8,128)} fusion(f32[64,256]{1,0:T(8,128)} %param.14, s32[64,256]{1,0:T(8,128)} %param.15), kind=kLoop, calls=%fused_computation.121 | loop fusion | flops 32768 | bytes 196608 | tf_op jit(solution)/shard_map/mul | solution.py:226
  6.4 55.7 %shard_map.131 = bf16[16,81,1024]{2,1,0:T(8,128)(2,1)} custom-call(f32[81]{0:T(128)} %cosine_multiply_fusion.rx_ref, f32[81]{0:T(128)} %get-tuple-element.2.ry_ref, f32[81,64,256]{2,1,0:T(8,128)} %spec_ref.1, f32[64,256]{1,0:T(8,128)} %convert_multiply_fusion.factor_ref, f32[64,256]{1,0:T(8,128)} %convert_element_type.51.sea_ref), custom_call_target="tpu_custom_call" | custom-call | flops 39813120 | bytes 7962624 | tf_op jit(solution)/shard_map/pallas_call | solution.py:172
  62.2 2.5 %multiply_reduce_fusion = f32[1024]{0:T(1024)S(1)} fusion(bf16[16,81,1024]{2,1,0:T(8,128)(2,1)} %shard_map.131), kind=kLoop, calls=%fused_computation.2 | loop fusion | flops 3980288 | bytes 2658304 | tf_op jit(solution)/shard_map/reduce_sum | solution.py:239
  64.7 4.1 %reshape.157 = f32[1296,1024]{1,0:T(8,128)} reshape(bf16[16,81,1024]{2,1,0:T(8,128)(2,1)} %shard_map.131) | data formatting | bytes 7962624 | tf_op jit(solution)/shard_map/reshape | solution.py:231
  68.9 0.7 dynamic-slice_bitcast_fusion
  69.7 11.4 %multiply_reduce_fusion.3 = (f32[1024]{0:T(1024)S(1)}, f32[1296,1024]{1,0:T(8,128)S(1)}) fusion(f32[1024]{0:T(1024)S(1)} %get-tuple-element.13, f32[1296,1024]{1,0:T(8,128)} %reshape.157, f32[1024]{0:T(1024)S(1)} %get-tuple-element.12, bf16[1296,1296]{1,0:T(8,128)(2,1)} %param.16, f32[1024]{0:T(1024)S(1)} %bitcast.104, f32[1296]{0:T(1024)S(1)} %get-tuple-element.21, ...), kind=kOutput, calls=%fused_computation.33 | convolution fusion | flops 3462413312 | bytes 14020288 | tf_op jit(solution)/shard_map/dot_general | solution.py:241
  81.1 6.6 %multiply_reduce_fusion.2 = (f32[1024]{0:T(1024)S(1)}, f32[1296,1024]{1,0:T(8,128)S(1)}) fusion(f32[1024]{0:T(1024)S(1)} %get-tuple-element.9, f32[1296,1024]{1,0:T(8,128)S(1)} %get-tuple-element.15, f32[1024]{0:T(1024)S(1)} %get-tuple-element.8, bf16[1296,1296]{1,0:T(8,128)(2,1)S(1)} %copy-done.6, f32[1024]{0:T(1024)S(1)} %bitcast.105, ...), kind=kOutput, calls=%fused_computation.32 | convolution fusion | flops 3462413312 | bytes 14020288 | tf_op jit(solution)/shard_map/dot_general | solution.py:241
  87.8 8.1 %multiply_reduce_fusion.1 = (f32[1024]{0:T(1024)S(1)}, f32[1296,1024]{1,0:T(8,128)}) fusion(f32[1024]{0:T(1024)S(1)} %get-tuple-element.7, f32[1296,1024]{1,0:T(8,128)S(1)} %get-tuple-element.17, f32[1024]{0:T(1024)S(1)} %get-tuple-element.6, bf16[1296,1296]{1,0:T(8,128)(2,1)S(1)} %copy-done.6, f32[1024]{0:T(1024)S(1)} %bitcast.106, ...), kind=kOutput, calls=%fused_computation.31 | convolution fusion | flops 3462413312 | bytes 14020288 | tf_op jit(solution)/shard_map/dot_general | solution.py:241
  96.5 0.4 fusion.31
  96.9 1.2 gather_fusion.1
  98.2 11.1 %fusion.5 = f32[1296,1024]{1,0:T(8,128)S(1)} fusion(f32[1296,1024]{1,0:T(8,128)} %get-tuple-element.19, bf16[1296,1296]{1,0:T(8,128)(2,1)} %param.16, f32[1024]{0:T(1024)S(1)} %get-tuple-element.5, f32[1024]{0:T(1024)S(1)} %get-tuple-element.4, f32[1024]{0:T(1024)S(1)} %bitcast.107, f32[1296]{0:T(1024)S(1)} %get-tuple-element.21, f32[1024]{0:T(1024)S(1)} %bitcast.103, ...), kind=kOutput, calls=%fused_computation.9 | convolution fusion | flops 3459760128 | bytes 14016192 | tf_op jit(solution)/shard_map/dot_general | solution.py:241
  109.3 2.3 %copy-done.1 = f32[1296,1024]{1,0:T(8,128)} copy-done((f32[1296,1024]{1,0:T(8,128)}, f32[1296,1024]{1,0:T(8,128)S(1)}, u32[]{:S(2)}) %copy-start.1) | copy-done | bytes 5308440
  111.6 4.4 %fusion.28 = bf16[256,1296]{0,1:T(8,128)(2,1)S(1)} fusion(f32[256,1024]{1,0:T(8,128)S(1)} %fusion.31, f32[1296,1024]{1,0:T(8,128)S(1)} %fusion.5, f32[256]{0:T(256)S(1)} %bitcast.114), kind=kOutput, calls=%fused_computation.40 | convolution fusion | flops 4077527040 | bytes 7021568 | tf_op jit(solution)/shard_map/dot_general | solution.py:265
  116.0 0.3 copy.15
  116.5 0.3 concatenate.12
  116.8 1.0 pad_maximum_fusion
  117.8 9.0 %all-to-all-start = ((bf16[16,16,1297]{2,1,0:T(8,128)(2,1)}), bf16[16,16,1297]{2,1,0:T(8,128)(2,1)S(1)}, u32[]{:S(2)}, u32[]{:S(2)}) async-start(bf16[16,16,1297]{2,1,0:T(8,128)(2,1)} %pad_maximum_fusion), calls=%async_computation | async-start | bytes 1441792 | tf_op jit(solution)/shard_map/all_to_all | solution.py:271
  126.8 7.6 %reshape.158 = f32[1296,4,256]{2,1,0:T(4,128)} reshape(f32[1296,1024]{1,0:T(8,128)} %copy-done.1) | data formatting | bytes 10616832 | tf_op jit(solution)/shard_map/reshape | solution.py:280
  134.5 13.7 %all-to-all-done = bf16[16,16,1297]{2,1,0:T(8,128)(2,1)S(1)} async-done(((bf16[16,16,1297]{2,1,0:T(8,128)(2,1)}), bf16[16,16,1297]{2,1,0:T(8,128)(2,1)S(1)}, u32[]{:S(2)}, u32[]{:S(2)}) %all-to-all-start) | async-done | bytes 664096 | tf_op jit(solution)/shard_map/all_to_all | solution.py:271
  148.3 1.3 fusion.29
  (40 shorter events, 1.2 us)
Async XLA Ops:
  0.6 96.2 %copy-start = (f32[64]{0:T(128)S(1)}, f32[64]{0:T(128)}, u32[]{:S(2)}) copy-start(f32[64]{0:T(128)} %param.23) | copy-start | bytes 772
  62.2 7.4 %copy-start.2 = (f32[4,256]{1,0:T(4,128)S(1)}, f32[4,256]{1,0:T(4,128)}, u32[]{:S(2)}) copy-start(f32[4,256]{1,0:T(4,128)} %param.18) | copy-start | bytes 12292
  62.2 7.5 %copy-start.3 = (f32[4,256]{1,0:T(4,128)S(1)}, f32[4,256]{1,0:T(4,128)}, u32[]{:S(2)}) copy-start(f32[4,256]{1,0:T(4,128)} %param.17) | copy-start | bytes 12292
  69.7 11.4 %copy-start.6 = (bf16[1296,1296]{1,0:T(8,128)(2,1)S(1)}, bf16[1296,1296]{1,0:T(8,128)(2,1)}, u32[]{:S(2)}) copy-start(bf16[1296,1296]{1,0:T(8,128)(2,1)} %param.16) | copy-start | bytes 10077700
  87.8 8.2 %copy-start.4 = (s32[128,1]{0,1:T(1,128)S(1)}, s32[128,1]{0,1:T(1,128)}, u32[]{:S(2)}) copy-start(s32[128,1]{0,1:T(1,128)} %param.19) | copy-start | bytes 1540
  87.8 8.6 %copy-start.7 = (s32[128]{0:T(128)S(1)}, s32[128]{0:T(128)}, u32[]{:S(2)}) copy-start(s32[128]{0:T(128)} %param.22) | copy-start | bytes 1540
  87.8 8.7 %copy-start.5 = (s32[128]{0:T(128)S(1)}, s32[128]{0:T(128)}, u32[]{:S(2)}) copy-start(s32[128]{0:T(128)} %param.21) | copy-start | bytes 1540
  109.3 2.3 %copy-start.1 = (f32[1296,1024]{1,0:T(8,128)}, f32[1296,1024]{1,0:T(8,128)S(1)}, u32[]{:S(2)}) copy-start(f32[1296,1024]{1,0:T(8,128)S(1)} %fusion.5) | copy-start | bytes 15925252
  109.3 7.0 %copy-start.8 = (s32[128]{0:T(128)S(1)}, s32[128]{0:T(128)}, u32[]{:S(2)}) copy-start(s32[128]{0:T(128)} %param.20) | copy-start | bytes 1540
  117.8 30.4 %all-to-all-start = ((bf16[16,16,1297]{2,1,0:T(8,128)(2,1)}), bf16[16,16,1297]{2,1,0:T(8,128)(2,1)S(1)}, u32[]{:S(2)}, u32[]{:S(2)}) async-start(bf16[16,16,1297]{2,1,0:T(8,128)(2,1)} %pad_maximum_fusion), calls=%async_computation | async-start | bytes 1441792 | tf_op jit(solution)/shard_map/all_to_all | solution.py:271

commit v3 on v2

--- a/solution.py
+++ b/solution.py
@@ -196,6 +196,54 @@
     )(rate_x, rate_y, spectrum, factor, sea_float)
 
 
+def source_kernel(state_ref, inter_ref, colv_ref, rowv_ref, out_ref, gain, current):
+    cols = colv_ref[...]
+    rowv = rowv_ref[...]
+    speed, cos_w, sin_w, sea = rowv[0:1], rowv[1:2], rowv[2:3], rowv[3:4]
+    scale, cos_h, sin_h = cols[:, 0:1], cols[:, 1:2], cols[:, 2:3]
+    gain[...] = scale * speed * jnp.maximum(cos_h * cos_w + sin_h * sin_w, 0.0)
+    current[...] = state_ref[...]
+    comps = current.shape[0]
+    for step_number in range(SOURCE_STEPS):
+        state = current[...]
+        spread = jnp.sqrt(jnp.sum(state * state, axis=0, keepdims=True) / comps + EPSILON)
+        transfer = jnp.dot(inter_ref[...], state.astype(jnp.bfloat16), preferred_element_type=jnp.float32)
+        current[...] = (
+            sea
+            * (state + RATE * (gain[...] * state + state * transfer / spread))
+            / (1.0 + RATE * WHITECAP * spread)
+        )
+    out_ref[...] = current[...]
+
+
+def source_steps(state, interaction, colv, rowv):
+    comps, cells = state.shape
+    block = 256
+    return pl.pallas_call(
+        source_kernel,
+        grid=(cells // block,),
+        in_specs=[
+            pl.BlockSpec((comps, block), lambda j: (0, j)),
+            pl.BlockSpec((comps, comps), lambda j: (0, 0)),
+            pl.BlockSpec((comps, 128), lambda j: (0, 0)),
+            pl.BlockSpec((8, block), lambda j: (0, j)),
+        ],
+        out_specs=pl.BlockSpec((comps, block), lambda j: (0, j)),
+        out_shape=jax.ShapeDtypeStruct((comps, cells), jnp.float32),
+        scratch_shapes=[
+            pltpu.VMEM((comps, block), jnp.float32),
+            pltpu.VMEM((comps, block), jnp.float32),
+        ],
+        compiler_params=pltpu.CompilerParams(
+            dimension_semantics=("arbitrary",), vmem_limit_bytes=56 * 1024 * 1024
+        ),
+        cost_estimate=pl.CostEstimate(
+            flops=SOURCE_STEPS * 2 * comps * comps * cells, bytes_accessed=8 * comps * cells,
+            transcendentals=SOURCE_STEPS * cells,
+        ),
+    )(state, interaction, colv, rowv)
+
+
 def local(
     spectrum,
     group_speed,
@@ -232,21 +280,16 @@
     sea_rows = lax.dynamic_slice_in_dim(sea_float, lax.axis_index("spec") * row_count, row_count, 0)
     sea_cells = sea_rows.reshape(-1)
     all_heading, all_freq = headings(0, comp_total, freq_count, dir_count)
-    wind_gain = wind_term(
-        all_heading, all_freq, freq_count, wind_speed.reshape(-1), wind_dir.reshape(-1)
-    )
-    for step_number in range(SOURCE_STEPS):
-        spread = jnp.sqrt(jnp.mean(spectra_now * spectra_now, axis=0) + EPSILON)
-        rounded = spectra_now.astype(jnp.bfloat16)
-        transfer = jnp.dot(interaction, rounded, preferred_element_type=jnp.float32)
-        spectra_now = (
-            sea_cells[None]
-            * (
-                spectra_now
-                + RATE * (wind_gain * spectra_now + spectra_now * transfer / spread[None])
-            )
-            / (1.0 + RATE * WHITECAP * spread[None])
-        )
+    scale_freq = (all_freq + 1).astype(jnp.float32) / freq_count
+    colv = jnp.zeros((comp_total, 128), jnp.float32)
+    colv = colv.at[:, 0].set(WIND_GAIN * scale_freq).at[:, 1].set(jnp.cos(all_heading)).at[:, 2].set(jnp.sin(all_heading))
+    direction = wind_dir.reshape(-1)
+    rowv = jnp.zeros((8, cell_count), jnp.float32)
+    rowv = (
+        rowv.at[0].set(wind_speed.reshape(-1)).at[1].set(jnp.cos(direction))
+        .at[2].set(jnp.sin(direction)).at[3].set(sea_cells)
+    )
+    spectra_now = source_steps(spectra_now, interaction, colv, rowv)
 
     slots = grid_count * CAP
     owners = nest_owner[:, 0]

time: 150 us -> 166 us (1.11)
  Pallas kernels: 55.7 us -> 92.6 us
  matrix products: 43.5 us -> 8.82 us
  local copies, waits for them, and re-layouts: 18.5 us -> 26.1 us
  other arithmetic: 8.24 us -> 14.6 us
    dot_general x4 -> x0, matrix products: 37.2 us -> none  [local(): transfer = jnp.dot(interaction, rounded, preferred_element_type=jnp.float32)]
    pallas_call x0 -> x1, Pallas kernels: none -> 36.9 us  [source_steps(): pl.pallas_call(source_kernel, grid=(cells // block,), in_specs=[pl.BlockS...]
    another operation x1 -> x7, other arithmetic: 0.01 us -> 8.99 us
    scatter x0 -> x7, local copies, waits for them, and re-layouts: none -> 8.87 us  [the longest x3 8.33 us: local(): colv.at[:, 0].set(WIND_GAIN * scale_freq).at[:, 1].set(jnp.cos(all_heading))]
    dot_general x1, matrix products: 4.38 us -> 6.88 us  [local(): lax.dot_general(slot_cell, spectra_now, (((1,), (1,)), ((), ())), precisi...]
    reduce_sum x1 -> x0, other arithmetic: 2.48 us -> none  [local(): spread = jnp.sqrt(jnp.mean(spectra_now * spectra_now, axis=0) + EPSILON)]
where the time goes in v3:
time: 166 us
  Pallas kernels  92.6 us (56%)
  local copies, waits for them, and re-layouts  26.1 us (16%)
  other arithmetic  14.6 us (9%)
  waiting for transfers between devices  13.7 us (8%)
  starting transfers between devices  9.03 us (5%)
  matrix products  8.82 us (5%)
    pallas_call x1, Pallas kernels, propagate(): pl.pallas_call(propagate_kernel, in_specs=[smem, smem, vmem, vmem, vmem],...  55.7 us
    pallas_call x1, Pallas kernels, source_steps(): pl.pallas_call(source_kernel, grid=(cells // block,), in_specs=[pl.BlockS...  36.9 us
    all_to_all x1, waiting for transfers between devices, local(): lax.all_to_all(send, 'grid', split_axis=0, concat_axis=0, tiled=True)  13.7 us
    all_to_all x1, starting transfers between devices, local(): lax.all_to_all(send, 'grid', split_axis=0, concat_axis=0, tiled=True)  9.03 us
    another operation x7, other arithmetic  8.99 us
    scatter x3, local copies, waits for them, and re-layouts, local(): colv.at[:, 0].set(WIND_GAIN * scale_freq).at[:, 1].set(jnp.cos(all_heading))  8.33 us
    reshape x1, local copies, waits for them, and re-layouts, local(): return (spectra_now.reshape(comp_total, row_count, lon_count), nest_spectra)  7.64 us
    dot_general x1, matrix products, local(): lax.dot_general(slot_cell, spectra_now, (((1,), (1,)), ((), ())), precisi...  6.88 us
  transfers between devices with their start and end apart: 1, of which 1 were waited for; matrix products, arithmetic and copies ran while one was open for 5% of the time, Pallas kernels for 0%

profile of v3, /device:TPU:1, one launch (start us, length us, event | category | flops | bytes accessed | tf_op | source)
XLA Modules:
  0.0 165.7 jit_solution(11396775179725449461)
XLA Ops:
  0.6 0.6 compare_reduce_fusion.2
  1.3 0.7 compare_reduce_fusion.1
  1.9 0.6 compare_reduce_fusion
  2.6 1.6 gather_fusion
  4.2 0.6 sine_multiply_fusion
  5.3 1.5 convert_element_type.40.sea_ref
  6.8 1.5 convert_multiply_fusion.factor_ref
  8.3 55.7 %shard_map.131 = bf16[16,81,1024]{2,1,0:T(8,128)(2,1)} custom-call(f32[81]{0:T(128)} %cosine_multiply_fusion.rx_ref, f32[81]{0:T(128)} %get-tuple-element.86.ry_ref, f32[81,64,256]{2,1,0:T(8,128)} %spec_ref.1, f32[64,256]{1,0:T(8,128)} %convert_multiply_fusion.factor_ref, f32[64,256]{1,0:T(8,128)} %convert_element_type.40.sea_ref), custom_call_target="tpu_custom_call" | custom-call | flops 39813120 | bytes 7962624 | tf_op jit(solution)/shard_map/pallas_call | solution.py:172
  64.1 4.1 %reshape.312.state_ref = f32[1296,1024]{1,0:T(8,128)} reshape(bf16[16,81,1024]{2,1,0:T(8,128)(2,1)} %shard_map.131) | data formatting | bytes 7962624 | tf_op jit(solution)/shard_map/reshape | solution.py:279
  68.2 0.7 dynamic-slice_bitcast_fusion
  69.0 0.9 fusion.9
  70.0 2.9 %cosine_select_fusion = f32[1296,1]{1,0:T(8,128)S(1)} fusion(pred[]{:T(512)} %compare_reduce_fusion.1), kind=kLoop, calls=%fused_computation.20 | loop fusion | flops 15552 | bytes 5185 | tf_op jit(solution)/shard_map/select.26
  73.8 1.2 gather_fusion.1
  75.3 4.1 %scatter.25 = f32[1296,128]{1,0:T(8,128)S(1)} dynamic-update-slice(f32[1296,128]{1,0:T(8,128)S(1)} %scatter.24, f32[1296,1]{1,0:T(8,128)S(1)} %cosine_select_fusion, s32[]{:T(128)} %constant.265.clone.1, s32[]{:T(128)} %constant.268.clone.1) | dynamic-update-slice | bytes 10372 | tf_op jit(solution)/shard_map/scatter | solution.py:285
  79.5 3.3 %slice_select_fusion = f32[1296,1]{1,0:T(8,128)S(1)} fusion(f32[1296,128]{1,0:T(8,128)S(1)} %scatter.25, pred[]{:T(512)} %compare_reduce_fusion), kind=kLoop, calls=%fused_computation.19 | loop fusion | flops 15552 | bytes 10369 | tf_op jit(solution)/shard_map/select.9
  82.8 4.1 %scatter.26.colv_ref = f32[1296,128]{1,0:T(8,128)S(1)} dynamic-update-slice(f32[1296,128]{1,0:T(8,128)S(1)} %scatter.25, f32[1296,1]{1,0:T(8,128)S(1)} %slice_select_fusion, s32[]{:T(128)} %constant.265.clone.1, s32[]{:T(128)} %constant.276.clone.1) | dynamic-update-slice | bytes 10372 | tf_op jit(solution)/shard_map/scatter | solution.py:285
  87.8 0.6 copy-done.2
  88.4 36.9 %shard_map.132 = f32[1296,1024]{1,0:T(8,128)} custom-call(f32[1296,1024]{1,0:T(8,128)} %reshape.312.state_ref, bf16[1296,1296]{1,0:T(8,128)(2,1)} %inter_ref.1, f32[1296,128]{1,0:T(8,128)} %copy-done.1, f32[8,1024]{1,0:T(8,128)} %copy-done.2), custom_call_target="tpu_custom_call" | custom-call | flops 13759414272 | bytes 10616832 | tf_op jit(solution)/shard_map/pallas_call | solution.py:222
  125.2 6.9 %fusion = bf16[256,1296]{0,1:T(8,128)(2,1)S(1)} fusion(f32[256,1024]{1,0:T(8,128)S(1)} %fusion.15, f32[1296,1024]{1,0:T(8,128)} %shard_map.132, f32[256]{0:T(256)S(1)} %bitcast.46), kind=kOutput, calls=%fused_computation.3 | convolution fusion | flops 4077527040 | bytes 7021568 | tf_op jit(solution)/shard_map/dot_general | solution.py:308
  132.9 1.0 pad_maximum_fusion
  133.9 9.0 %all-to-all-start = ((bf16[16,16,1297]{2,1,0:T(8,128)(2,1)}), bf16[16,16,1297]{2,1,0:T(8,128)(2,1)S(1)}, u32[]{:S(2)}, u32[]{:S(2)}) async-start(bf16[16,16,1297]{2,1,0:T(8,128)(2,1)} %pad_maximum_fusion), calls=%async_computation | async-start | bytes 1441792 | tf_op jit(solution)/shard_map/all_to_all | solution.py:314
  142.9 7.6 %reshape.309 = f32[1296,4,256]{2,1,0:T(4,128)} reshape(f32[1296,1024]{1,0:T(8,128)} %shard_map.132) | data formatting | bytes 10616832 | tf_op jit(solution)/shard_map/reshape | solution.py:323
  150.6 13.7 %all-to-all-done = bf16[16,16,1297]{2,1,0:T(8,128)(2,1)S(1)} async-done(((bf16[16,16,1297]{2,1,0:T(8,128)(2,1)}), bf16[16,16,1297]{2,1,0:T(8,128)(2,1)S(1)}, u32[]{:S(2)}, u32[]{:S(2)}) %all-to-all-start) | async-done | bytes 664096 | tf_op jit(solution)/shard_map/all_to_all | solution.py:314
  164.5 1.3 fusion.1
  (43 shorter events, 3.7 us)
Async XLA Ops:
  0.6 73.2 %copy-start = (f32[64]{0:T(128)S(1)}, f32[64]{0:T(128)}, u32[]{:S(2)}) copy-start(f32[64]{0:T(128)} %param.37) | copy-start | bytes 772
  64.0 4.9 %copy-start.3 = (f32[4,256]{1,0:T(4,128)S(1)}, f32[4,256]{1,0:T(4,128)}, u32[]{:S(2)}) copy-start(f32[4,256]{1,0:T(4,128)} %param.32) | copy-start | bytes 12292
  64.0 4.9 %copy-start.4 = (f32[4,256]{1,0:T(4,128)S(1)}, f32[4,256]{1,0:T(4,128)}, u32[]{:S(2)}) copy-start(f32[4,256]{1,0:T(4,128)} %param.31) | copy-start | bytes 12292
  64.1 8.8 %copy-start.5 = (s32[128,1]{0,1:T(1,128)S(1)}, s32[128,1]{0,1:T(1,128)}, u32[]{:S(2)}) copy-start(s32[128,1]{0,1:T(1,128)} %param.33) | copy-start | bytes 1540
  64.1 9.3 %copy-start.7 = (s32[128]{0:T(128)S(1)}, s32[128]{0:T(128)}, u32[]{:S(2)}) copy-start(s32[128]{0:T(128)} %param.36) | copy-start | bytes 1540
  64.1 9.3 %copy-start.6 = (s32[128]{0:T(128)S(1)}, s32[128]{0:T(128)}, u32[]{:S(2)}) copy-start(s32[128]{0:T(128)} %param.35) | copy-start | bytes 1540
  86.9 0.8 copy-start.1
  87.8 0.6 copy-start.2
  125.2 7.2 %copy-start.8 = (s32[128]{0:T(128)S(1)}, s32[128]{0:T(128)}, u32[]{:S(2)}) copy-start(s32[128]{0:T(128)} %param.34) | copy-start | bytes 1540
  133.9 30.4 %all-to-all-start = ((bf16[16,16,1297]{2,1,0:T(8,128)(2,1)}), bf16[16,16,1297]{2,1,0:T(8,128)(2,1)S(1)}, u32[]{:S(2)}, u32[]{:S(2)}) async-start(bf16[16,16,1297]{2,1,0:T(8,128)(2,1)} %pad_maximum_fusion), calls=%async_computation | async-start | bytes 1441792 | tf_op jit(solution)/shard_map/all_to_all | solution.py:314

commit v4 on v2

--- a/solution.py
+++ b/solution.py
@@ -62,8 +62,8 @@
     lax.fori_loop(0, spec_count, greet, 0)
     pl.semaphore_wait(barrier, 2 + spec_count - 1)
 
-    factor = factor_ref[...]
-    sea = sea_ref[...]
+    sea = sea_ref[...].astype(jnp.float32)
+    factor = factor_ref[...] * sea
     edge_lane = lax.broadcasted_iota(jnp.int32, (rows, 128), 1)
     factor_first = factor[:, 0:1]
     factor_last = factor[:, lons - 1 : lons]
@@ -132,7 +132,8 @@
     for start, size in blocks:
         lax.fori_loop(start, start + size, one, 0)
 
-        def regroup(d, carry, start=start, size=size):
+        def regroup(t, carry, start=start, size=size):
+            d = lax.rem(spec + t, spec_count)
             for r in range(chunk):
                 i = start * rows + d * chunk + r
                 for half, part in ((0, result_lo), (1, result_hi)):
@@ -225,7 +226,7 @@
     sea_float = sea_mask.astype(jnp.float32)
     factor = depth_factor * sea_float
     lon_count = spectrum.shape[2]
-    received = propagate(spectrum, rate_x, rate_y, factor, sea_float, spec_count)
+    received = propagate(spectrum, rate_x, rate_y, depth_factor, sea_mask, spec_count)
     row_count = spectrum.shape[1] // spec_count
     cell_count = row_count * lon_count
     spectra_now = received.astype(jnp.float32).reshape(comp_total, cell_count)
@@ -263,7 +264,7 @@
         preferred_element_type=jnp.float32,
     ) - 1.0
     gathered = lax.dot_general(
-        slot_cell, spectra_now, (((1,), (1,)), ((), ())), precision=HIGHEST,
+        slot_cell, spectra_now, (((1,), (1,)), ((), ())), precision=lax.Precision.HIGH,
         preferred_element_type=jnp.float32,
     )
     send = jnp.concatenate([gathered * slot_weight[:, None], slot_label[:, None]], axis=1)

time: 150 us -> 142 us (0.947)
  other arithmetic: 8.24 us -> 5.95 us
  matrix products: 43.5 us -> 41.6 us
  Pallas kernels: 55.7 us -> 54 us
    dot_general x1, matrix products: 4.38 us -> 2.4 us  [local(): lax.dot_general(slot_cell, spectra_now, (((1,), (1,)), ((), ())), precisi...]
    pallas_call x1, Pallas kernels: 55.7 us -> 54 us  [propagate(): pl.pallas_call(propagate_kernel, in_specs=[smem, smem, vmem, vmem, vmem],...]
    mul x1 -> x0, other arithmetic: 1.51 us -> none  [local(): factor = depth_factor * sea_float]
    unnamed x24 -> x23, local copies, waits for them, and re-layouts: 3.12 us -> 2.42 us
where the time goes in v4:
time: 142 us
  Pallas kernels  54 us (38%)
  matrix products  41.6 us (29%)
  local copies, waits for them, and re-layouts  17.8 us (13%)
  waiting for transfers between devices  13.7 us (10%)
  starting transfers between devices  8.2 us (6%)
  other arithmetic  5.95 us (4%)
    pallas_call x1, Pallas kernels, propagate(): pl.pallas_call(propagate_kernel, in_specs=[smem, smem, vmem, vmem, vmem],...  54 us
    dot_general x4, matrix products, local(): transfer = jnp.dot(interaction, rounded, preferred_element_type=jnp.float32)  37.2 us
    all_to_all x1, waiting for transfers between devices, local(): lax.all_to_all(send, 'grid', split_axis=0, concat_axis=0, tiled=True)  13.7 us
    all_to_all x1, starting transfers between devices, local(): lax.all_to_all(send, 'grid', split_axis=0, concat_axis=0, tiled=True)  8.2 us
    reshape x1, local copies, waits for them, and re-layouts, local(): return (spectra_now.reshape(comp_total, row_count, lon_count), nest_spectra)  7.64 us
    reshape x1, local copies, waits for them, and re-layouts, local(): spectra_now = received.astype(jnp.float32).reshape(comp_total, cell_count)  4.08 us
  transfers between devices with their start and end apart: 1, of which 1 were waited for; matrix products, arithmetic and copies ran while one was open for 5% of the time, Pallas kernels for 0%

profile of v4, /device:TPU:1, one launch (start us, length us, event | category | flops | bytes accessed | tf_op | source)
XLA Modules:
  0.0 142.0 jit_solution(3189896636341022400)
XLA Ops:
  0.7 1.6 %gather_fusion = f32[81]{0:T(128)S(1)} fusion(f32[36]{0:T(128)} %param.13, s32[1024]{0:T(1024)S(1)} %pad_clamp_fusion.1), kind=kCustom, calls=%fused_computation | custom fusion | bytes 972 | tf_op jit(solution)/shard_map/jit(_take)/gather | solution.py:223
  2.3 0.6 sine_multiply_fusion
  2.9 0.6 cosine_multiply_fusion.rx_ref
  3.4 54.0 %shard_map.131 = bf16[16,81,1024]{2,1,0:T(8,128)(2,1)} custom-call(f32[81]{0:T(128)} %cosine_multiply_fusion.rx_ref, f32[81]{0:T(128)} %get-tuple-element.2.ry_ref, f32[81,64,256]{2,1,0:T(8,128)} %spec_ref.1, f32[64,256]{1,0:T(8,128)} %factor_ref.1, s32[64,256]{1,0:T(8,128)} %sea_ref.1), custom_call_target="tpu_custom_call" | custom-call | flops 39813120 | bytes 7962624 | tf_op jit(solution)/shard_map/pallas_call | solution.py:173
  57.4 2.5 %multiply_reduce_fusion = f32[1024]{0:T(1024)S(1)} fusion(bf16[16,81,1024]{2,1,0:T(8,128)(2,1)} %shard_map.131), kind=kLoop, calls=%fused_computation.2 | loop fusion | flops 3980288 | bytes 2658304 | tf_op jit(solution)/shard_map/reduce_sum | solution.py:240
  59.9 4.1 %reshape.157 = f32[1296,1024]{1,0:T(8,128)} reshape(bf16[16,81,1024]{2,1,0:T(8,128)(2,1)} %shard_map.131) | data formatting | bytes 7962624 | tf_op jit(solution)/shard_map/reshape | solution.py:232
  64.1 0.7 fusion.53
  64.9 11.4 %multiply_reduce_fusion.3 = (f32[1024]{0:T(1024)S(1)}, f32[1296,1024]{1,0:T(8,128)S(1)}) fusion(f32[1024]{0:T(1024)S(1)} %get-tuple-element.13, f32[1296,1024]{1,0:T(8,128)} %reshape.157, f32[1024]{0:T(1024)S(1)} %get-tuple-element.12, bf16[1296,1296]{1,0:T(8,128)(2,1)} %param.16, f32[1024]{0:T(1024)S(1)} %bitcast.104, f32[1296]{0:T(1024)S(1)} %get-tuple-element.21, ...), kind=kOutput, calls=%fused_computation.33 | convolution fusion | flops 3462413312 | bytes 14020288 | tf_op jit(solution)/shard_map/dot_general | solution.py:242
  76.3 6.6 %multiply_reduce_fusion.2 = (f32[1024]{0:T(1024)S(1)}, f32[1296,1024]{1,0:T(8,128)S(1)}) fusion(f32[1024]{0:T(1024)S(1)} %get-tuple-element.9, f32[1296,1024]{1,0:T(8,128)S(1)} %get-tuple-element.15, f32[1024]{0:T(1024)S(1)} %get-tuple-element.8, bf16[1296,1296]{1,0:T(8,128)(2,1)S(1)} %copy-done.6, f32[1024]{0:T(1024)S(1)} %bitcast.105, ...), kind=kOutput, calls=%fused_computation.32 | convolution fusion | flops 3462413312 | bytes 14020288 | tf_op jit(solution)/shard_map/dot_general | solution.py:242
  83.0 8.1 %multiply_reduce_fusion.1 = (f32[1024]{0:T(1024)S(1)}, f32[1296,1024]{1,0:T(8,128)}) fusion(f32[1024]{0:T(1024)S(1)} %get-tuple-element.7, f32[1296,1024]{1,0:T(8,128)S(1)} %get-tuple-element.17, f32[1024]{0:T(1024)S(1)} %get-tuple-element.6, bf16[1296,1296]{1,0:T(8,128)(2,1)S(1)} %copy-done.6, f32[1024]{0:T(1024)S(1)} %bitcast.106, ...), kind=kOutput, calls=%fused_computation.31 | convolution fusion | flops 3462413312 | bytes 14020288 | tf_op jit(solution)/shard_map/dot_general | solution.py:242
  91.3 0.2 reduce_window_sum.11
  91.7 0.4 fusion.31
  92.1 1.2 gather_fusion.1
  93.5 11.1 %fusion.5 = f32[1296,1024]{1,0:T(8,128)S(1)} fusion(f32[1296,1024]{1,0:T(8,128)} %get-tuple-element.19, bf16[1296,1296]{1,0:T(8,128)(2,1)} %param.16, f32[1024]{0:T(1024)S(1)} %get-tuple-element.5, f32[1024]{0:T(1024)S(1)} %get-tuple-element.4, f32[1024]{0:T(1024)S(1)} %bitcast.107, f32[1296]{0:T(1024)S(1)} %get-tuple-element.21, f32[1024]{0:T(1024)S(1)} %bitcast.103, ...), kind=kOutput, calls=%fused_computation.9 | convolution fusion | flops 3459760128 | bytes 14016192 | tf_op jit(solution)/shard_map/dot_general | solution.py:242
  104.6 2.3 %copy-done.1 = f32[1296,1024]{1,0:T(8,128)} copy-done((f32[1296,1024]{1,0:T(8,128)}, f32[1296,1024]{1,0:T(8,128)S(1)}, u32[]{:S(2)}) %copy-start.1) | copy-done | bytes 5308440
  106.9 2.4 %fusion.28 = bf16[256,1296]{0,1:T(8,128)(2,1)S(1)} fusion(f32[256,1024]{1,0:T(8,128)S(1)} %fusion.31, f32[1296,1024]{1,0:T(8,128)S(1)} %fusion.5, f32[256]{0:T(256)S(1)} %bitcast.114), kind=kOutput, calls=%fused_computation.40 | convolution fusion | flops 2039095296 | bytes 7021568 | tf_op jit(solution)/shard_map/dot_general | solution.py:266
  109.3 0.3 copy.15
  109.8 0.3 concatenate.12
  110.1 1.0 pad_maximum_fusion
  111.1 8.2 %all-to-all-start = ((bf16[16,16,1297]{2,1,0:T(8,128)(2,1)}), bf16[16,16,1297]{2,1,0:T(8,128)(2,1)S(1)}, u32[]{:S(2)}, u32[]{:S(2)}) async-start(bf16[16,16,1297]{2,1,0:T(8,128)(2,1)} %pad_maximum_fusion), calls=%async_computation | async-start | bytes 1441792 | tf_op jit(solution)/shard_map/all_to_all | solution.py:272
  119.3 7.6 %reshape.158 = f32[1296,4,256]{2,1,0:T(4,128)} reshape(f32[1296,1024]{1,0:T(8,128)} %copy-done.1) | data formatting | bytes 10616832 | tf_op jit(solution)/shard_map/reshape | solution.py:281
  126.9 13.7 %all-to-all-done = bf16[16,16,1297]{2,1,0:T(8,128)(2,1)S(1)} async-done(((bf16[16,16,1297]{2,1,0:T(8,128)(2,1)}), bf16[16,16,1297]{2,1,0:T(8,128)(2,1)S(1)}, u32[]{:S(2)}, u32[]{:S(2)}) %all-to-all-start) | async-done | bytes 664096 | tf_op jit(solution)/shard_map/all_to_all | solution.py:272
  140.6 0.2 slice_reduce_fusion
  140.8 1.3 fusion.29
  (38 shorter events, 0.8 us)
Async XLA Ops:
  0.6 91.5 %copy-start = (f32[64]{0:T(128)S(1)}, f32[64]{0:T(128)}, u32[]{:S(2)}) copy-start(f32[64]{0:T(128)} %param.23) | copy-start | bytes 772
  57.4 7.4 %copy-start.2 = (f32[4,256]{1,0:T(4,128)S(1)}, f32[4,256]{1,0:T(4,128)}, u32[]{:S(2)}) copy-start(f32[4,256]{1,0:T(4,128)} %param.18) | copy-start | bytes 12292
  57.4 7.5 %copy-start.3 = (f32[4,256]{1,0:T(4,128)S(1)}, f32[4,256]{1,0:T(4,128)}, u32[]{:S(2)}) copy-start(f32[4,256]{1,0:T(4,128)} %param.17) | copy-start | bytes 12292
  64.9 11.4 %copy-start.6 = (bf16[1296,1296]{1,0:T(8,128)(2,1)S(1)}, bf16[1296,1296]{1,0:T(8,128)(2,1)}, u32[]{:S(2)}) copy-start(bf16[1296,1296]{1,0:T(8,128)(2,1)} %param.16) | copy-start | bytes 10077700
  83.0 8.2 %copy-start.4 = (s32[128,1]{0,1:T(1,128)S(1)}, s32[128,1]{0,1:T(1,128)}, u32[]{:S(2)}) copy-start(s32[128,1]{0,1:T(1,128)} %param.19) | copy-start | bytes 1540
  83.0 8.6 %copy-start.7 = (s32[128]{0:T(128)S(1)}, s32[128]{0:T(128)}, u32[]{:S(2)}) copy-start(s32[128]{0:T(128)} %param.22) | copy-start | bytes 1540
  83.0 8.7 %copy-start.5 = (s32[128]{0:T(128)S(1)}, s32[128]{0:T(128)}, u32[]{:S(2)}) copy-start(s32[128]{0:T(128)} %param.21) | copy-start | bytes 1540
  104.6 2.3 %copy-start.1 = (f32[1296,1024]{1,0:T(8,128)}, f32[1296,1024]{1,0:T(8,128)S(1)}, u32[]{:S(2)}) copy-start(f32[1296,1024]{1,0:T(8,128)S(1)} %fusion.5) | copy-start | bytes 15925252
  104.6 5.1 %copy-start.8 = (s32[128]{0:T(128)S(1)}, s32[128]{0:T(128)}, u32[]{:S(2)}) copy-start(s32[128]{0:T(128)} %param.20) | copy-start | bytes 1540
  111.1 29.5 %all-to-all-start = ((bf16[16,16,1297]{2,1,0:T(8,128)(2,1)}), bf16[16,16,1297]{2,1,0:T(8,128)(2,1)S(1)}, u32[]{:S(2)}, u32[]{:S(2)}) async-start(bf16[16,16,1297]{2,1,0:T(8,128)(2,1)} %pad_maximum_fusion), calls=%async_computation | async-start | bytes 1441792 | tf_op jit(solution)/shard_map/all_to_all | solution.py:272

commit v5 on v4

--- a/solution.py
+++ b/solution.py
@@ -39,7 +39,7 @@
 def propagate_kernel(
     rx_ref, ry_ref, spec_ref, factor_ref, sea_ref, out_ref,
     send_first, send_last, recv_west, recv_east, send_sem, recv_sem,
-    result_lo, result_hi, send_buf, a2a_send, a2a_recv,
+    result_lo, result_hi, send_buf, a2a_send, a2a_recv, recv_buf,
 ):
     comps, rows, lons = spec_ref.shape
     spec_count = lax.axis_size("spec")
@@ -120,7 +120,7 @@
 
     def copy_to(d, slot, start, size):
         return pltpu.make_async_remote_copy(
-            src_ref=send_buf.at[d, pl.ds(start, size)], dst_ref=out_ref.at[slot, pl.ds(start, size)],
+            src_ref=send_buf.at[d, pl.ds(start, size)], dst_ref=recv_buf.at[slot, pl.ds(start, size)],
             send_sem=a2a_send.at[d], recv_sem=a2a_recv.at[slot], device_id=(d, me),
             device_id_type=pl.DeviceIdType.MESH,
         )
@@ -148,7 +148,7 @@
 
             @pl.when(d == spec)
             def _():
-                out_ref[d, pl.ds(start, size), :] = send_buf[d, pl.ds(start, size), :]
+                recv_buf[d, pl.ds(start, size), :] = send_buf[d, pl.ds(start, size), :]
 
             return carry
 
@@ -163,6 +163,8 @@
         return carry
 
     lax.fori_loop(0, spec_count, finish, 0)
+    for s in range(spec_count):
+        out_ref[s * comps : (s + 1) * comps, :] = recv_buf[s].astype(out_ref.dtype)
 
 
 def propagate(spectrum, rate_x, rate_y, factor, sea_float, spec_count):
@@ -174,7 +176,7 @@
         propagate_kernel,
         in_specs=[smem, smem, vmem, vmem, vmem],
         out_specs=vmem,
-        out_shape=jax.ShapeDtypeStruct((spec_count, comps, chunk * lons), jnp.bfloat16),
+        out_shape=jax.ShapeDtypeStruct((spec_count * comps, chunk * lons), jnp.float32),
         scratch_shapes=[
             pltpu.VMEM((rows, 128), jnp.float32),
             pltpu.VMEM((rows, 128), jnp.float32),
@@ -187,6 +189,7 @@
             pltpu.VMEM((spec_count, comps, chunk * lons), jnp.bfloat16),
             pltpu.SemaphoreType.DMA((spec_count,)),
             pltpu.SemaphoreType.DMA((spec_count,)),
+            pltpu.VMEM((spec_count, comps, chunk * lons), jnp.bfloat16),
         ],
         compiler_params=pltpu.CompilerParams(
             collective_id=0, has_side_effects=True, vmem_limit_bytes=56 * 1024 * 1024
@@ -229,7 +232,7 @@
     received = propagate(spectrum, rate_x, rate_y, depth_factor, sea_mask, spec_count)
     row_count = spectrum.shape[1] // spec_count
     cell_count = row_count * lon_count
-    spectra_now = received.astype(jnp.float32).reshape(comp_total, cell_count)
+    spectra_now = received
     sea_rows = lax.dynamic_slice_in_dim(sea_float, lax.axis_index("spec") * row_count, row_count, 0)
     sea_cells = sea_rows.reshape(-1)
     all_heading, all_freq = headings(0, comp_total, freq_count, dir_count)

time: 142 us -> 140 us (0.986)
  local copies, waits for them, and re-layouts: 17.8 us -> 13.7 us
    reshape x1 -> x0, local copies, waits for them, and re-layouts: 4.08 us -> none  [local(): spectra_now = received.astype(jnp.float32).reshape(comp_total, cell_count)]
where the time goes in v5:
time: 140 us
  Pallas kernels  55.2 us (39%)
  matrix products  41.4 us (30%)
  local copies, waits for them, and re-layouts  13.7 us (10%)
  waiting for transfers between devices  13.7 us (10%)
  starting transfers between devices  8.2 us (6%)
  other arithmetic  6.42 us (5%)
    pallas_call x1, Pallas kernels, propagate(): pl.pallas_call(propagate_kernel, in_specs=[smem, smem, vmem, vmem, vmem],...  55.2 us
    dot_general x4, matrix products, local(): transfer = jnp.dot(interaction, rounded, preferred_element_type=jnp.float32)  37.1 us
    all_to_all x1, waiting for transfers between devices, local(): lax.all_to_all(send, 'grid', split_axis=0, concat_axis=0, tiled=True)  13.7 us
    all_to_all x1, starting transfers between devices, local(): lax.all_to_all(send, 'grid', split_axis=0, concat_axis=0, tiled=True)  8.2 us
    reshape x1, local copies, waits for them, and re-layouts, local(): return (spectra_now.reshape(comp_total, row_count, lon_count), nest_spectra)  7.64 us
    reduce_sum x1, other arithmetic, local(): spread = jnp.sqrt(jnp.mean(spectra_now * spectra_now, axis=0) + EPSILON)  2.94 us
  transfers between devices with their start and end apart: 1, of which 1 were waited for; matrix products, arithmetic and copies ran while one was open for 5% of the time, Pallas kernels for 0%

profile of v5, /device:TPU:1, one launch (start us, length us, event | category | flops | bytes accessed | tf_op | source)
XLA Modules:
  0.0 139.5 jit_solution(549648393140386693)
XLA Ops:
  0.8 1.6 %gather_fusion = f32[81]{0:T(128)S(1)} fusion(f32[36]{0:T(128)} %param.13, s32[1024]{0:T(1024)S(1)} %pad_clamp_fusion.1), kind=kCustom, calls=%fused_computation | custom fusion | bytes 972 | tf_op jit(solution)/shard_map/jit(_take)/gather | solution.py:226
  2.4 0.6 sine_multiply_fusion
  3.0 0.6 cosine_multiply_fusion.rx_ref
  3.5 55.2 %shard_map.131 = f32[1296,1024]{1,0:T(8,128)} custom-call(f32[81]{0:T(128)} %cosine_multiply_fusion.rx_ref, f32[81]{0:T(128)} %get-tuple-element.2.ry_ref, f32[81,64,256]{2,1,0:T(8,128)} %spec_ref.1, f32[64,256]{1,0:T(8,128)} %factor_ref.1, s32[64,256]{1,0:T(8,128)} %sea_ref.1), custom_call_target="tpu_custom_call" | custom-call | flops 39813120 | bytes 7962624 | tf_op jit(solution)/shard_map/pallas_call | solution.py:175
  58.8 2.9 %multiply_reduce_fusion.3 = f32[1024]{0:T(1024)S(1)} fusion(f32[1296,1024]{1,0:T(8,128)} %shard_map.131), kind=kLoop, calls=%fused_computation.33 | loop fusion | flops 2653184 | bytes 5312512 | tf_op jit(solution)/shard_map/reduce_sum | solution.py:243
  61.7 0.7 fusion.53
  62.6 11.3 %multiply_reduce_fusion.2 = (f32[1024]{0:T(1024)S(1)}, f32[1296,1024]{1,0:T(8,128)S(1)}) fusion(f32[1024]{0:T(1024)S(1)} %get-tuple-element.13, f32[1296,1024]{1,0:T(8,128)} %shard_map.131, f32[1024]{0:T(1024)S(1)} %get-tuple-element.12, bf16[1296,1296]{1,0:T(8,128)(2,1)} %param.16, f32[1024]{0:T(1024)S(1)} %bitcast.104, f32[1296]{0:T(1024)S(1)} %get-tuple-element.21, ...), kind=kOutput, calls=%fused_computation.32 | convolution fusion | flops 3462413312 | bytes 14020288 | tf_op jit(solution)/shard_map/dot_general | solution.py:245
  73.9 6.6 %multiply_reduce_fusion.1 = (f32[1024]{0:T(1024)S(1)}, f32[1296,1024]{1,0:T(8,128)S(1)}) fusion(f32[1024]{0:T(1024)S(1)} %get-tuple-element.9, f32[1296,1024]{1,0:T(8,128)S(1)} %get-tuple-element.15, f32[1024]{0:T(1024)S(1)} %get-tuple-element.8, bf16[1296,1296]{1,0:T(8,128)(2,1)S(1)} %copy-done.6, f32[1024]{0:T(1024)S(1)} %bitcast.105, ...), kind=kOutput, calls=%fused_computation.31 | convolution fusion | flops 3462413312 | bytes 14020288 | tf_op jit(solution)/shard_map/dot_general | solution.py:245
  80.5 8.1 %multiply_reduce_fusion = (f32[1024]{0:T(1024)S(1)}, f32[1296,1024]{1,0:T(8,128)}) fusion(f32[1024]{0:T(1024)S(1)} %get-tuple-element.7, f32[1296,1024]{1,0:T(8,128)S(1)} %get-tuple-element.17, f32[1024]{0:T(1024)S(1)} %get-tuple-element.6, bf16[1296,1296]{1,0:T(8,128)(2,1)S(1)} %copy-done.6, f32[1024]{0:T(1024)S(1)} %bitcast.106, ...), kind=kOutput, calls=%fused_computation.30 | convolution fusion | flops 3462413312 | bytes 14020288 | tf_op jit(solution)/shard_map/dot_general | solution.py:245
  88.8 0.2 reduce_window_sum.11
  89.0 0.2 select_reduce_fusion
  89.2 0.4 fusion.31
  89.6 1.2 gather_fusion.1
  91.0 11.1 %fusion.5 = f32[1296,1024]{1,0:T(8,128)S(1)} fusion(f32[1296,1024]{1,0:T(8,128)} %get-tuple-element.19, bf16[1296,1296]{1,0:T(8,128)(2,1)} %param.16, f32[1024]{0:T(1024)S(1)} %get-tuple-element.5, f32[1024]{0:T(1024)S(1)} %get-tuple-element.4, f32[1024]{0:T(1024)S(1)} %bitcast.107, f32[1296]{0:T(1024)S(1)} %get-tuple-element.21, f32[1024]{0:T(1024)S(1)} %bitcast.103, ...), kind=kOutput, calls=%fused_computation.8 | convolution fusion | flops 3459760128 | bytes 14016192 | tf_op jit(solution)/shard_map/dot_general | solution.py:245
  102.1 2.3 %copy-done.1 = f32[1296,1024]{1,0:T(8,128)} copy-done((f32[1296,1024]{1,0:T(8,128)}, f32[1296,1024]{1,0:T(8,128)S(1)}, u32[]{:S(2)}) %copy-start.1) | copy-done | bytes 5308440
  104.4 2.4 %fusion.28 = bf16[256,1296]{0,1:T(8,128)(2,1)S(1)} fusion(f32[256,1024]{1,0:T(8,128)S(1)} %fusion.31, f32[1296,1024]{1,0:T(8,128)S(1)} %fusion.5, f32[256]{0:T(256)S(1)} %bitcast.114), kind=kOutput, calls=%fused_computation.40 | convolution fusion | flops 2039095296 | bytes 7021568 | tf_op jit(solution)/shard_map/dot_general | solution.py:269
  106.8 0.3 copy.15
  107.3 0.3 concatenate.12
  107.6 1.0 pad_maximum_fusion
  108.6 8.2 %all-to-all-start = ((bf16[16,16,1297]{2,1,0:T(8,128)(2,1)}), bf16[16,16,1297]{2,1,0:T(8,128)(2,1)S(1)}, u32[]{:S(2)}, u32[]{:S(2)}) async-start(bf16[16,16,1297]{2,1,0:T(8,128)(2,1)} %pad_maximum_fusion), calls=%async_computation | async-start | bytes 1441792 | tf_op jit(solution)/shard_map/all_to_all | solution.py:275
  116.8 7.6 %reshape.154 = f32[1296,4,256]{2,1,0:T(4,128)} reshape(f32[1296,1024]{1,0:T(8,128)} %copy-done.1) | data formatting | bytes 10616832 | tf_op jit(solution)/shard_map/reshape | solution.py:284
  124.4 13.7 %all-to-all-done = bf16[16,16,1297]{2,1,0:T(8,128)(2,1)S(1)} async-done(((bf16[16,16,1297]{2,1,0:T(8,128)(2,1)}), bf16[16,16,1297]{2,1,0:T(8,128)(2,1)S(1)}, u32[]{:S(2)}, u32[]{:S(2)}) %all-to-all-start) | async-done | bytes 664096 | tf_op jit(solution)/shard_map/all_to_all | solution.py:275
  138.1 0.2 slice_reduce_fusion
  138.3 1.3 fusion.29
  (37 shorter events, 0.7 us)
Async XLA Ops:
  0.6 89.0 %copy-start = (f32[64]{0:T(128)S(1)}, f32[64]{0:T(128)}, u32[]{:S(2)}) copy-start(f32[64]{0:T(128)} %param.23) | copy-start | bytes 772
  58.8 3.7 %copy-start.2 = (f32[4,256]{1,0:T(4,128)S(1)}, f32[4,256]{1,0:T(4,128)}, u32[]{:S(2)}) copy-start(f32[4,256]{1,0:T(4,128)} %param.18) | copy-start | bytes 12292
  58.8 3.8 %copy-start.3 = (f32[4,256]{1,0:T(4,128)S(1)}, f32[4,256]{1,0:T(4,128)}, u32[]{:S(2)}) copy-start(f32[4,256]{1,0:T(4,128)} %param.17) | copy-start | bytes 12292
  62.6 11.3 %copy-start.6 = (bf16[1296,1296]{1,0:T(8,128)(2,1)S(1)}, bf16[1296,1296]{1,0:T(8,128)(2,1)}, u32[]{:S(2)}) copy-start(bf16[1296,1296]{1,0:T(8,128)(2,1)} %param.16) | copy-start | bytes 10077700
  80.5 8.2 %copy-start.4 = (s32[128,1]{0,1:T(1,128)S(1)}, s32[128,1]{0,1:T(1,128)}, u32[]{:S(2)}) copy-start(s32[128,1]{0,1:T(1,128)} %param.19) | copy-start | bytes 1540
  80.5 8.6 %copy-start.7 = (s32[128]{0:T(128)S(1)}, s32[128]{0:T(128)}, u32[]{:S(2)}) copy-start(s32[128]{0:T(128)} %param.22) | copy-start | bytes 1540
  80.5 8.6 %copy-start.5 = (s32[128]{0:T(128)S(1)}, s32[128]{0:T(128)}, u32[]{:S(2)}) copy-start(s32[128]{0:T(128)} %param.21) | copy-start | bytes 1540
  102.1 2.3 %copy-start.1 = (f32[1296,1024]{1,0:T(8,128)}, f32[1296,1024]{1,0:T(8,128)S(1)}, u32[]{:S(2)}) copy-start(f32[1296,1024]{1,0:T(8,128)S(1)} %fusion.5) | copy-start | bytes 15925252
  102.1 5.1 %copy-start.8 = (s32[128]{0:T(128)S(1)}, s32[128]{0:T(128)}, u32[]{:S(2)}) copy-start(s32[128]{0:T(128)} %param.20) | copy-start | bytes 1540
  108.6 29.5 %all-to-all-start = ((bf16[16,16,1297]{2,1,0:T(8,128)(2,1)}), bf16[16,16,1297]{2,1,0:T(8,128)(2,1)S(1)}, u32[]{:S(2)}, u32[]{:S(2)}) async-start(bf16[16,16,1297]{2,1,0:T(8,128)(2,1)} %pad_maximum_fusion), calls=%async_computation | async-start | bytes 1441792 | tf_op jit(solution)/shard_map/all_to_all | solution.py:275

commit v6 on v5

--- a/solution.py
+++ b/solution.py
@@ -239,18 +239,17 @@
     wind_gain = wind_term(
         all_heading, all_freq, freq_count, wind_speed.reshape(-1), wind_dir.reshape(-1)
     )
-    for step_number in range(SOURCE_STEPS):
-        spread = jnp.sqrt(jnp.mean(spectra_now * spectra_now, axis=0) + EPSILON)
-        rounded = spectra_now.astype(jnp.bfloat16)
+    def source_step(step_number, state):
+        spread = jnp.sqrt(jnp.mean(state * state, axis=0) + EPSILON)
+        rounded = state.astype(jnp.bfloat16)
         transfer = jnp.dot(interaction, rounded, preferred_element_type=jnp.float32)
-        spectra_now = (
+        return (
             sea_cells[None]
-            * (
-                spectra_now
-                + RATE * (wind_gain * spectra_now + spectra_now * transfer / spread[None])
-            )
+            * (state + RATE * (wind_gain * state + state * transfer / spread[None]))
             / (1.0 + RATE * WHITECAP * spread[None])
         )
+
+    spectra_now = lax.fori_loop(0, SOURCE_STEPS, source_step, spectra_now)
 
     slots = grid_count * CAP
     owners = nest_owner[:, 0]

time: 140 us -> 147 us (1.050)
  local copies, waits for them, and re-layouts: 13.7 us -> 28.1 us
  matrix products: 41.4 us -> 38.6 us
  other arithmetic: 6.42 us -> 3.93 us
  Pallas kernels: 55.2 us -> 52.9 us
    while x0 -> x16, local copies, waits for them, and re-layouts: none -> 14.4 us
    dot_general x4, matrix products: 37.1 us -> 31.8 us  [source_step(): transfer = jnp.dot(interaction, rounded, preferred_element_type=jnp.float32)]
    reduce_sum x1, other arithmetic: 2.94 us -> 0.46 us  [source_step(): spread = jnp.sqrt(jnp.mean(state * state, axis=0) + EPSILON)]
    dot_general x1, matrix products: 2.4 us -> 4.85 us  [local(): lax.dot_general(slot_cell, spectra_now, (((1,), (1,)), ((), ())), precisi...]
    pallas_call x1, Pallas kernels: 55.2 us -> 52.9 us  [propagate(): pl.pallas_call(propagate_kernel, in_specs=[smem, smem, vmem, vmem, vmem],...]
where the time goes in v6:
time: 147 us; the launch traced here: 146 us
  Pallas kernels  52.9 us (36%)
  matrix products  38.6 us (26%)
  local copies, waits for them, and re-layouts  28.1 us (19%)
  waiting for transfers between devices  13.7 us (9%)
  starting transfers between devices  8.2 us (6%)
  other arithmetic  3.93 us (3%)
    pallas_call x1, Pallas kernels, propagate(): pl.pallas_call(propagate_kernel, in_specs=[smem, smem, vmem, vmem, vmem],...  52.9 us
    dot_general x4, matrix products, source_step(): transfer = jnp.dot(interaction, rounded, preferred_element_type=jnp.float32)  31.8 us
    while x16, local copies, waits for them, and re-layouts  14.4 us
    all_to_all x1, waiting for transfers between devices, local(): lax.all_to_all(send, 'grid', split_axis=0, concat_axis=0, tiled=True)  13.7 us
    all_to_all x1, starting transfers between devices, local(): lax.all_to_all(send, 'grid', split_axis=0, concat_axis=0, tiled=True)  8.2 us
    reshape x1, local copies, waits for them, and re-layouts, local(): return (spectra_now.reshape(comp_total, row_count, lon_count), nest_spectra)  7.64 us
    dot_general x1, matrix products, local(): lax.dot_general(slot_cell, spectra_now, (((1,), (1,)), ((), ())), precisi...  4.85 us
  transfers between devices with their start and end apart: 1, of which 1 were waited for; matrix products, arithmetic and copies ran while one was open for 5% of the time, Pallas kernels for 0%

profile of v6, /device:TPU:1, one launch (start us, length us, event | category | flops | bytes accessed | tf_op | source)
XLA Modules:
  0.0 146.3 jit_solution(6958083669302503820)
XLA Ops:
  0.8 1.6 %gather_fusion = f32[81]{0:T(128)S(1)} fusion(f32[36]{0:T(128)} %param.15, s32[1024]{0:T(1024)S(1)} %pad_clamp_fusion.1), kind=kCustom, calls=%fused_computation | custom fusion | bytes 972 | tf_op jit(solution)/shard_map/jit(_take)/gather | solution.py:226
  3.5 52.9 %shard_map.131 = f32[1296,1024]{1,0:T(8,128)S(1)} custom-call(f32[81]{0:T(128)} %cosine_multiply_fusion.rx_ref, f32[81]{0:T(128)} %get-tuple-element.131.ry_ref, f32[81,64,256]{2,1,0:T(8,128)} %spec_ref.1, f32[64,256]{1,0:T(8,128)} %factor_ref.1, s32[64,256]{1,0:T(8,128)} %sea_ref.1), custom_call_target="tpu_custom_call" | custom-call | flops 39813120 | bytes 7962624 | tf_op jit(solution)/shard_map/pallas_call | solution.py:175
  56.5 2.3 %copy-done.1 = f32[1296,1024]{1,0:T(8,128)} copy-done((f32[1296,1024]{1,0:T(8,128)}, f32[1296,1024]{1,0:T(8,128)S(1)}, u32[]{:S(2)}) %copy-start.1) | copy-done | bytes 5308440
  59.2 0.7 dynamic-slice_convert_fusion
  60.1 46.3 %while.11 = (s32[]{:T(128)}, f32[1296,1024]{1,0:T(8,128)}, f32[4,256]{1,0:T(4,128)S(1)}, bf16[1296,1296]{1,0:T(8,128)(2,1)}, f32[1024]{0:T(1024)S(1)}, /*index=5...) while((s32[]{:T(128)}, f32[1296,1024]{1,0:T(8,128)}, ...), condition=%wide.region_2.3_spmd.clone, body=%wide.region_0.2_spmd.clone.sunk | while | flops 3462417408 | bytes 38094672 | solution.py:252
  60.1 2.7 %copy.33 = f32[1296,1024]{1,0:T(8,128)S(1)} copy(f32[1296,1024]{1,0:T(8,128)} %get-tuple-element.229) | data formatting | bytes 10616832 | tf_op jit(solution)/shard_map/while
  62.8 0.9 copy-done.6
  63.7 7.9 %multiply_reduce_fusion.3 = (f32[1024]{0:T(1024)S(1)}, f32[1296,1024]{1,0:T(8,128)}) fusion(f32[1024]{0:T(1024)S(1)} %get-tuple-element.212, f32[1296,1024]{1,0:T(8,128)S(1)} %copy.33, f32[1024]{0:T(1024)S(1)} %get-tuple-element.213, bf16[1296,1296]{1,0:T(8,128)(2,1)S(1)} %copy-done.6, f32[1024]{0:T(1024)S(1)} %get-tuple-element.248, ...), kind=kOutput, calls=%fused_computation.3.clone.1 | convolution fusion | flops 3462413312 | bytes 14020288 | tf_op jit(solution)/shard_map/while/body/eval_jaxpr/dot_general | solution.py:245
  71.7 2.7 %copy.33 = f32[1296,1024]{1,0:T(8,128)S(1)} copy(f32[1296,1024]{1,0:T(8,128)} %get-tuple-element.229) | data formatting | bytes 10616832 | tf_op jit(solution)/shard_map/while
  74.4 0.9 copy-done.6
  75.3 7.9 %multiply_reduce_fusion.3 = (f32[1024]{0:T(1024)S(1)}, f32[1296,1024]{1,0:T(8,128)}) fusion(f32[1024]{0:T(1024)S(1)} %get-tuple-element.212, f32[1296,1024]{1,0:T(8,128)S(1)} %copy.33, f32[1024]{0:T(1024)S(1)} %get-tuple-element.213, bf16[1296,1296]{1,0:T(8,128)(2,1)S(1)} %copy-done.6, f32[1024]{0:T(1024)S(1)} %get-tuple-element.248, ...), kind=kOutput, calls=%fused_computation.3.clone.1 | convolution fusion | flops 3462413312 | bytes 14020288 | tf_op jit(solution)/shard_map/while/body/eval_jaxpr/dot_general | solution.py:245
  83.3 2.7 %copy.33 = f32[1296,1024]{1,0:T(8,128)S(1)} copy(f32[1296,1024]{1,0:T(8,128)} %get-tuple-element.229) | data formatting | bytes 10616832 | tf_op jit(solution)/shard_map/while
  85.9 0.9 copy-done.6
  86.9 7.9 %multiply_reduce_fusion.3 = (f32[1024]{0:T(1024)S(1)}, f32[1296,1024]{1,0:T(8,128)}) fusion(f32[1024]{0:T(1024)S(1)} %get-tuple-element.212, f32[1296,1024]{1,0:T(8,128)S(1)} %copy.33, f32[1024]{0:T(1024)S(1)} %get-tuple-element.213, bf16[1296,1296]{1,0:T(8,128)(2,1)S(1)} %copy-done.6, f32[1024]{0:T(1024)S(1)} %get-tuple-element.248, ...), kind=kOutput, calls=%fused_computation.3.clone.1 | convolution fusion | flops 3462413312 | bytes 14020288 | tf_op jit(solution)/shard_map/while/body/eval_jaxpr/dot_general | solution.py:245
  94.8 2.7 %copy.33 = f32[1296,1024]{1,0:T(8,128)S(1)} copy(f32[1296,1024]{1,0:T(8,128)} %get-tuple-element.229) | data formatting | bytes 10616832 | tf_op jit(solution)/shard_map/while
  97.5 0.9 copy-done.6
  98.4 7.9 %multiply_reduce_fusion.3 = (f32[1024]{0:T(1024)S(1)}, f32[1296,1024]{1,0:T(8,128)}) fusion(f32[1024]{0:T(1024)S(1)} %get-tuple-element.212, f32[1296,1024]{1,0:T(8,128)S(1)} %copy.33, f32[1024]{0:T(1024)S(1)} %get-tuple-element.213, bf16[1296,1296]{1,0:T(8,128)(2,1)S(1)} %copy-done.6, f32[1024]{0:T(1024)S(1)} %get-tuple-element.248, ...), kind=kOutput, calls=%fused_computation.3.clone.1 | convolution fusion | flops 3462413312 | bytes 14020288 | tf_op jit(solution)/shard_map/while/body/eval_jaxpr/dot_general | solution.py:245
  107.3 1.2 gather_fusion.1
  108.7 4.8 %fusion.8 = bf16[256,1296]{0,1:T(8,128)(2,1)S(1)} fusion(f32[256,1024]{1,0:T(8,128)S(1)} %fusion.11, f32[1296,1024]{1,0:T(8,128)} %get-tuple-element.29, f32[256]{0:T(256)S(1)} %bitcast.49), kind=kOutput, calls=%fused_computation.15 | convolution fusion | flops 2039095296 | bytes 7021568 | tf_op jit(solution)/shard_map/dot_general | solution.py:268
  114.3 1.0 pad_maximum_fusion
  115.3 8.2 %all-to-all-start = ((bf16[16,16,1297]{2,1,0:T(8,128)(2,1)}), bf16[16,16,1297]{2,1,0:T(8,128)(2,1)S(1)}, u32[]{:S(2)}, u32[]{:S(2)}) async-start(bf16[16,16,1297]{2,1,0:T(8,128)(2,1)} %pad_maximum_fusion), calls=%async_computation | async-start | bytes 1441792 | tf_op jit(solution)/shard_map/all_to_all | solution.py:274
  123.5 7.6 %reshape.121 = f32[1296,4,256]{2,1,0:T(4,128)} reshape(f32[1296,1024]{1,0:T(8,128)} %get-tuple-element.29) | data formatting | bytes 10616832 | tf_op jit(solution)/shard_map/reshape | solution.py:283
  131.2 13.7 %all-to-all-done = bf16[16,16,1297]{2,1,0:T(8,128)(2,1)S(1)} async-done(((bf16[16,16,1297]{2,1,0:T(8,128)(2,1)}), bf16[16,16,1297]{2,1,0:T(8,128)(2,1)S(1)}, u32[]{:S(2)}, u32[]{:S(2)}) %all-to-all-start) | async-done | bytes 664096 | tf_op jit(solution)/shard_map/all_to_all | solution.py:274
  145.0 1.3 fusion.9
  (51 shorter events, 3.8 us)
Async XLA Ops:
  0.6 106.7 %copy-start = (f32[64]{0:T(128)S(1)}, f32[64]{0:T(128)}, u32[]{:S(2)}) copy-start(f32[64]{0:T(128)} %param.25) | copy-start | bytes 772
  56.4 2.3 %copy-start.1 = (f32[1296,1024]{1,0:T(8,128)}, f32[1296,1024]{1,0:T(8,128)S(1)}, u32[]{:S(2)}) copy-start(f32[1296,1024]{1,0:T(8,128)S(1)} %shard_map.131) | copy-start | bytes 15925252
  58.8 1.2 copy-start.2
  58.8 1.2 copy-start.3
  60.0 46.3 %copy-start.4 = (s32[128,1]{0,1:T(1,128)S(1)}, s32[128,1]{0,1:T(1,128)}, u32[]{:S(2)}) copy-start(s32[128,1]{0,1:T(1,128)} %param.21) | copy-start | bytes 1540
  60.0 46.8 %copy-start.7 = (s32[128]{0:T(128)S(1)}, s32[128]{0:T(128)}, u32[]{:S(2)}) copy-start(s32[128]{0:T(128)} %param.24) | copy-start | bytes 1540
  60.1 46.8 %copy-start.5 = (s32[128]{0:T(128)S(1)}, s32[128]{0:T(128)}, u32[]{:S(2)}) copy-start(s32[128]{0:T(128)} %param.23) | copy-start | bytes 1540
  60.1 3.6 %copy-start.6 = (bf16[1296,1296]{1,0:T(8,128)(2,1)S(1)}, bf16[1296,1296]{1,0:T(8,128)(2,1)}, u32[]{:S(2)}) copy-start(bf16[1296,1296]{1,0:T(8,128)(2,1)} %get-tuple-element.243) | copy-start | bytes 10077700 | tf_op jit(solution)/shard_map/while
  71.7 3.6 %copy-start.6 = (bf16[1296,1296]{1,0:T(8,128)(2,1)S(1)}, bf16[1296,1296]{1,0:T(8,128)(2,1)}, u32[]{:S(2)}) copy-start(bf16[1296,1296]{1,0:T(8,128)(2,1)} %get-tuple-element.243) | copy-start | bytes 10077700 | tf_op jit(solution)/shard_map/while
  83.3 3.6 %copy-start.6 = (bf16[1296,1296]{1,0:T(8,128)(2,1)S(1)}, bf16[1296,1296]{1,0:T(8,128)(2,1)}, u32[]{:S(2)}) copy-start(bf16[1296,1296]{1,0:T(8,128)(2,1)} %get-tuple-element.243) | copy-start | bytes 10077700 | tf_op jit(solution)/shard_map/while
  94.8 3.6 %copy-start.6 = (bf16[1296,1296]{1,0:T(8,128)(2,1)S(1)}, bf16[1296,1296]{1,0:T(8,128)(2,1)}, u32[]{:S(2)}) copy-start(bf16[1296,1296]{1,0:T(8,128)(2,1)} %get-tuple-element.243) | copy-start | bytes 10077700 | tf_op jit(solution)/shard_map/while
  106.4 7.5 %copy-start.8 = (s32[128]{0:T(128)S(1)}, s32[128]{0:T(128)}, u32[]{:S(2)}) copy-start(s32[128]{0:T(128)} %param.22) | copy-start | bytes 1540
  115.3 29.5 %all-to-all-start = ((bf16[16,16,1297]{2,1,0:T(8,128)(2,1)}), bf16[16,16,1297]{2,1,0:T(8,128)(2,1)S(1)}, u32[]{:S(2)}, u32[]{:S(2)}) async-start(bf16[16,16,1297]{2,1,0:T(8,128)(2,1)} %pad_maximum_fusion), calls=%async_computation | async-start | bytes 1441792 | tf_op jit(solution)/shard_map/all_to_all | solution.py:274

commit v7 on v5

--- a/solution.py
+++ b/solution.py
@@ -37,7 +37,7 @@
 
 
 def propagate_kernel(
-    rx_ref, ry_ref, spec_ref, factor_ref, sea_ref, out_ref,
+    rx_ref, ry_ref, spec_ref, factor_ref, sea_ref, out_ref, sumsq_ref,
     send_first, send_last, recv_west, recv_east, send_sem, recv_sem,
     result_lo, result_hi, send_buf, a2a_send, a2a_recv, recv_buf,
 ):
@@ -163,8 +163,12 @@
         return carry
 
     lax.fori_loop(0, spec_count, finish, 0)
+    total = jnp.zeros(sumsq_ref.shape, jnp.float32)
     for s in range(spec_count):
-        out_ref[s * comps : (s + 1) * comps, :] = recv_buf[s].astype(out_ref.dtype)
+        part = recv_buf[s].astype(out_ref.dtype)
+        out_ref[s * comps : (s + 1) * comps, :] = part
+        total = total + jnp.sum(part * part, axis=0, keepdims=True)
+    sumsq_ref[...] = total
 
 
 def propagate(spectrum, rate_x, rate_y, factor, sea_float, spec_count):
@@ -175,8 +179,11 @@
     return pl.pallas_call(
         propagate_kernel,
         in_specs=[smem, smem, vmem, vmem, vmem],
-        out_specs=vmem,
-        out_shape=jax.ShapeDtypeStruct((spec_count * comps, chunk * lons), jnp.float32),
+        out_specs=[vmem, vmem],
+        out_shape=[
+            jax.ShapeDtypeStruct((spec_count * comps, chunk * lons), jnp.float32),
+            jax.ShapeDtypeStruct((1, chunk * lons), jnp.float32),
+        ],
         scratch_shapes=[
             pltpu.VMEM((rows, 128), jnp.float32),
             pltpu.VMEM((rows, 128), jnp.float32),
@@ -223,13 +230,16 @@
     heading, freq_index = headings(
         lax.axis_index("spec") * comp_dev, comp_dev, freq_count, dir_count
     )
-    group_rate = jnp.take(group_speed, freq_index)
+    repeats = -(-(freq_count + comp_dev) // freq_count)
+    group_rate = lax.dynamic_slice_in_dim(
+        jnp.tile(group_speed, repeats), lax.rem(lax.axis_index("spec") * comp_dev, freq_count), comp_dev
+    )
     rate_x = group_rate * jnp.cos(heading)
     rate_y = group_rate * jnp.sin(heading)
     sea_float = sea_mask.astype(jnp.float32)
     factor = depth_factor * sea_float
     lon_count = spectrum.shape[2]
-    received = propagate(spectrum, rate_x, rate_y, depth_factor, sea_mask, spec_count)
+    received, first_sumsq = propagate(spectrum, rate_x, rate_y, depth_factor, sea_mask, spec_count)
     row_count = spectrum.shape[1] // spec_count
     cell_count = row_count * lon_count
     spectra_now = received
@@ -240,7 +250,10 @@
         all_heading, all_freq, freq_count, wind_speed.reshape(-1), wind_dir.reshape(-1)
     )
     for step_number in range(SOURCE_STEPS):
-        spread = jnp.sqrt(jnp.mean(spectra_now * spectra_now, axis=0) + EPSILON)
+        if step_number == 0:
+            spread = jnp.sqrt(first_sumsq[0] / comp_total + EPSILON)
+        else:
+            spread = jnp.sqrt(jnp.mean(spectra_now * spectra_now, axis=0) + EPSILON)
         rounded = spectra_now.astype(jnp.bfloat16)
         transfer = jnp.dot(interaction, rounded, preferred_element_type=jnp.float32)
         spectra_now = (

time: 140 us -> 137 us (0.979)
  other arithmetic: 6.42 us -> 3.6 us
    reduce_sum x1 -> x0, other arithmetic: 2.94 us -> none  [local(): spread = jnp.sqrt(jnp.mean(spectra_now * spectra_now, axis=0) + EPSILON)]
    gather x1 -> x0, local copies, waits for them, and re-layouts: 1.59 us -> none  [local(): group_rate = jnp.take(group_speed, freq_index)]
  transfers between devices with their start and end apart: 1 -> 1, of which waited for: 1 -> 1; matrix products, arithmetic and copies ran while one was open for 5% -> 6% of each run, Pallas kernels for 0% -> 0%
where the time goes in v7:
time: 137 us; the launch traced here: 136 us
  Pallas kernels  55.5 us (41%)
  matrix products  41.4 us (30%)
  waiting for transfers between devices  13.7 us (10%)
  local copies, waits for them, and re-layouts  12.8 us (9%)
  starting transfers between devices  8.2 us (6%)
  other arithmetic  3.6 us (3%)
    pallas_call x1, Pallas kernels, propagate(): pl.pallas_call(propagate_kernel, in_specs=[smem, smem, vmem, vmem, vmem],...  55.5 us
    dot_general x4, matrix products, local(): transfer = jnp.dot(interaction, rounded, preferred_element_type=jnp.float32)  37.1 us
    all_to_all x1, waiting for transfers between devices, local(): lax.all_to_all(send, 'grid', split_axis=0, concat_axis=0, tiled=True)  13.7 us
    all_to_all x1, starting transfers between devices, local(): lax.all_to_all(send, 'grid', split_axis=0, concat_axis=0, tiled=True)  8.2 us
    reshape x1, local copies, waits for them, and re-layouts, local(): return (spectra_now.reshape(comp_total, row_count, lon_count), nest_spectra)  7.64 us
  transfers between devices with their start and end apart: 1, of which 1 were waited for; matrix products, arithmetic and copies ran while one was open for 6% of the time, Pallas kernels for 0%

profile of v7, /device:TPU:1, one launch (start us, length us, event | category | flops | bytes accessed | tf_op | source)
XLA Modules:
  0.0 136.1 jit_solution(952740940531182180)
XLA Ops:
  0.8 0.7 tile.4
  1.5 0.6 sine_multiply_fusion
  2.1 55.5 %shard_map.131 = (f32[1296,1024]{1,0:T(8,128)}, f32[1,1024]{1,0:T(1,128)}) custom-call(f32[81]{0:T(128)} %get-tuple-element.17.rx_ref, f32[81]{0:T(128)} %get-tuple-element.16.ry_ref, f32[81,64,256]{2,1,0:T(8,128)} %spec_ref.1, f32[64,256]{1,0:T(8,128)} %factor_ref.1, s32[64,256]{1,0:T(8,128)} %sea_ref.1), custom_call_target="tpu_custom_call" | custom-call | flops 39813120 | bytes 7962624 | tf_op jit(solution)/shard_map/pallas_call | solution.py:179
  57.6 0.7 multiply_add_fusion.3
  58.4 0.7 fusion.53
  59.2 11.3 %multiply_reduce_fusion.2 = (f32[1024]{0:T(1024)S(1)}, f32[1296,1024]{1,0:T(8,128)S(1)}) fusion(f32[1024]{0:T(1024)S(1)} %bitcast.95, f32[1296,1024]{1,0:T(8,128)} %get-tuple-element.4, f32[1024]{0:T(1024)S(1)} %bitcast.96, bf16[1296,1296]{1,0:T(8,128)(2,1)} %param.16, f32[1024]{0:T(1024)S(1)} %bitcast.106, f32[1296]{0:T(1024)S(1)} %get-tuple-element.25, ...), kind=kOutput, calls=%fused_computation.31 | convolution fusion | flops 3462413312 | bytes 14020288 | tf_op jit(solution)/shard_map/dot_general | solution.py:258
  70.5 6.6 %multiply_reduce_fusion.1 = (f32[1024]{0:T(1024)S(1)}, f32[1296,1024]{1,0:T(8,128)S(1)}) fusion(f32[1024]{0:T(1024)S(1)} %get-tuple-element.13, f32[1296,1024]{1,0:T(8,128)S(1)} %get-tuple-element.19, f32[1024]{0:T(1024)S(1)} %get-tuple-element.12, bf16[1296,1296]{1,0:T(8,128)(2,1)S(1)} %copy-done.6, f32[1024]{0:T(1024)S(1)} %bitcast.107, ...), kind=kOutput, calls=%fused_computation.30 | convolution fusion | flops 3462413312 | bytes 14020288 | tf_op jit(solution)/shard_map/dot_general | solution.py:258
  77.1 8.1 %multiply_reduce_fusion = (f32[1024]{0:T(1024)S(1)}, f32[1296,1024]{1,0:T(8,128)}) fusion(f32[1024]{0:T(1024)S(1)} %get-tuple-element.11, f32[1296,1024]{1,0:T(8,128)S(1)} %get-tuple-element.21, f32[1024]{0:T(1024)S(1)} %get-tuple-element.10, bf16[1296,1296]{1,0:T(8,128)(2,1)S(1)} %copy-done.6, f32[1024]{0:T(1024)S(1)} %bitcast.108, ...), kind=kOutput, calls=%fused_computation.29 | convolution fusion | flops 3462413312 | bytes 14020288 | tf_op jit(solution)/shard_map/dot_general | solution.py:258
  85.4 0.2 reduce_window_sum.11
  85.5 0.2 select_reduce_fusion
  85.8 0.4 fusion.31
  86.2 1.2 gather_fusion
  87.6 11.1 %fusion.5 = f32[1296,1024]{1,0:T(8,128)S(1)} fusion(f32[1296,1024]{1,0:T(8,128)} %get-tuple-element.23, bf16[1296,1296]{1,0:T(8,128)(2,1)} %param.16, f32[1024]{0:T(1024)S(1)} %get-tuple-element.9, f32[1024]{0:T(1024)S(1)} %get-tuple-element.8, f32[1024]{0:T(1024)S(1)} %bitcast.109, f32[1296]{0:T(1024)S(1)} %get-tuple-element.25, f32[1024]{0:T(1024)S(1)} %bitcast.105, ...), kind=kOutput, calls=%fused_computation.7 | convolution fusion | flops 3459760128 | bytes 14016192 | tf_op jit(solution)/shard_map/dot_general | solution.py:258
  98.7 2.3 %copy-done.1 = f32[1296,1024]{1,0:T(8,128)} copy-done((f32[1296,1024]{1,0:T(8,128)}, f32[1296,1024]{1,0:T(8,128)S(1)}, u32[]{:S(2)}) %copy-start.1) | copy-done | bytes 5308440
  101.0 2.4 %fusion.28 = bf16[256,1296]{0,1:T(8,128)(2,1)S(1)} fusion(f32[256,1024]{1,0:T(8,128)S(1)} %fusion.31, f32[1296,1024]{1,0:T(8,128)S(1)} %fusion.5, f32[256]{0:T(256)S(1)} %bitcast.116), kind=kOutput, calls=%fused_computation.38 | convolution fusion | flops 2039095296 | bytes 7021568 | tf_op jit(solution)/shard_map/dot_general | solution.py:282
  103.4 0.3 copy.15
  103.7 0.1 fusion.33
  103.8 0.3 concatenate.12
  104.2 1.0 pad_maximum_fusion
  105.2 8.2 %all-to-all-start = ((bf16[16,16,1297]{2,1,0:T(8,128)(2,1)}), bf16[16,16,1297]{2,1,0:T(8,128)(2,1)S(1)}, u32[]{:S(2)}, u32[]{:S(2)}) async-start(bf16[16,16,1297]{2,1,0:T(8,128)(2,1)} %pad_maximum_fusion), calls=%async_computation | async-start | bytes 1441792 | tf_op jit(solution)/shard_map/all_to_all | solution.py:288
  113.4 7.6 %reshape.107 = f32[1296,4,256]{2,1,0:T(4,128)} reshape(f32[1296,1024]{1,0:T(8,128)} %copy-done.1) | data formatting | bytes 10616832 | tf_op jit(solution)/shard_map/reshape | solution.py:297
  121.0 13.7 %all-to-all-done = bf16[16,16,1297]{2,1,0:T(8,128)(2,1)S(1)} async-done(((bf16[16,16,1297]{2,1,0:T(8,128)(2,1)}), bf16[16,16,1297]{2,1,0:T(8,128)(2,1)S(1)}, u32[]{:S(2)}, u32[]{:S(2)}) %all-to-all-start) | async-done | bytes 664096 | tf_op jit(solution)/shard_map/all_to_all | solution.py:288
  134.7 0.2 slice_reduce_fusion
  134.9 1.3 fusion.29
  (34 shorter events, 0.6 us)
Async XLA Ops:
  0.6 85.6 %copy-start = (f32[64]{0:T(128)S(1)}, f32[64]{0:T(128)}, u32[]{:S(2)}) copy-start(f32[64]{0:T(128)} %param.23) | copy-start | bytes 772
  0.6 58.4 %copy-start.2 = (f32[4,256]{1,0:T(4,128)S(1)}, f32[4,256]{1,0:T(4,128)}, u32[]{:S(2)}) copy-start(f32[4,256]{1,0:T(4,128)} %param.18) | copy-start | bytes 12292
  0.7 58.5 %copy-start.3 = (f32[4,256]{1,0:T(4,128)S(1)}, f32[4,256]{1,0:T(4,128)}, u32[]{:S(2)}) copy-start(f32[4,256]{1,0:T(4,128)} %param.17) | copy-start | bytes 12292
  59.2 11.3 %copy-start.6 = (bf16[1296,1296]{1,0:T(8,128)(2,1)S(1)}, bf16[1296,1296]{1,0:T(8,128)(2,1)}, u32[]{:S(2)}) copy-start(bf16[1296,1296]{1,0:T(8,128)(2,1)} %param.16) | copy-start | bytes 10077700
  77.1 8.2 %copy-start.4 = (s32[128,1]{0,1:T(1,128)S(1)}, s32[128,1]{0,1:T(1,128)}, u32[]{:S(2)}) copy-start(s32[128,1]{0,1:T(1,128)} %param.19) | copy-start | bytes 1540
  77.1 8.6 %copy-start.7 = (s32[128]{0:T(128)S(1)}, s32[128]{0:T(128)}, u32[]{:S(2)}) copy-start(s32[128]{0:T(128)} %param.22) | copy-start | bytes 1540
  77.1 8.7 %copy-start.5 = (s32[128]{0:T(128)S(1)}, s32[128]{0:T(128)}, u32[]{:S(2)}) copy-start(s32[128]{0:T(128)} %param.21) | copy-start | bytes 1540
  98.6 2.3 %copy-start.1 = (f32[1296,1024]{1,0:T(8,128)}, f32[1296,1024]{1,0:T(8,128)S(1)}, u32[]{:S(2)}) copy-start(f32[1296,1024]{1,0:T(8,128)S(1)} %fusion.5) | copy-start | bytes 15925252
  98.6 5.1 %copy-start.8 = (s32[128]{0:T(128)S(1)}, s32[128]{0:T(128)}, u32[]{:S(2)}) copy-start(s32[128]{0:T(128)} %param.20) | copy-start | bytes 1540
  105.2 29.5 %all-to-all-start = ((bf16[16,16,1297]{2,1,0:T(8,128)(2,1)}), bf16[16,16,1297]{2,1,0:T(8,128)(2,1)S(1)}, u32[]{:S(2)}, u32[]{:S(2)}) async-start(bf16[16,16,1297]{2,1,0:T(8,128)(2,1)} %pad_maximum_fusion), calls=%async_computation | async-start | bytes 1441792 | tf_op jit(solution)/shard_map/all_to_all | solution.py:288

commit v8 on v7

--- a/solution.py
+++ b/solution.py
@@ -270,7 +270,13 @@
     member = (owners[:, None] == jnp.arange(grid_count, dtype=jnp.int32)[None]).astype(jnp.int32)
     slot_rank = jnp.sum((jnp.cumsum(member, axis=0) - member) * member, axis=1)
     column = owners * CAP + slot_rank
-    weights = jnp.take(weight_table, weight_index)
+    table_rows = weight_table.shape[0]
+    weights = jnp.sum(
+        jnp.where(
+            weight_index[:, None] == jnp.arange(table_rows, dtype=jnp.int32)[None], weight_table[None], 0.0
+        ),
+        axis=1,
+    )
     pick_slot = (column[:, None] == jnp.arange(slots, dtype=jnp.int32)[None]).astype(jnp.float32)
     pick_cell = (nest_cell[:, None] == jnp.arange(cell_count, dtype=jnp.int32)[None]).astype(jnp.float32)
     slot_cell = jnp.dot(pick_slot.T, pick_cell, precision=HIGHEST, preferred_element_type=jnp.float32)

time: 137 us -> 135 us (0.985)
  no operation moved by 1% of the time
where the time goes in v8:
time: 135 us
  Pallas kernels  55.4 us (41%)
  matrix products  41.1 us (30%)
  waiting for transfers between devices  13.7 us (10%)
  local copies, waits for them, and re-layouts  11.6 us (9%)
  starting transfers between devices  8.31 us (6%)
  other arithmetic  3.67 us (3%)
    pallas_call x1, Pallas kernels, propagate(): pl.pallas_call(propagate_kernel, in_specs=[smem, smem, vmem, vmem, vmem],...  55.4 us
    dot_general x4, matrix products, local(): transfer = jnp.dot(interaction, rounded, preferred_element_type=jnp.float32)  36.7 us
    all_to_all x1, waiting for transfers between devices, local(): lax.all_to_all(send, 'grid', split_axis=0, concat_axis=0, tiled=True)  13.7 us
    all_to_all x1, starting transfers between devices, local(): lax.all_to_all(send, 'grid', split_axis=0, concat_axis=0, tiled=True)  8.31 us
    reshape x1, local copies, waits for them, and re-layouts, local(): return (spectra_now.reshape(comp_total, row_count, lon_count), nest_spectra)  7.64 us
  transfers between devices with their start and end apart: 1, of which 1 were waited for; matrix products, arithmetic and copies ran while one was open for 6% of the time, Pallas kernels for 0%

profile of v8, /device:TPU:1, one launch (start us, length us, event | category | flops | bytes accessed | tf_op | source)
XLA Modules:
  0.0 134.6 jit_solution(1412422347277014741)
XLA Ops:
  0.8 0.7 tile.4
  1.5 0.6 sine_multiply_fusion
  2.1 55.4 %shard_map.131 = (f32[1296,1024]{1,0:T(8,128)}, f32[1,1024]{1,0:T(1,128)}) custom-call(f32[81]{0:T(128)} %get-tuple-element.17.rx_ref, f32[81]{0:T(128)} %get-tuple-element.16.ry_ref, f32[81,64,256]{2,1,0:T(8,128)} %spec_ref.1, f32[64,256]{1,0:T(8,128)} %factor_ref.1, s32[64,256]{1,0:T(8,128)} %sea_ref.1), custom_call_target="tpu_custom_call" | custom-call | flops 39813120 | bytes 7962624 | tf_op jit(solution)/shard_map/pallas_call | solution.py:179
  57.5 0.7 multiply_add_fusion.3
  58.2 0.7 fusion.53
  59.0 11.2 %multiply_reduce_fusion.2 = (f32[1024]{0:T(1024)S(1)}, f32[1296,1024]{1,0:T(8,128)S(1)}) fusion(f32[1024]{0:T(1024)S(1)} %bitcast.95, f32[1296,1024]{1,0:T(8,128)} %get-tuple-element.4, f32[1024]{0:T(1024)S(1)} %bitcast.96, bf16[1296,1296]{1,0:T(8,128)(2,1)} %param.16, f32[1024]{0:T(1024)S(1)} %bitcast.106, f32[1296]{0:T(1024)S(1)} %get-tuple-element.25, ...), kind=kOutput, calls=%fused_computation.30 | convolution fusion | flops 3462413312 | bytes 14020288 | tf_op jit(solution)/shard_map/dot_general | solution.py:258
  70.3 6.4 %multiply_reduce_fusion.1 = (f32[1024]{0:T(1024)S(1)}, f32[1296,1024]{1,0:T(8,128)S(1)}) fusion(f32[1024]{0:T(1024)S(1)} %get-tuple-element.13, f32[1296,1024]{1,0:T(8,128)S(1)} %get-tuple-element.19, f32[1024]{0:T(1024)S(1)} %get-tuple-element.12, bf16[1296,1296]{1,0:T(8,128)(2,1)S(1)} %copy-done.5, f32[1024]{0:T(1024)S(1)} %bitcast.107, ...), kind=kOutput, calls=%fused_computation.29 | convolution fusion | flops 3462413312 | bytes 14020288 | tf_op jit(solution)/shard_map/dot_general | solution.py:258
  76.8 8.0 %multiply_reduce_fusion = (f32[1024]{0:T(1024)S(1)}, f32[1296,1024]{1,0:T(8,128)}) fusion(f32[1024]{0:T(1024)S(1)} %get-tuple-element.11, f32[1296,1024]{1,0:T(8,128)S(1)} %get-tuple-element.21, f32[1024]{0:T(1024)S(1)} %get-tuple-element.10, bf16[1296,1296]{1,0:T(8,128)(2,1)S(1)} %copy-done.5, f32[1024]{0:T(1024)S(1)} %bitcast.108, ...), kind=kOutput, calls=%fused_computation.28 | convolution fusion | flops 3462413312 | bytes 14020288 | tf_op jit(solution)/shard_map/dot_general | solution.py:258
  84.9 0.2 reduce_window_sum.11
  85.0 0.2 select_reduce_fusion
  85.2 0.4 fusion.31
  85.8 0.1 fusion.34
  85.9 11.0 %fusion.5 = f32[1296,1024]{1,0:T(8,128)S(1)} fusion(f32[1296,1024]{1,0:T(8,128)} %get-tuple-element.23, bf16[1296,1296]{1,0:T(8,128)(2,1)} %param.16, f32[1024]{0:T(1024)S(1)} %get-tuple-element.9, f32[1024]{0:T(1024)S(1)} %get-tuple-element.8, f32[1024]{0:T(1024)S(1)} %bitcast.109, f32[1296]{0:T(1024)S(1)} %get-tuple-element.25, f32[1024]{0:T(1024)S(1)} %bitcast.105, ...), kind=kOutput, calls=%fused_computation.6 | convolution fusion | flops 3459760128 | bytes 14016192 | tf_op jit(solution)/shard_map/dot_general | solution.py:258
  97.0 2.3 %copy-done = f32[1296,1024]{1,0:T(8,128)} copy-done((f32[1296,1024]{1,0:T(8,128)}, f32[1296,1024]{1,0:T(8,128)S(1)}, u32[]{:S(2)}) %copy-start) | copy-done | bytes 5308440
  99.3 2.4 %fusion.28 = bf16[256,1296]{0,1:T(8,128)(2,1)S(1)} fusion(f32[256,1024]{1,0:T(8,128)S(1)} %fusion.31, f32[1296,1024]{1,0:T(8,128)S(1)} %fusion.5, f32[256]{0:T(256)S(1)} %bitcast.116), kind=kOutput, calls=%fused_computation.37 | convolution fusion | flops 2039095296 | bytes 7021568 | tf_op jit(solution)/shard_map/dot_general | solution.py:288
  101.7 0.3 copy.17
  102.1 0.1 fusion.33
  102.2 0.3 concatenate.12
  102.5 1.0 pad_maximum_fusion
  103.5 8.3 %all-to-all-start = ((bf16[16,16,1297]{2,1,0:T(8,128)(2,1)}), bf16[16,16,1297]{2,1,0:T(8,128)(2,1)S(1)}, u32[]{:S(2)}, u32[]{:S(2)}) async-start(bf16[16,16,1297]{2,1,0:T(8,128)(2,1)} %pad_maximum_fusion), calls=%async_computation | async-start | bytes 1441792 | tf_op jit(solution)/shard_map/all_to_all | solution.py:294
  111.8 7.6 %reshape.104 = f32[1296,4,256]{2,1,0:T(4,128)} reshape(f32[1296,1024]{1,0:T(8,128)} %copy-done) | data formatting | bytes 10616832 | tf_op jit(solution)/shard_map/reshape | solution.py:303
  119.5 13.7 %all-to-all-done = bf16[16,16,1297]{2,1,0:T(8,128)(2,1)S(1)} async-done(((bf16[16,16,1297]{2,1,0:T(8,128)(2,1)}), bf16[16,16,1297]{2,1,0:T(8,128)(2,1)S(1)}, u32[]{:S(2)}, u32[]{:S(2)}) %all-to-all-start) | async-done | bytes 664096 | tf_op jit(solution)/shard_map/all_to_all | solution.py:294
  133.1 0.2 slice_reduce_fusion
  133.3 1.3 fusion.29
  (32 shorter events, 0.5 us)
Async XLA Ops:
  0.6 58.3 %copy-start.1 = (f32[4,256]{1,0:T(4,128)S(1)}, f32[4,256]{1,0:T(4,128)}, u32[]{:S(2)}) copy-start(f32[4,256]{1,0:T(4,128)} %param.18) | copy-start | bytes 12292
  0.6 58.3 %copy-start.2 = (f32[4,256]{1,0:T(4,128)S(1)}, f32[4,256]{1,0:T(4,128)}, u32[]{:S(2)}) copy-start(f32[4,256]{1,0:T(4,128)} %param.17) | copy-start | bytes 12292
  59.0 11.3 %copy-start.5 = (bf16[1296,1296]{1,0:T(8,128)(2,1)S(1)}, bf16[1296,1296]{1,0:T(8,128)(2,1)}, u32[]{:S(2)}) copy-start(bf16[1296,1296]{1,0:T(8,128)(2,1)} %param.16) | copy-start | bytes 10077700
  76.8 8.0 %copy-start.3 = (s32[128,1]{0,1:T(1,128)S(1)}, s32[128,1]{0,1:T(1,128)}, u32[]{:S(2)}) copy-start(s32[128,1]{0,1:T(1,128)} %param.19) | copy-start | bytes 1540
  76.8 8.5 %copy-start.4 = (s32[128]{0:T(128)S(1)}, s32[128]{0:T(128)}, u32[]{:S(2)}) copy-start(s32[128]{0:T(128)} %param.21) | copy-start | bytes 1540
  76.8 8.9 %copy-start.6 = (f32[64]{0:T(128)S(1)}, f32[64]{0:T(128)}, u32[]{:S(2)}) copy-start(f32[64]{0:T(128)} %param.23) | copy-start | bytes 772
  76.8 8.9 %copy-start.7 = (s32[128]{0:T(128)S(1)}, s32[128]{0:T(128)}, u32[]{:S(2)}) copy-start(s32[128]{0:T(128)} %param.22) | copy-start | bytes 1540
  97.0 2.3 %copy-start = (f32[1296,1024]{1,0:T(8,128)}, f32[1296,1024]{1,0:T(8,128)S(1)}, u32[]{:S(2)}) copy-start(f32[1296,1024]{1,0:T(8,128)S(1)} %fusion.5) | copy-start | bytes 15925252
  97.0 5.1 %copy-start.8 = (s32[128]{0:T(128)S(1)}, s32[128]{0:T(128)}, u32[]{:S(2)}) copy-start(s32[128]{0:T(128)} %param.20) | copy-start | bytes 1540
  103.5 29.6 %all-to-all-start = ((bf16[16,16,1297]{2,1,0:T(8,128)(2,1)}), bf16[16,16,1297]{2,1,0:T(8,128)(2,1)S(1)}, u32[]{:S(2)}, u32[]{:S(2)}) async-start(bf16[16,16,1297]{2,1,0:T(8,128)(2,1)} %pad_maximum_fusion), calls=%async_computation | async-start | bytes 1441792 | tf_op jit(solution)/shard_map/all_to_all | solution.py:294

commit v9 on v8

--- a/solution.py
+++ b/solution.py
@@ -130,7 +130,7 @@
     blocks = [(tile * b, tile) for b in range(count - 1)]
     blocks.append((tile * (count - 1), comps - tile * (count - 1)))
     for start, size in blocks:
-        lax.fori_loop(start, start + size, one, 0)
+        lax.fori_loop(start, start + size, one, 0, unroll=2)
 
         def regroup(t, carry, start=start, size=size):
             d = lax.rem(spec + t, spec_count)

time: 135 us -> 134 us (level)
  Pallas kernels: 55.4 us -> 51.1 us
  starting transfers between devices: 8.31 us -> 11.9 us
    pallas_call x1, Pallas kernels: 55.4 us -> 51.1 us  [propagate(): pl.pallas_call(propagate_kernel, in_specs=[smem, smem, vmem, vmem, vmem],...]
    all_to_all x1, starting transfers between devices: 8.31 us -> 11.9 us  [local(): lax.all_to_all(send, 'grid', split_axis=0, concat_axis=0, tiled=True)]
where the time goes in v9:
time: 134 us
  Pallas kernels  51.1 us (38%)
  matrix products  41.1 us (31%)
  waiting for transfers between devices  13.7 us (10%)
  starting transfers between devices  11.9 us (9%)
  local copies, waits for them, and re-layouts  11.6 us (9%)
  other arithmetic  3.67 us (3%)
    pallas_call x1, Pallas kernels, propagate(): pl.pallas_call(propagate_kernel, in_specs=[smem, smem, vmem, vmem, vmem],...  51.1 us
    dot_general x4, matrix products, local(): transfer = jnp.dot(interaction, rounded, preferred_element_type=jnp.float32)  36.7 us
    all_to_all x1, waiting for transfers between devices, local(): lax.all_to_all(send, 'grid', split_axis=0, concat_axis=0, tiled=True)  13.7 us
    all_to_all x1, starting transfers between devices, local(): lax.all_to_all(send, 'grid', split_axis=0, concat_axis=0, tiled=True)  11.9 us
    reshape x1, local copies, waits for them, and re-layouts, local(): return (spectra_now.reshape(comp_total, row_count, lon_count), nest_spectra)  7.64 us
  transfers between devices with their start and end apart: 1, of which 1 were waited for; matrix products, arithmetic and copies ran while one was open for 6% of the time, Pallas kernels for 0%

profile of v9, /device:TPU:1, one launch (start us, length us, event | category | flops | bytes accessed | tf_op | source)
XLA Modules:
  0.0 134.0 jit_solution(3889932977270785216)
XLA Ops:
  0.8 0.7 tile.4
  1.5 0.6 sine_multiply_fusion
  2.1 51.1 %shard_map.131 = (f32[1296,1024]{1,0:T(8,128)}, f32[1,1024]{1,0:T(1,128)}) custom-call(f32[81]{0:T(128)} %get-tuple-element.17.rx_ref, f32[81]{0:T(128)} %get-tuple-element.16.ry_ref, f32[81,64,256]{2,1,0:T(8,128)} %spec_ref.1, f32[64,256]{1,0:T(8,128)} %factor_ref.1, s32[64,256]{1,0:T(8,128)} %sea_ref.1), custom_call_target="tpu_custom_call" | custom-call | flops 39813120 | bytes 7962624 | tf_op jit(solution)/shard_map/pallas_call | solution.py:179
  53.2 0.7 multiply_add_fusion.3
  53.9 0.7 fusion.53
  54.8 11.2 %multiply_reduce_fusion.2 = (f32[1024]{0:T(1024)S(1)}, f32[1296,1024]{1,0:T(8,128)S(1)}) fusion(f32[1024]{0:T(1024)S(1)} %bitcast.95, f32[1296,1024]{1,0:T(8,128)} %get-tuple-element.4, f32[1024]{0:T(1024)S(1)} %bitcast.96, bf16[1296,1296]{1,0:T(8,128)(2,1)} %param.16, f32[1024]{0:T(1024)S(1)} %bitcast.106, f32[1296]{0:T(1024)S(1)} %get-tuple-element.25, ...), kind=kOutput, calls=%fused_computation.30 | convolution fusion | flops 3462413312 | bytes 14020288 | tf_op jit(solution)/shard_map/dot_general | solution.py:258
  66.0 6.4 %multiply_reduce_fusion.1 = (f32[1024]{0:T(1024)S(1)}, f32[1296,1024]{1,0:T(8,128)S(1)}) fusion(f32[1024]{0:T(1024)S(1)} %get-tuple-element.13, f32[1296,1024]{1,0:T(8,128)S(1)} %get-tuple-element.19, f32[1024]{0:T(1024)S(1)} %get-tuple-element.12, bf16[1296,1296]{1,0:T(8,128)(2,1)S(1)} %copy-done.5, f32[1024]{0:T(1024)S(1)} %bitcast.107, ...), kind=kOutput, calls=%fused_computation.29 | convolution fusion | flops 3462413312 | bytes 14020288 | tf_op jit(solution)/shard_map/dot_general | solution.py:258
  72.5 8.0 %multiply_reduce_fusion = (f32[1024]{0:T(1024)S(1)}, f32[1296,1024]{1,0:T(8,128)}) fusion(f32[1024]{0:T(1024)S(1)} %get-tuple-element.11, f32[1296,1024]{1,0:T(8,128)S(1)} %get-tuple-element.21, f32[1024]{0:T(1024)S(1)} %get-tuple-element.10, bf16[1296,1296]{1,0:T(8,128)(2,1)S(1)} %copy-done.5, f32[1024]{0:T(1024)S(1)} %bitcast.108, ...), kind=kOutput, calls=%fused_computation.28 | convolution fusion | flops 3462413312 | bytes 14020288 | tf_op jit(solution)/shard_map/dot_general | solution.py:258
  80.6 0.2 reduce_window_sum.11
  80.8 0.2 select_reduce_fusion
  81.0 0.4 fusion.31
  81.5 0.1 fusion.34
  81.7 11.0 %fusion.5 = f32[1296,1024]{1,0:T(8,128)S(1)} fusion(f32[1296,1024]{1,0:T(8,128)} %get-tuple-element.23, bf16[1296,1296]{1,0:T(8,128)(2,1)} %param.16, f32[1024]{0:T(1024)S(1)} %get-tuple-element.9, f32[1024]{0:T(1024)S(1)} %get-tuple-element.8, f32[1024]{0:T(1024)S(1)} %bitcast.109, f32[1296]{0:T(1024)S(1)} %get-tuple-element.25, f32[1024]{0:T(1024)S(1)} %bitcast.105, ...), kind=kOutput, calls=%fused_computation.6 | convolution fusion | flops 3459760128 | bytes 14016192 | tf_op jit(solution)/shard_map/dot_general | solution.py:258
  92.7 2.3 %copy-done = f32[1296,1024]{1,0:T(8,128)} copy-done((f32[1296,1024]{1,0:T(8,128)}, f32[1296,1024]{1,0:T(8,128)S(1)}, u32[]{:S(2)}) %copy-start) | copy-done | bytes 5308440
  95.0 2.4 %fusion.28 = bf16[256,1296]{0,1:T(8,128)(2,1)S(1)} fusion(f32[256,1024]{1,0:T(8,128)S(1)} %fusion.31, f32[1296,1024]{1,0:T(8,128)S(1)} %fusion.5, f32[256]{0:T(256)S(1)} %bitcast.116), kind=kOutput, calls=%fused_computation.37 | convolution fusion | flops 2039095296 | bytes 7021568 | tf_op jit(solution)/shard_map/dot_general | solution.py:288
  97.5 0.3 copy.17
  97.8 0.1 fusion.33
  97.9 0.3 concatenate.12
  98.2 1.0 pad_maximum_fusion
  99.3 11.9 %all-to-all-start = ((bf16[16,16,1297]{2,1,0:T(8,128)(2,1)}), bf16[16,16,1297]{2,1,0:T(8,128)(2,1)S(1)}, u32[]{:S(2)}, u32[]{:S(2)}) async-start(bf16[16,16,1297]{2,1,0:T(8,128)(2,1)} %pad_maximum_fusion), calls=%async_computation | async-start | bytes 1441792 | tf_op jit(solution)/shard_map/all_to_all | solution.py:294
  111.2 7.6 %reshape.104 = f32[1296,4,256]{2,1,0:T(4,128)} reshape(f32[1296,1024]{1,0:T(8,128)} %copy-done) | data formatting | bytes 10616832 | tf_op jit(solution)/shard_map/reshape | solution.py:303
  118.8 13.7 %all-to-all-done = bf16[16,16,1297]{2,1,0:T(8,128)(2,1)S(1)} async-done(((bf16[16,16,1297]{2,1,0:T(8,128)(2,1)}), bf16[16,16,1297]{2,1,0:T(8,128)(2,1)S(1)}, u32[]{:S(2)}, u32[]{:S(2)}) %all-to-all-start) | async-done | bytes 664096 | tf_op jit(solution)/shard_map/all_to_all | solution.py:294
  132.5 0.2 slice_reduce_fusion
  132.7 1.3 fusion.29
  (32 shorter events, 0.5 us)
Async XLA Ops:
  0.6 54.0 %copy-start.1 = (f32[4,256]{1,0:T(4,128)S(1)}, f32[4,256]{1,0:T(4,128)}, u32[]{:S(2)}) copy-start(f32[4,256]{1,0:T(4,128)} %param.18) | copy-start | bytes 12292
  0.6 54.1 %copy-start.2 = (f32[4,256]{1,0:T(4,128)S(1)}, f32[4,256]{1,0:T(4,128)}, u32[]{:S(2)}) copy-start(f32[4,256]{1,0:T(4,128)} %param.17) | copy-start | bytes 12292
  54.7 11.3 %copy-start.5 = (bf16[1296,1296]{1,0:T(8,128)(2,1)S(1)}, bf16[1296,1296]{1,0:T(8,128)(2,1)}, u32[]{:S(2)}) copy-start(bf16[1296,1296]{1,0:T(8,128)(2,1)} %param.16) | copy-start | bytes 10077700
  72.5 8.0 %copy-start.3 = (s32[128,1]{0,1:T(1,128)S(1)}, s32[128,1]{0,1:T(1,128)}, u32[]{:S(2)}) copy-start(s32[128,1]{0,1:T(1,128)} %param.19) | copy-start | bytes 1540
  72.5 8.5 %copy-start.4 = (s32[128]{0:T(128)S(1)}, s32[128]{0:T(128)}, u32[]{:S(2)}) copy-start(s32[128]{0:T(128)} %param.21) | copy-start | bytes 1540
  72.5 8.9 %copy-start.6 = (f32[64]{0:T(128)S(1)}, f32[64]{0:T(128)}, u32[]{:S(2)}) copy-start(f32[64]{0:T(128)} %param.23) | copy-start | bytes 772
  72.5 8.9 %copy-start.7 = (s32[128]{0:T(128)S(1)}, s32[128]{0:T(128)}, u32[]{:S(2)}) copy-start(s32[128]{0:T(128)} %param.22) | copy-start | bytes 1540
  92.7 2.3 %copy-start = (f32[1296,1024]{1,0:T(8,128)}, f32[1296,1024]{1,0:T(8,128)S(1)}, u32[]{:S(2)}) copy-start(f32[1296,1024]{1,0:T(8,128)S(1)} %fusion.5) | copy-start | bytes 15925252
  92.7 5.1 %copy-start.8 = (s32[128]{0:T(128)S(1)}, s32[128]{0:T(128)}, u32[]{:S(2)}) copy-start(s32[128]{0:T(128)} %param.20) | copy-start | bytes 1540
  99.3 33.2 %all-to-all-start = ((bf16[16,16,1297]{2,1,0:T(8,128)(2,1)}), bf16[16,16,1297]{2,1,0:T(8,128)(2,1)S(1)}, u32[]{:S(2)}, u32[]{:S(2)}) async-start(bf16[16,16,1297]{2,1,0:T(8,128)(2,1)} %pad_maximum_fusion), calls=%async_computation | async-start | bytes 1441792 | tf_op jit(solution)/shard_map/all_to_all | solution.py:294

commit v10 on v9

--- a/solution.py
+++ b/solution.py
@@ -130,7 +130,7 @@
     blocks = [(tile * b, tile) for b in range(count - 1)]
     blocks.append((tile * (count - 1), comps - tile * (count - 1)))
     for start, size in blocks:
-        lax.fori_loop(start, start + size, one, 0, unroll=2)
+        lax.fori_loop(start, start + size, one, 0, unroll=4)
 
         def regroup(t, carry, start=start, size=size):
             d = lax.rem(spec + t, spec_count)
@@ -152,7 +152,7 @@
 
             return carry
 
-        lax.fori_loop(0, spec_count, regroup, 0)
+        lax.fori_loop(0, spec_count, regroup, 0, unroll=2)
 
     def finish(d, carry):
         @pl.when(d != spec)

time: 134 us -> 134 us (level)
  no operation moved by 1% of the time
where the time goes in v10:
time: 134 us
  Pallas kernels  50.8 us (38%)
  matrix products  41.1 us (31%)
  waiting for transfers between devices  13.7 us (10%)
  starting transfers between devices  11.9 us (9%)
  local copies, waits for them, and re-layouts  11.6 us (9%)
  other arithmetic  3.67 us (3%)
    pallas_call x1, Pallas kernels, propagate(): pl.pallas_call(propagate_kernel, in_specs=[smem, smem, vmem, vmem, vmem],...  50.8 us
    dot_general x4, matrix products, local(): transfer = jnp.dot(interaction, rounded, preferred_element_type=jnp.float32)  36.7 us
    all_to_all x1, waiting for transfers between devices, local(): lax.all_to_all(send, 'grid', split_axis=0, concat_axis=0, tiled=True)  13.7 us
    all_to_all x1, starting transfers between devices, local(): lax.all_to_all(send, 'grid', split_axis=0, concat_axis=0, tiled=True)  11.9 us
    reshape x1, local copies, waits for them, and re-layouts, local(): return (spectra_now.reshape(comp_total, row_count, lon_count), nest_spectra)  7.64 us
  transfers between devices with their start and end apart: 1, of which 1 were waited for; matrix products, arithmetic and copies ran while one was open for 6% of the time, Pallas kernels for 0%

profile of v10, /device:TPU:1, one launch (start us, length us, event | category | flops | bytes accessed | tf_op | source)
XLA Modules:
  0.0 133.6 jit_solution(11622219983849025303)
XLA Ops:
  0.8 0.7 tile.4
  1.5 0.6 sine_multiply_fusion
  2.1 50.8 %shard_map.131 = (f32[1296,1024]{1,0:T(8,128)}, f32[1,1024]{1,0:T(1,128)}) custom-call(f32[81]{0:T(128)} %get-tuple-element.17.rx_ref, f32[81]{0:T(128)} %get-tuple-element.16.ry_ref, f32[81,64,256]{2,1,0:T(8,128)} %spec_ref.1, f32[64,256]{1,0:T(8,128)} %factor_ref.1, s32[64,256]{1,0:T(8,128)} %sea_ref.1), custom_call_target="tpu_custom_call" | custom-call | flops 39813120 | bytes 7962624 | tf_op jit(solution)/shard_map/pallas_call | solution.py:179
  53.0 0.7 multiply_add_fusion.3
  53.7 0.7 fusion.53
  54.5 11.3 %multiply_reduce_fusion.2 = (f32[1024]{0:T(1024)S(1)}, f32[1296,1024]{1,0:T(8,128)S(1)}) fusion(f32[1024]{0:T(1024)S(1)} %bitcast.95, f32[1296,1024]{1,0:T(8,128)} %get-tuple-element.4, f32[1024]{0:T(1024)S(1)} %bitcast.96, bf16[1296,1296]{1,0:T(8,128)(2,1)} %param.16, f32[1024]{0:T(1024)S(1)} %bitcast.106, f32[1296]{0:T(1024)S(1)} %get-tuple-element.25, ...), kind=kOutput, calls=%fused_computation.30 | convolution fusion | flops 3462413312 | bytes 14020288 | tf_op jit(solution)/shard_map/dot_general | solution.py:258
  65.8 6.4 %multiply_reduce_fusion.1 = (f32[1024]{0:T(1024)S(1)}, f32[1296,1024]{1,0:T(8,128)S(1)}) fusion(f32[1024]{0:T(1024)S(1)} %get-tuple-element.13, f32[1296,1024]{1,0:T(8,128)S(1)} %get-tuple-element.19, f32[1024]{0:T(1024)S(1)} %get-tuple-element.12, bf16[1296,1296]{1,0:T(8,128)(2,1)S(1)} %copy-done.5, f32[1024]{0:T(1024)S(1)} %bitcast.107, ...), kind=kOutput, calls=%fused_computation.29 | convolution fusion | flops 3462413312 | bytes 14020288 | tf_op jit(solution)/shard_map/dot_general | solution.py:258
  72.3 8.0 %multiply_reduce_fusion = (f32[1024]{0:T(1024)S(1)}, f32[1296,1024]{1,0:T(8,128)}) fusion(f32[1024]{0:T(1024)S(1)} %get-tuple-element.11, f32[1296,1024]{1,0:T(8,128)S(1)} %get-tuple-element.21, f32[1024]{0:T(1024)S(1)} %get-tuple-element.10, bf16[1296,1296]{1,0:T(8,128)(2,1)S(1)} %copy-done.5, f32[1024]{0:T(1024)S(1)} %bitcast.108, ...), kind=kOutput, calls=%fused_computation.28 | convolution fusion | flops 3462413312 | bytes 14020288 | tf_op jit(solution)/shard_map/dot_general | solution.py:258
  80.4 0.2 reduce_window_sum.11
  80.5 0.2 select_reduce_fusion
  80.7 0.4 fusion.31
  81.3 0.1 fusion.34
  81.4 11.0 %fusion.5 = f32[1296,1024]{1,0:T(8,128)S(1)} fusion(f32[1296,1024]{1,0:T(8,128)} %get-tuple-element.23, bf16[1296,1296]{1,0:T(8,128)(2,1)} %param.16, f32[1024]{0:T(1024)S(1)} %get-tuple-element.9, f32[1024]{0:T(1024)S(1)} %get-tuple-element.8, f32[1024]{0:T(1024)S(1)} %bitcast.109, f32[1296]{0:T(1024)S(1)} %get-tuple-element.25, f32[1024]{0:T(1024)S(1)} %bitcast.105, ...), kind=kOutput, calls=%fused_computation.6 | convolution fusion | flops 3459760128 | bytes 14016192 | tf_op jit(solution)/shard_map/dot_general | solution.py:258
  92.5 2.3 %copy-done = f32[1296,1024]{1,0:T(8,128)} copy-done((f32[1296,1024]{1,0:T(8,128)}, f32[1296,1024]{1,0:T(8,128)S(1)}, u32[]{:S(2)}) %copy-start) | copy-done | bytes 5308440
  94.8 2.4 %fusion.28 = bf16[256,1296]{0,1:T(8,128)(2,1)S(1)} fusion(f32[256,1024]{1,0:T(8,128)S(1)} %fusion.31, f32[1296,1024]{1,0:T(8,128)S(1)} %fusion.5, f32[256]{0:T(256)S(1)} %bitcast.116), kind=kOutput, calls=%fused_computation.37 | convolution fusion | flops 2039095296 | bytes 7021568 | tf_op jit(solution)/shard_map/dot_general | solution.py:288
  97.2 0.3 copy.17
  97.5 0.1 fusion.33
  97.7 0.3 concatenate.12
  98.0 1.0 pad_maximum_fusion
  99.0 11.9 %all-to-all-start = ((bf16[16,16,1297]{2,1,0:T(8,128)(2,1)}), bf16[16,16,1297]{2,1,0:T(8,128)(2,1)S(1)}, u32[]{:S(2)}, u32[]{:S(2)}) async-start(bf16[16,16,1297]{2,1,0:T(8,128)(2,1)} %pad_maximum_fusion), calls=%async_computation | async-start | bytes 1441792 | tf_op jit(solution)/shard_map/all_to_all | solution.py:294
  110.8 7.6 %reshape.104 = f32[1296,4,256]{2,1,0:T(4,128)} reshape(f32[1296,1024]{1,0:T(8,128)} %copy-done) | data formatting | bytes 10616832 | tf_op jit(solution)/shard_map/reshape | solution.py:303
  118.5 13.7 %all-to-all-done = bf16[16,16,1297]{2,1,0:T(8,128)(2,1)S(1)} async-done(((bf16[16,16,1297]{2,1,0:T(8,128)(2,1)}), bf16[16,16,1297]{2,1,0:T(8,128)(2,1)S(1)}, u32[]{:S(2)}, u32[]{:S(2)}) %all-to-all-start) | async-done | bytes 664096 | tf_op jit(solution)/shard_map/all_to_all | solution.py:294
  132.2 0.2 slice_reduce_fusion
  132.3 1.3 fusion.29
  (32 shorter events, 0.5 us)
Async XLA Ops:
  0.6 53.7 %copy-start.1 = (f32[4,256]{1,0:T(4,128)S(1)}, f32[4,256]{1,0:T(4,128)}, u32[]{:S(2)}) copy-start(f32[4,256]{1,0:T(4,128)} %param.18) | copy-start | bytes 12292
  0.6 53.8 %copy-start.2 = (f32[4,256]{1,0:T(4,128)S(1)}, f32[4,256]{1,0:T(4,128)}, u32[]{:S(2)}) copy-start(f32[4,256]{1,0:T(4,128)} %param.17) | copy-start | bytes 12292
  54.5 11.3 %copy-start.5 = (bf16[1296,1296]{1,0:T(8,128)(2,1)S(1)}, bf16[1296,1296]{1,0:T(8,128)(2,1)}, u32[]{:S(2)}) copy-start(bf16[1296,1296]{1,0:T(8,128)(2,1)} %param.16) | copy-start | bytes 10077700
  72.2 8.0 %copy-start.3 = (s32[128,1]{0,1:T(1,128)S(1)}, s32[128,1]{0,1:T(1,128)}, u32[]{:S(2)}) copy-start(s32[128,1]{0,1:T(1,128)} %param.19) | copy-start | bytes 1540
  72.2 8.5 %copy-start.4 = (s32[128]{0:T(128)S(1)}, s32[128]{0:T(128)}, u32[]{:S(2)}) copy-start(s32[128]{0:T(128)} %param.21) | copy-start | bytes 1540
  72.3 8.9 %copy-start.6 = (f32[64]{0:T(128)S(1)}, f32[64]{0:T(128)}, u32[]{:S(2)}) copy-start(f32[64]{0:T(128)} %param.23) | copy-start | bytes 772
  72.3 8.9 %copy-start.7 = (s32[128]{0:T(128)S(1)}, s32[128]{0:T(128)}, u32[]{:S(2)}) copy-start(s32[128]{0:T(128)} %param.22) | copy-start | bytes 1540
  92.4 2.3 %copy-start = (f32[1296,1024]{1,0:T(8,128)}, f32[1296,1024]{1,0:T(8,128)S(1)}, u32[]{:S(2)}) copy-start(f32[1296,1024]{1,0:T(8,128)S(1)} %fusion.5) | copy-start | bytes 15925252
  92.4 5.1 %copy-start.8 = (s32[128]{0:T(128)S(1)}, s32[128]{0:T(128)}, u32[]{:S(2)}) copy-start(s32[128]{0:T(128)} %param.20) | copy-start | bytes 1540
  99.0 33.2 %all-to-all-start = ((bf16[16,16,1297]{2,1,0:T(8,128)(2,1)}), bf16[16,16,1297]{2,1,0:T(8,128)(2,1)S(1)}, u32[]{:S(2)}, u32[]{:S(2)}) async-start(bf16[16,16,1297]{2,1,0:T(8,128)(2,1)} %pad_maximum_fusion), calls=%async_computation | async-start | bytes 1441792 | tf_op jit(solution)/shard_map/all_to_all | solution.py:294

commit v11 on v10

--- a/solution.py
+++ b/solution.py
@@ -154,17 +154,14 @@
 
         lax.fori_loop(0, spec_count, regroup, 0, unroll=2)
 
-    def finish(d, carry):
-        @pl.when(d != spec)
-        def _():
-            copy_to(d, d, 0, comps).wait_send()
-            copy_to(d, d, 0, comps).wait_recv()
-
-        return carry
-
-    lax.fori_loop(0, spec_count, finish, 0)
     total = jnp.zeros(sumsq_ref.shape, jnp.float32)
     for s in range(spec_count):
+
+        @pl.when(s != spec)
+        def _():
+            copy_to(s, s, 0, comps).wait_send()
+            copy_to(s, s, 0, comps).wait_recv()
+
         part = recv_buf[s].astype(out_ref.dtype)
         out_ref[s * comps : (s + 1) * comps, :] = part
         total = total + jnp.sum(part * part, axis=0, keepdims=True)

time: 134 us -> 134 us (level)
  no operation moved by 1% of the time
where the time goes in v11:
time: 134 us
  Pallas kernels  50.8 us (38%)
  matrix products  41.1 us (31%)
  waiting for transfers between devices  13.7 us (10%)
  starting transfers between devices  11.8 us (9%)
  local copies, waits for them, and re-layouts  11.6 us (9%)
  other arithmetic  3.67 us (3%)
    pallas_call x1, Pallas kernels, propagate(): pl.pallas_call(propagate_kernel, in_specs=[smem, smem, vmem, vmem, vmem],...  50.8 us
    dot_general x4, matrix products, local(): transfer = jnp.dot(interaction, rounded, preferred_element_type=jnp.float32)  36.7 us
    all_to_all x1, waiting for transfers between devices, local(): lax.all_to_all(send, 'grid', split_axis=0, concat_axis=0, tiled=True)  13.7 us
    all_to_all x1, starting transfers between devices, local(): lax.all_to_all(send, 'grid', split_axis=0, concat_axis=0, tiled=True)  11.8 us
    reshape x1, local copies, waits for them, and re-layouts, local(): return (spectra_now.reshape(comp_total, row_count, lon_count), nest_spectra)  7.64 us
  transfers between devices with their start and end apart: 1, of which 1 were waited for; matrix products, arithmetic and copies ran while one was open for 6% of the time, Pallas kernels for 0%

profile of v11, /device:TPU:1, one launch (start us, length us, event | category | flops | bytes accessed | tf_op | source)
XLA Modules:
  0.0 133.6 jit_solution(10419356091099343908)
XLA Ops:
  0.8 0.7 tile.4
  1.5 0.6 sine_multiply_fusion
  2.1 50.8 %shard_map.131 = (f32[1296,1024]{1,0:T(8,128)}, f32[1,1024]{1,0:T(1,128)}) custom-call(f32[81]{0:T(128)} %get-tuple-element.17.rx_ref, f32[81]{0:T(128)} %get-tuple-element.16.ry_ref, f32[81,64,256]{2,1,0:T(8,128)} %spec_ref.1, f32[64,256]{1,0:T(8,128)} %factor_ref.1, s32[64,256]{1,0:T(8,128)} %sea_ref.1), custom_call_target="tpu_custom_call" | custom-call | flops 39813120 | bytes 7962624 | tf_op jit(solution)/shard_map/pallas_call | solution.py:176
  53.0 0.7 multiply_add_fusion.3
  53.6 0.7 fusion.53
  54.5 11.3 %multiply_reduce_fusion.2 = (f32[1024]{0:T(1024)S(1)}, f32[1296,1024]{1,0:T(8,128)S(1)}) fusion(f32[1024]{0:T(1024)S(1)} %bitcast.95, f32[1296,1024]{1,0:T(8,128)} %get-tuple-element.4, f32[1024]{0:T(1024)S(1)} %bitcast.96, bf16[1296,1296]{1,0:T(8,128)(2,1)} %param.16, f32[1024]{0:T(1024)S(1)} %bitcast.106, f32[1296]{0:T(1024)S(1)} %get-tuple-element.25, ...), kind=kOutput, calls=%fused_computation.30 | convolution fusion | flops 3462413312 | bytes 14020288 | tf_op jit(solution)/shard_map/dot_general | solution.py:255
  65.8 6.4 %multiply_reduce_fusion.1 = (f32[1024]{0:T(1024)S(1)}, f32[1296,1024]{1,0:T(8,128)S(1)}) fusion(f32[1024]{0:T(1024)S(1)} %get-tuple-element.13, f32[1296,1024]{1,0:T(8,128)S(1)} %get-tuple-element.19, f32[1024]{0:T(1024)S(1)} %get-tuple-element.12, bf16[1296,1296]{1,0:T(8,128)(2,1)S(1)} %copy-done.5, f32[1024]{0:T(1024)S(1)} %bitcast.107, ...), kind=kOutput, calls=%fused_computation.29 | convolution fusion | flops 3462413312 | bytes 14020288 | tf_op jit(solution)/shard_map/dot_general | solution.py:255
  72.3 8.0 %multiply_reduce_fusion = (f32[1024]{0:T(1024)S(1)}, f32[1296,1024]{1,0:T(8,128)}) fusion(f32[1024]{0:T(1024)S(1)} %get-tuple-element.11, f32[1296,1024]{1,0:T(8,128)S(1)} %get-tuple-element.21, f32[1024]{0:T(1024)S(1)} %get-tuple-element.10, bf16[1296,1296]{1,0:T(8,128)(2,1)S(1)} %copy-done.5, f32[1024]{0:T(1024)S(1)} %bitcast.108, ...), kind=kOutput, calls=%fused_computation.28 | convolution fusion | flops 3462413312 | bytes 14020288 | tf_op jit(solution)/shard_map/dot_general | solution.py:255
  80.3 0.2 reduce_window_sum.11
  80.5 0.2 select_reduce_fusion
  80.7 0.4 fusion.31
  81.3 0.1 fusion.34
  81.4 11.0 %fusion.5 = f32[1296,1024]{1,0:T(8,128)S(1)} fusion(f32[1296,1024]{1,0:T(8,128)} %get-tuple-element.23, bf16[1296,1296]{1,0:T(8,128)(2,1)} %param.16, f32[1024]{0:T(1024)S(1)} %get-tuple-element.9, f32[1024]{0:T(1024)S(1)} %get-tuple-element.8, f32[1024]{0:T(1024)S(1)} %bitcast.109, f32[1296]{0:T(1024)S(1)} %get-tuple-element.25, f32[1024]{0:T(1024)S(1)} %bitcast.105, ...), kind=kOutput, calls=%fused_computation.6 | convolution fusion | flops 3459760128 | bytes 14016192 | tf_op jit(solution)/shard_map/dot_general | solution.py:255
  92.5 2.3 %copy-done = f32[1296,1024]{1,0:T(8,128)} copy-done((f32[1296,1024]{1,0:T(8,128)}, f32[1296,1024]{1,0:T(8,128)S(1)}, u32[]{:S(2)}) %copy-start) | copy-done | bytes 5308440
  94.7 2.4 %fusion.28 = bf16[256,1296]{0,1:T(8,128)(2,1)S(1)} fusion(f32[256,1024]{1,0:T(8,128)S(1)} %fusion.31, f32[1296,1024]{1,0:T(8,128)S(1)} %fusion.5, f32[256]{0:T(256)S(1)} %bitcast.116), kind=kOutput, calls=%fused_computation.37 | convolution fusion | flops 2039095296 | bytes 7021568 | tf_op jit(solution)/shard_map/dot_general | solution.py:285
  97.2 0.3 copy.17
  97.5 0.1 fusion.33
  97.7 0.3 concatenate.12
  98.0 1.0 pad_maximum_fusion
  99.0 11.8 %all-to-all-start = ((bf16[16,16,1297]{2,1,0:T(8,128)(2,1)}), bf16[16,16,1297]{2,1,0:T(8,128)(2,1)S(1)}, u32[]{:S(2)}, u32[]{:S(2)}) async-start(bf16[16,16,1297]{2,1,0:T(8,128)(2,1)} %pad_maximum_fusion), calls=%async_computation | async-start | bytes 1441792 | tf_op jit(solution)/shard_map/all_to_all | solution.py:291
  110.8 7.6 %reshape.104 = f32[1296,4,256]{2,1,0:T(4,128)} reshape(f32[1296,1024]{1,0:T(8,128)} %copy-done) | data formatting | bytes 10616832 | tf_op jit(solution)/shard_map/reshape | solution.py:300
  118.4 13.7 %all-to-all-done = bf16[16,16,1297]{2,1,0:T(8,128)(2,1)S(1)} async-done(((bf16[16,16,1297]{2,1,0:T(8,128)(2,1)}), bf16[16,16,1297]{2,1,0:T(8,128)(2,1)S(1)}, u32[]{:S(2)}, u32[]{:S(2)}) %all-to-all-start) | async-done | bytes 664096 | tf_op jit(solution)/shard_map/all_to_all | solution.py:291
  132.1 0.2 slice_reduce_fusion
  132.3 1.3 fusion.29
  (32 shorter events, 0.5 us)
Async XLA Ops:
  0.6 53.7 %copy-start.1 = (f32[4,256]{1,0:T(4,128)S(1)}, f32[4,256]{1,0:T(4,128)}, u32[]{:S(2)}) copy-start(f32[4,256]{1,0:T(4,128)} %param.18) | copy-start | bytes 12292
  0.6 53.8 %copy-start.2 = (f32[4,256]{1,0:T(4,128)S(1)}, f32[4,256]{1,0:T(4,128)}, u32[]{:S(2)}) copy-start(f32[4,256]{1,0:T(4,128)} %param.17) | copy-start | bytes 12292
  54.5 11.3 %copy-start.5 = (bf16[1296,1296]{1,0:T(8,128)(2,1)S(1)}, bf16[1296,1296]{1,0:T(8,128)(2,1)}, u32[]{:S(2)}) copy-start(bf16[1296,1296]{1,0:T(8,128)(2,1)} %param.16) | copy-start | bytes 10077700
  72.2 8.0 %copy-start.3 = (s32[128,1]{0,1:T(1,128)S(1)}, s32[128,1]{0,1:T(1,128)}, u32[]{:S(2)}) copy-start(s32[128,1]{0,1:T(1,128)} %param.19) | copy-start | bytes 1540
  72.2 8.5 %copy-start.4 = (s32[128]{0:T(128)S(1)}, s32[128]{0:T(128)}, u32[]{:S(2)}) copy-start(s32[128]{0:T(128)} %param.21) | copy-start | bytes 1540
  72.2 8.9 %copy-start.6 = (f32[64]{0:T(128)S(1)}, f32[64]{0:T(128)}, u32[]{:S(2)}) copy-start(f32[64]{0:T(128)} %param.23) | copy-start | bytes 772
  72.3 8.9 %copy-start.7 = (s32[128]{0:T(128)S(1)}, s32[128]{0:T(128)}, u32[]{:S(2)}) copy-start(s32[128]{0:T(128)} %param.22) | copy-start | bytes 1540
  92.4 2.3 %copy-start = (f32[1296,1024]{1,0:T(8,128)}, f32[1296,1024]{1,0:T(8,128)S(1)}, u32[]{:S(2)}) copy-start(f32[1296,1024]{1,0:T(8,128)S(1)} %fusion.5) | copy-start | bytes 15925252
  92.4 5.1 %copy-start.8 = (s32[128]{0:T(128)S(1)}, s32[128]{0:T(128)}, u32[]{:S(2)}) copy-start(s32[128]{0:T(128)} %param.20) | copy-start | bytes 1540
  99.0 33.1 %all-to-all-start = ((bf16[16,16,1297]{2,1,0:T(8,128)(2,1)}), bf16[16,16,1297]{2,1,0:T(8,128)(2,1)S(1)}, u32[]{:S(2)}, u32[]{:S(2)}) async-start(bf16[16,16,1297]{2,1,0:T(8,128)(2,1)} %pad_maximum_fusion), calls=%async_computation | async-start | bytes 1441792 | tf_op jit(solution)/shard_map/all_to_all | solution.py:291

commit v12 on v10

--- a/solution.py
+++ b/solution.py
@@ -60,7 +60,6 @@
         return carry
 
     lax.fori_loop(0, spec_count, greet, 0)
-    pl.semaphore_wait(barrier, 2 + spec_count - 1)
 
     sea = sea_ref[...].astype(jnp.float32)
     factor = factor_ref[...] * sea
@@ -81,6 +80,7 @@
     first, last = lax.fori_loop(0, comps, edges, (zero, zero), unroll=3)
     send_first[...] = first
     send_last[...] = last
+    pl.semaphore_wait(barrier, 2 + spec_count - 1)
     to_right = pltpu.make_async_remote_copy(
         src_ref=send_last, dst_ref=recv_west, send_sem=send_sem.at[0], recv_sem=recv_sem.at[0],
         device_id=(spec, right), device_id_type=pl.DeviceIdType.MESH,

time: 134 us -> 131 us (0.978)
  Pallas kernels: 50.8 us -> 47.8 us
    pallas_call x1, Pallas kernels: 50.8 us -> 47.8 us  [propagate(): pl.pallas_call(propagate_kernel, in_specs=[smem, smem, vmem, vmem, vmem],...]
where the time goes in v12:
time: 131 us; the launch traced here: 130 us
  Pallas kernels  47.8 us (36%)
  matrix products  41.1 us (31%)
  waiting for transfers between devices  13.7 us (10%)
  local copies, waits for them, and re-layouts  11.6 us (9%)
  starting transfers between devices  11.4 us (9%)
  other arithmetic  3.67 us (3%)
    pallas_call x1, Pallas kernels, propagate(): pl.pallas_call(propagate_kernel, in_specs=[smem, smem, vmem, vmem, vmem],...  47.8 us
    dot_general x4, matrix products, local(): transfer = jnp.dot(interaction, rounded, preferred_element_type=jnp.float32)  36.7 us
    all_to_all x1, waiting for transfers between devices, local(): lax.all_to_all(send, 'grid', split_axis=0, concat_axis=0, tiled=True)  13.7 us
    all_to_all x1, starting transfers between devices, local(): lax.all_to_all(send, 'grid', split_axis=0, concat_axis=0, tiled=True)  11.4 us
    reshape x1, local copies, waits for them, and re-layouts, local(): return (spectra_now.reshape(comp_total, row_count, lon_count), nest_spectra)  7.64 us
  transfers between devices with their start and end apart: 1, of which 1 were waited for; matrix products, arithmetic and copies ran while one was open for 6% of the time, Pallas kernels for 0%

profile of v12, /device:TPU:1, one launch (start us, length us, event | category | flops | bytes accessed | tf_op | source)
XLA Modules:
  0.0 130.2 jit_solution(13253293691853412712)
XLA Ops:
  0.8 0.7 tile.4
  1.5 0.6 sine_multiply_fusion
  2.1 47.8 %shard_map.131 = (f32[1296,1024]{1,0:T(8,128)}, f32[1,1024]{1,0:T(1,128)}) custom-call(f32[81]{0:T(128)} %get-tuple-element.17.rx_ref, f32[81]{0:T(128)} %get-tuple-element.16.ry_ref, f32[81,64,256]{2,1,0:T(8,128)} %spec_ref.1, f32[64,256]{1,0:T(8,128)} %factor_ref.1, s32[64,256]{1,0:T(8,128)} %sea_ref.1), custom_call_target="tpu_custom_call" | custom-call | flops 39813120 | bytes 7962624 | tf_op jit(solution)/shard_map/pallas_call | solution.py:179
  49.9 0.7 multiply_add_fusion.3
  50.6 0.7 fusion.53
  51.5 11.2 %multiply_reduce_fusion.2 = (f32[1024]{0:T(1024)S(1)}, f32[1296,1024]{1,0:T(8,128)S(1)}) fusion(f32[1024]{0:T(1024)S(1)} %bitcast.95, f32[1296,1024]{1,0:T(8,128)} %get-tuple-element.4, f32[1024]{0:T(1024)S(1)} %bitcast.96, bf16[1296,1296]{1,0:T(8,128)(2,1)} %param.16, f32[1024]{0:T(1024)S(1)} %bitcast.106, f32[1296]{0:T(1024)S(1)} %get-tuple-element.25, ...), kind=kOutput, calls=%fused_computation.30 | convolution fusion | flops 3462413312 | bytes 14020288 | tf_op jit(solution)/shard_map/dot_general | solution.py:258
  62.7 6.4 %multiply_reduce_fusion.1 = (f32[1024]{0:T(1024)S(1)}, f32[1296,1024]{1,0:T(8,128)S(1)}) fusion(f32[1024]{0:T(1024)S(1)} %get-tuple-element.13, f32[1296,1024]{1,0:T(8,128)S(1)} %get-tuple-element.19, f32[1024]{0:T(1024)S(1)} %get-tuple-element.12, bf16[1296,1296]{1,0:T(8,128)(2,1)S(1)} %copy-done.5, f32[1024]{0:T(1024)S(1)} %bitcast.107, ...), kind=kOutput, calls=%fused_computation.29 | convolution fusion | flops 3462413312 | bytes 14020288 | tf_op jit(solution)/shard_map/dot_general | solution.py:258
  69.3 8.0 %multiply_reduce_fusion = (f32[1024]{0:T(1024)S(1)}, f32[1296,1024]{1,0:T(8,128)}) fusion(f32[1024]{0:T(1024)S(1)} %get-tuple-element.11, f32[1296,1024]{1,0:T(8,128)S(1)} %get-tuple-element.21, f32[1024]{0:T(1024)S(1)} %get-tuple-element.10, bf16[1296,1296]{1,0:T(8,128)(2,1)S(1)} %copy-done.5, f32[1024]{0:T(1024)S(1)} %bitcast.108, ...), kind=kOutput, calls=%fused_computation.28 | convolution fusion | flops 3462413312 | bytes 14020288 | tf_op jit(solution)/shard_map/dot_general | solution.py:258
  77.3 0.2 reduce_window_sum.11
  77.5 0.2 select_reduce_fusion
  77.7 0.4 fusion.31
  78.2 0.1 fusion.34
  78.4 11.0 %fusion.5 = f32[1296,1024]{1,0:T(8,128)S(1)} fusion(f32[1296,1024]{1,0:T(8,128)} %get-tuple-element.23, bf16[1296,1296]{1,0:T(8,128)(2,1)} %param.16, f32[1024]{0:T(1024)S(1)} %get-tuple-element.9, f32[1024]{0:T(1024)S(1)} %get-tuple-element.8, f32[1024]{0:T(1024)S(1)} %bitcast.109, f32[1296]{0:T(1024)S(1)} %get-tuple-element.25, f32[1024]{0:T(1024)S(1)} %bitcast.105, ...), kind=kOutput, calls=%fused_computation.6 | convolution fusion | flops 3459760128 | bytes 14016192 | tf_op jit(solution)/shard_map/dot_general | solution.py:258
  89.4 2.3 %copy-done = f32[1296,1024]{1,0:T(8,128)} copy-done((f32[1296,1024]{1,0:T(8,128)}, f32[1296,1024]{1,0:T(8,128)S(1)}, u32[]{:S(2)}) %copy-start) | copy-done | bytes 5308440
  91.7 2.4 %fusion.28 = bf16[256,1296]{0,1:T(8,128)(2,1)S(1)} fusion(f32[256,1024]{1,0:T(8,128)S(1)} %fusion.31, f32[1296,1024]{1,0:T(8,128)S(1)} %fusion.5, f32[256]{0:T(256)S(1)} %bitcast.116), kind=kOutput, calls=%fused_computation.37 | convolution fusion | flops 2039095296 | bytes 7021568 | tf_op jit(solution)/shard_map/dot_general | solution.py:288
  94.2 0.3 copy.17
  94.5 0.1 fusion.33
  94.6 0.3 concatenate.12
  95.0 1.0 pad_maximum_fusion
  96.0 11.4 %all-to-all-start = ((bf16[16,16,1297]{2,1,0:T(8,128)(2,1)}), bf16[16,16,1297]{2,1,0:T(8,128)(2,1)S(1)}, u32[]{:S(2)}, u32[]{:S(2)}) async-start(bf16[16,16,1297]{2,1,0:T(8,128)(2,1)} %pad_maximum_fusion), calls=%async_computation | async-start | bytes 1441792 | tf_op jit(solution)/shard_map/all_to_all | solution.py:294
  107.4 7.6 %reshape.104 = f32[1296,4,256]{2,1,0:T(4,128)} reshape(f32[1296,1024]{1,0:T(8,128)} %copy-done) | data formatting | bytes 10616832 | tf_op jit(solution)/shard_map/reshape | solution.py:303
  115.0 13.7 %all-to-all-done = bf16[16,16,1297]{2,1,0:T(8,128)(2,1)S(1)} async-done(((bf16[16,16,1297]{2,1,0:T(8,128)(2,1)}), bf16[16,16,1297]{2,1,0:T(8,128)(2,1)S(1)}, u32[]{:S(2)}, u32[]{:S(2)}) %all-to-all-start) | async-done | bytes 664096 | tf_op jit(solution)/shard_map/all_to_all | solution.py:294
  128.7 0.2 slice_reduce_fusion
  128.9 1.3 fusion.29
  (32 shorter events, 0.5 us)
Async XLA Ops:
  0.6 50.7 %copy-start.1 = (f32[4,256]{1,0:T(4,128)S(1)}, f32[4,256]{1,0:T(4,128)}, u32[]{:S(2)}) copy-start(f32[4,256]{1,0:T(4,128)} %param.18) | copy-start | bytes 12292
  0.6 50.8 %copy-start.2 = (f32[4,256]{1,0:T(4,128)S(1)}, f32[4,256]{1,0:T(4,128)}, u32[]{:S(2)}) copy-start(f32[4,256]{1,0:T(4,128)} %param.17) | copy-start | bytes 12292
  51.5 11.3 %copy-start.5 = (bf16[1296,1296]{1,0:T(8,128)(2,1)S(1)}, bf16[1296,1296]{1,0:T(8,128)(2,1)}, u32[]{:S(2)}) copy-start(bf16[1296,1296]{1,0:T(8,128)(2,1)} %param.16) | copy-start | bytes 10077700
  69.2 8.0 %copy-start.3 = (s32[128,1]{0,1:T(1,128)S(1)}, s32[128,1]{0,1:T(1,128)}, u32[]{:S(2)}) copy-start(s32[128,1]{0,1:T(1,128)} %param.19) | copy-start | bytes 1540
  69.2 8.5 %copy-start.4 = (s32[128]{0:T(128)S(1)}, s32[128]{0:T(128)}, u32[]{:S(2)}) copy-start(s32[128]{0:T(128)} %param.21) | copy-start | bytes 1540
  69.2 8.9 %copy-start.6 = (f32[64]{0:T(128)S(1)}, f32[64]{0:T(128)}, u32[]{:S(2)}) copy-start(f32[64]{0:T(128)} %param.23) | copy-start | bytes 772
  69.2 8.9 %copy-start.7 = (s32[128]{0:T(128)S(1)}, s32[128]{0:T(128)}, u32[]{:S(2)}) copy-start(s32[128]{0:T(128)} %param.22) | copy-start | bytes 1540
  89.4 2.3 %copy-start = (f32[1296,1024]{1,0:T(8,128)}, f32[1296,1024]{1,0:T(8,128)S(1)}, u32[]{:S(2)}) copy-start(f32[1296,1024]{1,0:T(8,128)S(1)} %fusion.5) | copy-start | bytes 15925252
  89.4 5.1 %copy-start.8 = (s32[128]{0:T(128)S(1)}, s32[128]{0:T(128)}, u32[]{:S(2)}) copy-start(s32[128]{0:T(128)} %param.20) | copy-start | bytes 1540
  96.0 32.7 %all-to-all-start = ((bf16[16,16,1297]{2,1,0:T(8,128)(2,1)}), bf16[16,16,1297]{2,1,0:T(8,128)(2,1)S(1)}, u32[]{:S(2)}, u32[]{:S(2)}) async-start(bf16[16,16,1297]{2,1,0:T(8,128)(2,1)} %pad_maximum_fusion), calls=%async_computation | async-start | bytes 1441792 | tf_op jit(solution)/shard_map/all_to_all | solution.py:294

commit v13 on v12

--- a/solution.py
+++ b/solution.py
@@ -130,7 +130,7 @@
     blocks = [(tile * b, tile) for b in range(count - 1)]
     blocks.append((tile * (count - 1), comps - tile * (count - 1)))
     for start, size in blocks:
-        lax.fori_loop(start, start + size, one, 0, unroll=4)
+        lax.fori_loop(start, start + size, one, 0, unroll=8)
 
         def regroup(t, carry, start=start, size=size):
             d = lax.rem(spec + t, spec_count)

time: 131 us -> 131 us (level)
  no operation moved by 1% of the time
where the time goes in v13:
time: 131 us; the launch traced here: 130 us
  Pallas kernels  47.6 us (36%)
  matrix products  41.3 us (32%)
  waiting for transfers between devices  13.7 us (10%)
  local copies, waits for them, and re-layouts  11.6 us (9%)
  starting transfers between devices  11.4 us (9%)
  other arithmetic  3.67 us (3%)
    pallas_call x1, Pallas kernels, propagate(): pl.pallas_call(propagate_kernel, in_specs=[smem, smem, vmem, vmem, vmem],...  47.6 us
    dot_general x4, matrix products, local(): transfer = jnp.dot(interaction, rounded, preferred_element_type=jnp.float32)  36.9 us
    all_to_all x1, waiting for transfers between devices, local(): lax.all_to_all(send, 'grid', split_axis=0, concat_axis=0, tiled=True)  13.7 us
    all_to_all x1, starting transfers between devices, local(): lax.all_to_all(send, 'grid', split_axis=0, concat_axis=0, tiled=True)  11.4 us
    reshape x1, local copies, waits for them, and re-layouts, local(): return (spectra_now.reshape(comp_total, row_count, lon_count), nest_spectra)  7.64 us
  transfers between devices with their start and end apart: 1, of which 1 were waited for; matrix products, arithmetic and copies ran while one was open for 6% of the time, Pallas kernels for 0%

profile of v13, /device:TPU:1, one launch (start us, length us, event | category | flops | bytes accessed | tf_op | source)
XLA Modules:
  0.0 130.2 jit_solution(7583217993174607831)
XLA Ops:
  0.8 0.7 tile.4
  1.5 0.6 sine_multiply_fusion
  2.1 47.6 %shard_map.131 = (f32[1296,1024]{1,0:T(8,128)}, f32[1,1024]{1,0:T(1,128)}) custom-call(f32[81]{0:T(128)} %get-tuple-element.17.rx_ref, f32[81]{0:T(128)} %get-tuple-element.16.ry_ref, f32[81,64,256]{2,1,0:T(8,128)} %spec_ref.1, f32[64,256]{1,0:T(8,128)} %factor_ref.1, s32[64,256]{1,0:T(8,128)} %sea_ref.1), custom_call_target="tpu_custom_call" | custom-call | flops 39813120 | bytes 7962624 | tf_op jit(solution)/shard_map/pallas_call | solution.py:179
  49.8 0.7 multiply_add_fusion.3
  50.5 0.7 fusion.53
  51.3 11.4 %multiply_reduce_fusion.2 = (f32[1024]{0:T(1024)S(1)}, f32[1296,1024]{1,0:T(8,128)S(1)}) fusion(f32[1024]{0:T(1024)S(1)} %bitcast.95, f32[1296,1024]{1,0:T(8,128)} %get-tuple-element.4, f32[1024]{0:T(1024)S(1)} %bitcast.96, bf16[1296,1296]{1,0:T(8,128)(2,1)} %param.16, f32[1024]{0:T(1024)S(1)} %bitcast.106, f32[1296]{0:T(1024)S(1)} %get-tuple-element.25, ...), kind=kOutput, calls=%fused_computation.30 | convolution fusion | flops 3462413312 | bytes 14020288 | tf_op jit(solution)/shard_map/dot_general | solution.py:258
  62.8 6.4 %multiply_reduce_fusion.1 = (f32[1024]{0:T(1024)S(1)}, f32[1296,1024]{1,0:T(8,128)S(1)}) fusion(f32[1024]{0:T(1024)S(1)} %get-tuple-element.13, f32[1296,1024]{1,0:T(8,128)S(1)} %get-tuple-element.19, f32[1024]{0:T(1024)S(1)} %get-tuple-element.12, bf16[1296,1296]{1,0:T(8,128)(2,1)S(1)} %copy-done.5, f32[1024]{0:T(1024)S(1)} %bitcast.107, ...), kind=kOutput, calls=%fused_computation.29 | convolution fusion | flops 3462413312 | bytes 14020288 | tf_op jit(solution)/shard_map/dot_general | solution.py:258
  69.3 7.8 %multiply_reduce_fusion = (f32[1024]{0:T(1024)S(1)}, f32[1296,1024]{1,0:T(8,128)}) fusion(f32[1024]{0:T(1024)S(1)} %get-tuple-element.11, f32[1296,1024]{1,0:T(8,128)S(1)} %get-tuple-element.21, f32[1024]{0:T(1024)S(1)} %get-tuple-element.10, bf16[1296,1296]{1,0:T(8,128)(2,1)S(1)} %copy-done.5, f32[1024]{0:T(1024)S(1)} %bitcast.108, ...), kind=kOutput, calls=%fused_computation.28 | convolution fusion | flops 3462413312 | bytes 14020288 | tf_op jit(solution)/shard_map/dot_general | solution.py:258
  77.2 0.2 reduce_window_sum.11
  77.4 0.2 select_reduce_fusion
  77.5 0.4 fusion.31
  78.1 0.1 fusion.34
  78.2 11.3 %fusion.5 = f32[1296,1024]{1,0:T(8,128)S(1)} fusion(f32[1296,1024]{1,0:T(8,128)} %get-tuple-element.23, bf16[1296,1296]{1,0:T(8,128)(2,1)} %param.16, f32[1024]{0:T(1024)S(1)} %get-tuple-element.9, f32[1024]{0:T(1024)S(1)} %get-tuple-element.8, f32[1024]{0:T(1024)S(1)} %bitcast.109, f32[1296]{0:T(1024)S(1)} %get-tuple-element.25, f32[1024]{0:T(1024)S(1)} %bitcast.105, ...), kind=kOutput, calls=%fused_computation.6 | convolution fusion | flops 3459760128 | bytes 14016192 | tf_op jit(solution)/shard_map/dot_general | solution.py:258
  89.5 2.3 %copy-done = f32[1296,1024]{1,0:T(8,128)} copy-done((f32[1296,1024]{1,0:T(8,128)}, f32[1296,1024]{1,0:T(8,128)S(1)}, u32[]{:S(2)}) %copy-start) | copy-done | bytes 5308440
  91.8 2.4 %fusion.28 = bf16[256,1296]{0,1:T(8,128)(2,1)S(1)} fusion(f32[256,1024]{1,0:T(8,128)S(1)} %fusion.31, f32[1296,1024]{1,0:T(8,128)S(1)} %fusion.5, f32[256]{0:T(256)S(1)} %bitcast.116), kind=kOutput, calls=%fused_computation.37 | convolution fusion | flops 2039095296 | bytes 7021568 | tf_op jit(solution)/shard_map/dot_general | solution.py:288
  94.2 0.3 copy.17
  94.6 0.1 fusion.33
  94.7 0.3 concatenate.12
  95.0 1.0 pad_maximum_fusion
  96.0 11.4 %all-to-all-start = ((bf16[16,16,1297]{2,1,0:T(8,128)(2,1)}), bf16[16,16,1297]{2,1,0:T(8,128)(2,1)S(1)}, u32[]{:S(2)}, u32[]{:S(2)}) async-start(bf16[16,16,1297]{2,1,0:T(8,128)(2,1)} %pad_maximum_fusion), calls=%async_computation | async-start | bytes 1441792 | tf_op jit(solution)/shard_map/all_to_all | solution.py:294
  107.4 7.6 %reshape.104 = f32[1296,4,256]{2,1,0:T(4,128)} reshape(f32[1296,1024]{1,0:T(8,128)} %copy-done) | data formatting | bytes 10616832 | tf_op jit(solution)/shard_map/reshape | solution.py:303
  115.1 13.7 %all-to-all-done = bf16[16,16,1297]{2,1,0:T(8,128)(2,1)S(1)} async-done(((bf16[16,16,1297]{2,1,0:T(8,128)(2,1)}), bf16[16,16,1297]{2,1,0:T(8,128)(2,1)S(1)}, u32[]{:S(2)}, u32[]{:S(2)}) %all-to-all-start) | async-done | bytes 664096 | tf_op jit(solution)/shard_map/all_to_all | solution.py:294
  128.8 0.2 slice_reduce_fusion
  128.9 1.3 fusion.29
  (32 shorter events, 0.5 us)
Async XLA Ops:
  0.6 50.6 %copy-start.1 = (f32[4,256]{1,0:T(4,128)S(1)}, f32[4,256]{1,0:T(4,128)}, u32[]{:S(2)}) copy-start(f32[4,256]{1,0:T(4,128)} %param.18) | copy-start | bytes 12292
  0.6 50.6 %copy-start.2 = (f32[4,256]{1,0:T(4,128)S(1)}, f32[4,256]{1,0:T(4,128)}, u32[]{:S(2)}) copy-start(f32[4,256]{1,0:T(4,128)} %param.17) | copy-start | bytes 12292
  51.3 11.5 %copy-start.5 = (bf16[1296,1296]{1,0:T(8,128)(2,1)S(1)}, bf16[1296,1296]{1,0:T(8,128)(2,1)}, u32[]{:S(2)}) copy-start(bf16[1296,1296]{1,0:T(8,128)(2,1)} %param.16) | copy-start | bytes 10077700
  69.2 7.8 %copy-start.3 = (s32[128,1]{0,1:T(1,128)S(1)}, s32[128,1]{0,1:T(1,128)}, u32[]{:S(2)}) copy-start(s32[128,1]{0,1:T(1,128)} %param.19) | copy-start | bytes 1540
  69.2 8.3 %copy-start.4 = (s32[128]{0:T(128)S(1)}, s32[128]{0:T(128)}, u32[]{:S(2)}) copy-start(s32[128]{0:T(128)} %param.21) | copy-start | bytes 1540
  69.3 8.7 %copy-start.6 = (f32[64]{0:T(128)S(1)}, f32[64]{0:T(128)}, u32[]{:S(2)}) copy-start(f32[64]{0:T(128)} %param.23) | copy-start | bytes 772
  69.3 8.7 %copy-start.7 = (s32[128]{0:T(128)S(1)}, s32[128]{0:T(128)}, u32[]{:S(2)}) copy-start(s32[128]{0:T(128)} %param.22) | copy-start | bytes 1540
  89.5 2.3 %copy-start = (f32[1296,1024]{1,0:T(8,128)}, f32[1296,1024]{1,0:T(8,128)S(1)}, u32[]{:S(2)}) copy-start(f32[1296,1024]{1,0:T(8,128)S(1)} %fusion.5) | copy-start | bytes 15925252
  89.5 5.1 %copy-start.8 = (s32[128]{0:T(128)S(1)}, s32[128]{0:T(128)}, u32[]{:S(2)}) copy-start(s32[128]{0:T(128)} %param.20) | copy-start | bytes 1540
  96.0 32.7 %all-to-all-start = ((bf16[16,16,1297]{2,1,0:T(8,128)(2,1)}), bf16[16,16,1297]{2,1,0:T(8,128)(2,1)S(1)}, u32[]{:S(2)}, u32[]{:S(2)}) async-start(bf16[16,16,1297]{2,1,0:T(8,128)(2,1)} %pad_maximum_fusion), calls=%async_computation | async-start | bytes 1441792 | tf_op jit(solution)/shard_map/all_to_all | solution.py:294

commit v14 on v12

--- a/solution.py
+++ b/solution.py
@@ -152,7 +152,7 @@
 
             return carry
 
-        lax.fori_loop(0, spec_count, regroup, 0, unroll=2)
+        lax.fori_loop(0, spec_count, regroup, 0, unroll=4)
 
     def finish(d, carry):
         @pl.when(d != spec)

time: 131 us -> 131 us (level)
  no operation moved by 1% of the time
where the time goes in v14:
time: 131 us; the launch traced here: 130 us
  Pallas kernels  47.8 us (36%)
  matrix products  41.3 us (32%)
  waiting for transfers between devices  13.7 us (10%)
  local copies, waits for them, and re-layouts  11.6 us (9%)
  starting transfers between devices  11.4 us (9%)
  other arithmetic  3.67 us (3%)
    pallas_call x1, Pallas kernels, propagate(): pl.pallas_call(propagate_kernel, in_specs=[smem, smem, vmem, vmem, vmem],...  47.8 us
    dot_general x4, matrix products, local(): transfer = jnp.dot(interaction, rounded, preferred_element_type=jnp.float32)  36.9 us
    all_to_all x1, waiting for transfers between devices, local(): lax.all_to_all(send, 'grid', split_axis=0, concat_axis=0, tiled=True)  13.7 us
    all_to_all x1, starting transfers between devices, local(): lax.all_to_all(send, 'grid', split_axis=0, concat_axis=0, tiled=True)  11.4 us
    reshape x1, local copies, waits for them, and re-layouts, local(): return (spectra_now.reshape(comp_total, row_count, lon_count), nest_spectra)  7.64 us
  transfers between devices with their start and end apart: 1, of which 1 were waited for; matrix products, arithmetic and copies ran while one was open for 6% of the time, Pallas kernels for 0%

profile of v14, /device:TPU:1, one launch (start us, length us, event | category | flops | bytes accessed | tf_op | source)
XLA Modules:
  0.0 130.4 jit_solution(8289698669444900805)
XLA Ops:
  0.8 0.7 tile.4
  1.5 0.6 sine_multiply_fusion
  2.1 47.8 %shard_map.131 = (f32[1296,1024]{1,0:T(8,128)}, f32[1,1024]{1,0:T(1,128)}) custom-call(f32[81]{0:T(128)} %get-tuple-element.17.rx_ref, f32[81]{0:T(128)} %get-tuple-element.16.ry_ref, f32[81,64,256]{2,1,0:T(8,128)} %spec_ref.1, f32[64,256]{1,0:T(8,128)} %factor_ref.1, s32[64,256]{1,0:T(8,128)} %sea_ref.1), custom_call_target="tpu_custom_call" | custom-call | flops 39813120 | bytes 7962624 | tf_op jit(solution)/shard_map/pallas_call | solution.py:179
  49.9 0.7 multiply_add_fusion.3
  50.6 0.7 fusion.53
  51.5 11.4 %multiply_reduce_fusion.2 = (f32[1024]{0:T(1024)S(1)}, f32[1296,1024]{1,0:T(8,128)S(1)}) fusion(f32[1024]{0:T(1024)S(1)} %bitcast.95, f32[1296,1024]{1,0:T(8,128)} %get-tuple-element.4, f32[1024]{0:T(1024)S(1)} %bitcast.96, bf16[1296,1296]{1,0:T(8,128)(2,1)} %param.16, f32[1024]{0:T(1024)S(1)} %bitcast.106, f32[1296]{0:T(1024)S(1)} %get-tuple-element.25, ...), kind=kOutput, calls=%fused_computation.30 | convolution fusion | flops 3462413312 | bytes 14020288 | tf_op jit(solution)/shard_map/dot_general | solution.py:258
  62.9 6.4 %multiply_reduce_fusion.1 = (f32[1024]{0:T(1024)S(1)}, f32[1296,1024]{1,0:T(8,128)S(1)}) fusion(f32[1024]{0:T(1024)S(1)} %get-tuple-element.13, f32[1296,1024]{1,0:T(8,128)S(1)} %get-tuple-element.19, f32[1024]{0:T(1024)S(1)} %get-tuple-element.12, bf16[1296,1296]{1,0:T(8,128)(2,1)S(1)} %copy-done.5, f32[1024]{0:T(1024)S(1)} %bitcast.107, ...), kind=kOutput, calls=%fused_computation.29 | convolution fusion | flops 3462413312 | bytes 14020288 | tf_op jit(solution)/shard_map/dot_general | solution.py:258
  69.4 7.8 %multiply_reduce_fusion = (f32[1024]{0:T(1024)S(1)}, f32[1296,1024]{1,0:T(8,128)}) fusion(f32[1024]{0:T(1024)S(1)} %get-tuple-element.11, f32[1296,1024]{1,0:T(8,128)S(1)} %get-tuple-element.21, f32[1024]{0:T(1024)S(1)} %get-tuple-element.10, bf16[1296,1296]{1,0:T(8,128)(2,1)S(1)} %copy-done.5, f32[1024]{0:T(1024)S(1)} %bitcast.108, ...), kind=kOutput, calls=%fused_computation.28 | convolution fusion | flops 3462413312 | bytes 14020288 | tf_op jit(solution)/shard_map/dot_general | solution.py:258
  77.3 0.2 reduce_window_sum.11
  77.5 0.2 select_reduce_fusion
  77.7 0.4 fusion.31
  78.2 0.1 fusion.34
  78.4 11.3 %fusion.5 = f32[1296,1024]{1,0:T(8,128)S(1)} fusion(f32[1296,1024]{1,0:T(8,128)} %get-tuple-element.23, bf16[1296,1296]{1,0:T(8,128)(2,1)} %param.16, f32[1024]{0:T(1024)S(1)} %get-tuple-element.9, f32[1024]{0:T(1024)S(1)} %get-tuple-element.8, f32[1024]{0:T(1024)S(1)} %bitcast.109, f32[1296]{0:T(1024)S(1)} %get-tuple-element.25, f32[1024]{0:T(1024)S(1)} %bitcast.105, ...), kind=kOutput, calls=%fused_computation.6 | convolution fusion | flops 3459760128 | bytes 14016192 | tf_op jit(solution)/shard_map/dot_general | solution.py:258
  89.7 2.3 %copy-done = f32[1296,1024]{1,0:T(8,128)} copy-done((f32[1296,1024]{1,0:T(8,128)}, f32[1296,1024]{1,0:T(8,128)S(1)}, u32[]{:S(2)}) %copy-start) | copy-done | bytes 5308440
  92.0 2.4 %fusion.28 = bf16[256,1296]{0,1:T(8,128)(2,1)S(1)} fusion(f32[256,1024]{1,0:T(8,128)S(1)} %fusion.31, f32[1296,1024]{1,0:T(8,128)S(1)} %fusion.5, f32[256]{0:T(256)S(1)} %bitcast.116), kind=kOutput, calls=%fused_computation.37 | convolution fusion | flops 2039095296 | bytes 7021568 | tf_op jit(solution)/shard_map/dot_general | solution.py:288
  94.4 0.3 copy.17
  94.7 0.1 fusion.33
  94.9 0.3 concatenate.12
  95.2 1.0 pad_maximum_fusion
  96.2 11.4 %all-to-all-start = ((bf16[16,16,1297]{2,1,0:T(8,128)(2,1)}), bf16[16,16,1297]{2,1,0:T(8,128)(2,1)S(1)}, u32[]{:S(2)}, u32[]{:S(2)}) async-start(bf16[16,16,1297]{2,1,0:T(8,128)(2,1)} %pad_maximum_fusion), calls=%async_computation | async-start | bytes 1441792 | tf_op jit(solution)/shard_map/all_to_all | solution.py:294
  107.6 7.6 %reshape.104 = f32[1296,4,256]{2,1,0:T(4,128)} reshape(f32[1296,1024]{1,0:T(8,128)} %copy-done) | data formatting | bytes 10616832 | tf_op jit(solution)/shard_map/reshape | solution.py:303
  115.2 13.7 %all-to-all-done = bf16[16,16,1297]{2,1,0:T(8,128)(2,1)S(1)} async-done(((bf16[16,16,1297]{2,1,0:T(8,128)(2,1)}), bf16[16,16,1297]{2,1,0:T(8,128)(2,1)S(1)}, u32[]{:S(2)}, u32[]{:S(2)}) %all-to-all-start) | async-done | bytes 664096 | tf_op jit(solution)/shard_map/all_to_all | solution.py:294
  128.9 0.2 slice_reduce_fusion
  129.1 1.3 fusion.29
  (32 shorter events, 0.5 us)
Async XLA Ops:
  0.6 50.7 %copy-start.1 = (f32[4,256]{1,0:T(4,128)S(1)}, f32[4,256]{1,0:T(4,128)}, u32[]{:S(2)}) copy-start(f32[4,256]{1,0:T(4,128)} %param.18) | copy-start | bytes 12292
  0.6 50.8 %copy-start.2 = (f32[4,256]{1,0:T(4,128)S(1)}, f32[4,256]{1,0:T(4,128)}, u32[]{:S(2)}) copy-start(f32[4,256]{1,0:T(4,128)} %param.17) | copy-start | bytes 12292
  51.5 11.5 %copy-start.5 = (bf16[1296,1296]{1,0:T(8,128)(2,1)S(1)}, bf16[1296,1296]{1,0:T(8,128)(2,1)}, u32[]{:S(2)}) copy-start(bf16[1296,1296]{1,0:T(8,128)(2,1)} %param.16) | copy-start | bytes 10077700
  69.4 7.8 %copy-start.3 = (s32[128,1]{0,1:T(1,128)S(1)}, s32[128,1]{0,1:T(1,128)}, u32[]{:S(2)}) copy-start(s32[128,1]{0,1:T(1,128)} %param.19) | copy-start | bytes 1540
  69.4 8.3 %copy-start.4 = (s32[128]{0:T(128)S(1)}, s32[128]{0:T(128)}, u32[]{:S(2)}) copy-start(s32[128]{0:T(128)} %param.21) | copy-start | bytes 1540
  69.4 8.7 %copy-start.6 = (f32[64]{0:T(128)S(1)}, f32[64]{0:T(128)}, u32[]{:S(2)}) copy-start(f32[64]{0:T(128)} %param.23) | copy-start | bytes 772
  69.4 8.7 %copy-start.7 = (s32[128]{0:T(128)S(1)}, s32[128]{0:T(128)}, u32[]{:S(2)}) copy-start(s32[128]{0:T(128)} %param.22) | copy-start | bytes 1540
  89.6 2.3 %copy-start = (f32[1296,1024]{1,0:T(8,128)}, f32[1296,1024]{1,0:T(8,128)S(1)}, u32[]{:S(2)}) copy-start(f32[1296,1024]{1,0:T(8,128)S(1)} %fusion.5) | copy-start | bytes 15925252
  89.7 5.1 %copy-start.8 = (s32[128]{0:T(128)S(1)}, s32[128]{0:T(128)}, u32[]{:S(2)}) copy-start(s32[128]{0:T(128)} %param.20) | copy-start | bytes 1540
  96.2 32.7 %all-to-all-start = ((bf16[16,16,1297]{2,1,0:T(8,128)(2,1)}), bf16[16,16,1297]{2,1,0:T(8,128)(2,1)S(1)}, u32[]{:S(2)}, u32[]{:S(2)}) async-start(bf16[16,16,1297]{2,1,0:T(8,128)(2,1)} %pad_maximum_fusion), calls=%async_computation | async-start | bytes 1441792 | tf_op jit(solution)/shard_map/all_to_all | solution.py:294
